TPU v7x, 128 devices: a whole 4x4x4 slice. The times are simulated.
128 devices in a mesh: ctx: 8 (over x_hi, z), head: 16 (over y, x_lo, core).
Axes of the slice: x: 4 (x_hi: 2, x_lo: 2; x = x_hi * 2 + x_lo), y: 4, z: 4, core: 2. Of those that a mesh axis runs over, the one named last changes fastest.
Arguments:
- hyena_query: bfloat16 [4096, 8192], P('ctx', 'head'), may hold values from -6 to 6
- hyena_key: bfloat16 [4096, 8192], P('ctx', 'head'), may hold values from -6 to 6
- hyena_value: bfloat16 [4096, 8192], P('ctx', 'head'), may hold values from -6 to 6
- hyena_filter: bfloat16 [128, 8192], P(None, 'head'), may hold values from -0.5 to 0.5
- attn_query: bfloat16 [4096, 8192], P('ctx', 'head'), may hold values from -100 to 100
- attn_key: bfloat16 [4096, 8192], P('ctx', 'head'), may hold values from -4 to 4
- attn_value: bfloat16 [4096, 8192], P('ctx', 'head'), may hold values from -12 to 12
- segment_ids: int32 [4096], replicated, may hold values from 0 to 5, never falling along the last dimension, each value on 1 to 2048 neighbouring positions
- out_weight: bfloat16 [8192, 8192], P('head'), may hold values from -0.09375 to 0.09375
Outputs:
- hyena_out: bfloat16 [4096, 8192], P('ctx', 'head')
- stream: bfloat16 [4096, 8192], P('ctx', 'head')
Inputs may be any that keep to these rules, and one draw needn't show every extreme that they name: `segment_ids`: never falls along the positions; each document is 1 to 2048 positions in a row, one exactly 2048.
All inputs are finite; a program needn't handle non-finite values.
Results may differ from a plain program's by a relative error of at most 0.014.
Values may be sent and summed in bfloat16 or wider, within the bound.
No kernel may reach another device: no remote copies, remote signals or barrier semaphores. Data moves between devices by JAX's collectives and lax.ppermute only.
A program may use at most 320 MiB of HBM per device.

v0:
```python
import functools
import math

import jax
import jax.numpy as jnp
from jax import lax
from jax.experimental import pallas as pl
from jax.experimental.pallas import tpu as pltpu
from jax.sharding import PartitionSpec as P

HEAD_DIM = 128
ROWS = 512
HALF = 2048
BK = 512
SCALE = HEAD_DIM ** -0.5
LOG2E = math.log2(math.e)
F32 = jnp.float32
BF16 = jnp.bfloat16
VMEM_LIMIT = 56 * 1024 * 1024


def z_pairs(by):
    return [(i, (i // 4) * 4 + (i % 4 + by) % 4) for i in range(8)]


def cross_pairs(by):
    return [(i, 4 + (i + by) % 4) for i in range(4)]


def y_pairs(by):
    return [(i, ((i // 4 + by) % 4) * 4 + i % 4) for i in range(16)]


def flip_pairs(mask):
    return [(i, i ^ mask) for i in range(16)]


def vmem_specs(count):
    return [pl.BlockSpec(memory_space=pltpu.VMEM)] * count


def pack_kernel(place, q_ref, k_ref, v_ref, *outs):
    z = place[0]
    for by in range(4):
        cols = pl.ds(pl.multiple_of(lax.rem(z + by, 4) * 128, 128), 128)
        qkv, kv = outs[by], outs[4 + by]
        qkv[:, 0:128] = q_ref[:, cols]
        key = k_ref[:, cols]
        val = v_ref[:, cols]
        qkv[:, 128:256] = key
        qkv[:, 256:384] = val
        kv[:, 0:128] = key
        kv[:, 128:256] = val


def pack(place, q, k, v):
    outs = [jax.ShapeDtypeStruct((ROWS, 384), BF16)] * 4 + [jax.ShapeDtypeStruct((ROWS, 256), BF16)] * 4
    return pl.pallas_call(
        pack_kernel,
        grid_spec=pltpu.PrefetchScalarGridSpec(
            num_scalar_prefetch=1, grid=(), in_specs=vmem_specs(3), out_specs=vmem_specs(8)
        ),
        out_shape=outs,
        name="pack",
        compiler_params=pltpu.CompilerParams(vmem_limit_bytes=VMEM_LIMIT),
        cost_estimate=pl.CostEstimate(flops=0, bytes_accessed=4 * 1024 * 1024, transcendentals=0),
    )(place, q, k, v)


def attention_kernel(place, low, start_ref, *refs):
    own = refs[0:4]
    cross = refs[4:8]
    outs = refs[8:12]
    q_s, k_s, v_s, m_s, l_s, acc_s = refs[12:]
    z = place[0]
    shift = place[1]
    for by in range(4):
        row = pl.multiple_of(lax.rem(z + 4 - by, 4) * ROWS, ROWS)
        q_s[pl.ds(row, ROWS), :] = own[by][:, 0:128]
        k_s[pl.ds(HALF + row, ROWS), :] = own[by][:, 128:256]
        v_s[pl.ds(HALF + row, ROWS), :] = own[by][:, 256:384]
        k_s[pl.ds(row, ROWS), :] = cross[by][:, 0:128]
        v_s[pl.ds(row, ROWS), :] = cross[by][:, 128:256]
    key_iota = lax.broadcasted_iota(jnp.int32, (BK, ROWS), 0)
    diff_iota = key_iota - lax.broadcasted_iota(jnp.int32, (BK, ROWS), 1)

    def step(block, query, first, bound, diagonal):
        row = pl.multiple_of(block * BK, BK)
        key = k_s[pl.ds(row, BK), :]
        val = v_s[pl.ds(row, BK), :]
        scores = lax.dot_general(key, query, (((1,), (1,)), ((), ())), preferred_element_type=F32)
        allowed = key_iota >= bound - row
        if diagonal:
            allowed = allowed & (diff_iota <= 0)
        scores = jnp.where(allowed, scores, -1e30)
        top = jnp.max(scores, axis=0, keepdims=True)
        if not first:
            old = m_s[0:1, :]
            top = jnp.maximum(old, top)
        probs = jnp.exp2((scores - top) * (SCALE * LOG2E))
        total = jnp.sum(probs, axis=0, keepdims=True)
        out = lax.dot_general(val, probs.astype(BF16), (((0,), (0,)), ((), ())), preferred_element_type=F32)
        if not first:
            factor = jnp.exp2((old - top) * (SCALE * LOG2E))
            total = total + l_s[0:1, :] * factor
            out = out + acc_s[...] * factor
        m_s[0:1, :] = top
        l_s[0:1, :] = total
        acc_s[...] = out

    for by in range(4):
        block = lax.rem(z + by, 4)
        query = q_s[pl.ds(pl.multiple_of(block * ROWS, ROWS), ROWS), :]
        bound = start_ref[pl.ds(block, 1), :] + shift
        step(4 + block, query, True, bound, True)

        def body(i, carry, block=block, query=query, bound=bound):
            step(3 + block - i, query, False, bound, False)
            return carry

        lax.fori_loop(0, 4 + block - low[block], body, 0)
        outs[by][...] = jnp.transpose(acc_s[...] / l_s[0:1, :]).astype(BF16)


def attention(place, low, starts, own, cross):
    return pl.pallas_call(
        attention_kernel,
        grid_spec=pltpu.PrefetchScalarGridSpec(
            num_scalar_prefetch=2,
            grid=(),
            in_specs=vmem_specs(9),
            out_specs=vmem_specs(4),
            scratch_shapes=[
                pltpu.VMEM((HALF, 128), BF16),
                pltpu.VMEM((2 * HALF, 128), BF16),
                pltpu.VMEM((2 * HALF, 128), BF16),
                pltpu.VMEM((8, ROWS), F32),
                pltpu.VMEM((8, ROWS), F32),
                pltpu.VMEM((128, ROWS), F32),
            ],
        ),
        out_shape=[jax.ShapeDtypeStruct((ROWS, 128), BF16)] * 4,
        name="attention",
        compiler_params=pltpu.CompilerParams(vmem_limit_bytes=VMEM_LIMIT),
        cost_estimate=pl.CostEstimate(flops=4 * 10**9, bytes_accessed=4 * 1024 * 1024, transcendentals=4 * 10**6),
    )(place, low, starts, *own, *cross)


def project_kernel(groups, half, place, own_ref, sib_ref, w_own, w_sib, *rest):
    outs = rest[:-1]
    att = rest[-1]
    j = pl.program_id(0)
    rows = ROWS // 2

    @pl.when(j == 0)
    def _():
        z = place[0]
        for by in range(4):
            col = pl.multiple_of(lax.rem(z + 4 - by, 4) * 128, 128)
            first = by * ROWS + half * rows
            att[:, pl.ds(col, 128)] = own_ref[first : first + rows, :]
            att[:, pl.ds(512 + col, 128)] = sib_ref[first : first + rows, :]

    term = jnp.dot(att[:, 0:512], w_own[...], preferred_element_type=F32)
    term = term + jnp.dot(att[:, 512:1024], w_sib[...], preferred_element_type=F32)
    term = term.astype(BF16)
    first = 0
    for out, group in zip(outs, groups):
        @pl.when((j >= first) & (j < first + len(group)))
        def _(out=out):
            out[0] = term

        first += len(group)


def project(groups, half, place, own, sib, w_own, w_sib):
    flat = [item for group in groups for item in group]
    steps = len(flat)
    rows = ROWS // 2

    def pick(j, which):
        value = jnp.int32(flat[0][which])
        for i in range(1, steps):
            value = jnp.where(j == i, jnp.int32(flat[i][which]), value)
        return value

    def column(j, place):
        y = lax.rem(place[2] + pick(j, 0), 4)
        x = lax.rem(place[3] + pick(j, 1), 2)
        return y * 2 + x

    out_specs = []
    out_shape = []
    first = 0
    for group in groups:
        out_specs.append(
            pl.BlockSpec(
                (1, rows, 512),
                lambda j, place, first=first, last=len(group) - 1: (jnp.clip(j - first, 0, last), 0, 0),
            )
        )
        out_shape.append(jax.ShapeDtypeStruct((len(group), rows, 512), BF16))
        first += len(group)
    return pl.pallas_call(
        functools.partial(project_kernel, groups, half),
        grid_spec=pltpu.PrefetchScalarGridSpec(
            num_scalar_prefetch=1,
            grid=(steps,),
            in_specs=[
                pl.BlockSpec((4 * ROWS, 128), lambda j, place: (0, 0)),
                pl.BlockSpec((4 * ROWS, 128), lambda j, place: (0, 0)),
                pl.BlockSpec((512, 512), lambda j, place: (0, column(j, place) * 2 + place[4])),
                pl.BlockSpec((512, 512), lambda j, place: (0, column(j, place))),
            ],
            out_specs=out_specs,
            scratch_shapes=[pltpu.VMEM((rows, 1024), BF16)],
        ),
        out_shape=out_shape,
        name="project",
        compiler_params=pltpu.CompilerParams(vmem_limit_bytes=VMEM_LIMIT),
        cost_estimate=pl.CostEstimate(
            flops=steps * 2 * rows * 1024 * 512, bytes_accessed=steps * 1024 * 1300 + 1024 * 1024, transcendentals=0
        ),
    )(place, own, sib, w_own, w_sib)


def hyena_kernel(q_ref, k_ref, v_ref, rim_ref, f_ref, out_ref, sig, shifted, taps):
    for lane in range(4):
        cols = slice(lane * 128, lane * 128 + 128)
        sig[0:128, :] = rim_ref[:, cols].astype(F32)
        product = k_ref[:, cols].astype(F32) * v_ref[:, cols].astype(F32)
        sig[128:640, :] = product.astype(BF16).astype(F32)
        taps[...] = f_ref[:, cols].astype(F32)
        for by in range(8):
            shifted[by, 8:640, :] = sig[8 - by : 640 - by, :]

        def block(b, carry):
            base = 128 + b * 128

            def one_shift(by, acc):
                for high in range(16):
                    tap = taps[pl.ds(high * 8 + by, 1), :]
                    acc = acc + tap * shifted[by, pl.ds(pl.multiple_of(base - high * 8, 8), 128), :]
                return acc

            acc = lax.fori_loop(0, 8, one_shift, jnp.zeros((128, 128), F32))
            rows = pl.ds(pl.multiple_of(b * 128, 128), 128)
            out_ref[rows, cols] = (q_ref[rows, cols].astype(F32) * acc).astype(BF16)
            return carry

        lax.fori_loop(0, 4, block, 0)


def hyena(q, k, v, rim, taps):
    return pl.pallas_call(
        hyena_kernel,
        in_specs=vmem_specs(5),
        out_specs=pl.BlockSpec(memory_space=pltpu.VMEM),
        scratch_shapes=[
            pltpu.VMEM((640, 128), F32),
            pltpu.VMEM((8, 640, 128), F32),
            pltpu.VMEM((128, 128), F32),
        ],
        out_shape=jax.ShapeDtypeStruct((ROWS, 512), BF16),
        name="hyena",
        compiler_params=pltpu.CompilerParams(vmem_limit_bytes=VMEM_LIMIT),
        cost_estimate=pl.CostEstimate(flops=10**10, bytes_accessed=3 * 1024 * 1024, transcendentals=0),
    )(q, k, v, rim, taps)


def on_device(
    hyena_query,
    hyena_key,
    hyena_value,
    hyena_filter,
    attn_query,
    attn_key,
    attn_value,
    segment_ids,
    out_weight,
):
    ctx = lax.axis_index("ctx")
    head = lax.axis_index("head")
    z = ctx % 4
    x_hi = ctx // 4
    core = head % 2
    shift = HALF - x_hi * HALF
    place = jnp.stack([z, shift, head // 4, (head // 2) % 2, core]).astype(jnp.int32)

    packed = pack(place, attn_query, attn_key, attn_value)
    own = [packed[0]] + [lax.ppermute(packed[by], "ctx", z_pairs(by)) for by in (1, 2, 3)]
    cross = [lax.ppermute(packed[4 + by], "ctx", cross_pairs(by)) for by in range(4)]

    weight_view = out_weight.reshape(512, 8, 2, 512)
    to_sibling = lax.dynamic_index_in_dim(weight_view, 1 - core, 2, keepdims=False).reshape(512, 4096)
    w_sib = lax.ppermute(to_sibling, "head", flip_pairs(1))

    edge = (hyena_key[384:].astype(F32) * hyena_value[384:].astype(F32)).astype(BF16)
    rim = lax.ppermute(edge, "ctx", [(i, i + 1) for i in range(7)])
    hyena_out = hyena(hyena_query, hyena_key, hyena_value, rim, hyena_filter)

    my_ids = lax.dynamic_slice_in_dim(segment_ids, x_hi * HALF, HALF)
    starts = jnp.zeros((HALF,), jnp.int32)
    for value in range(5):
        count = jnp.sum((segment_ids == value).astype(jnp.int32))
        starts = starts + jnp.where(my_ids > value, count, 0)
    starts = starts.reshape(4, ROWS)
    low = (starts[:, 0] + shift) // BK
    attended = attention(place, low, starts, own, cross)
    mine = jnp.concatenate(
        [attended[0]] + [lax.ppermute(attended[by], "ctx", z_pairs(by)) for by in (1, 2, 3)], axis=0
    )
    sib = lax.ppermute(mine, "head", flip_pairs(1))

    (b_send,) = project([[(d, 1) for d in range(4)]], 1, place, mine, sib, out_weight, w_sib)
    b_got = lax.ppermute(b_send, "head", flip_pairs(2))
    a_send = project([[(d, 0), (d, 1)] for d in (1, 2, 3)], 0, place, mine, sib, out_weight, w_sib)
    a_got = [lax.ppermute(a_send[d - 1], "head", y_pairs(d)) for d in (1, 2, 3)]
    (b_keep,) = project([[(d, 0) for d in range(4)]], 1, place, mine, sib, out_weight, w_sib)
    (a_keep,) = project([[(0, 0), (0, 1)]], 0, place, mine, sib, out_weight, w_sib)

    b_sum = b_keep.astype(F32) + b_got.astype(F32)
    b_parts = [b_sum[d].astype(BF16) for d in range(4)]
    b_terms = [lax.ppermute(b_parts[d], "head", y_pairs(d)) for d in (1, 2, 3)]

    def a_total(e):
        total = a_keep[e].astype(F32)
        for got in a_got:
            total = total + got[e].astype(F32)
        return total

    a_term = lax.ppermute(a_total(1).astype(BF16), "head", flip_pairs(2))
    a_final = a_total(0) + a_term.astype(F32)
    b_final = b_sum[0]
    for term in b_terms:
        b_final = b_final + term.astype(F32)
    stream_a = (hyena_out[:256].astype(F32) + a_final).astype(BF16)
    stream_b = (hyena_out[256:].astype(F32) + b_final).astype(BF16)
    stream = jnp.concatenate([stream_a, stream_b], axis=0)
    return (hyena_out, stream)


def solution(mesh):
    return jax.shard_map(
        on_device,
        mesh=mesh,
        in_specs=(
            P("ctx", "head"),
            P("ctx", "head"),
            P("ctx", "head"),
            P(None, "head"),
            P("ctx", "head"),
            P("ctx", "head"),
            P("ctx", "head"),
            P(),
            P("head", None),
        ),
        out_specs=(P("ctx", "head"), P("ctx", "head")),
        check_vma=False,
    )
```

profile of v0, /device:TPU:4, one launch (start us, length us, event | category | flops | bytes accessed | tf_op | source)
XLA Modules:
  0.0 184.8 jit_solution(14458437599619293046)
XLA Ops:
  0.6 14.5 %reshape.35 = bf16[512,8,2,512]{3,2,1,0:T(2,128)(2,1)} reshape(bf16[512,8192]{1,0:T(8,128)(2,1)} %w_own.7) | data formatting | bytes 16777216 | tf_op jit(solution)/shard_map/reshape | solution.py:294
  15.1 26.1 %dynamic-slice_reduce_fusion = bf16[512,8,512]{2,1,0:T(8,128)(2,1)S(1)} fusion(bf16[512,8,2,512]{3,2,1,0:T(2,128)(2,1)} %reshape.35, s32[]{:T(128)S(6)} %select_n.66), kind=kLoop, calls=%fused_computation | loop fusion | bytes 8388612 | tf_op jit(solution)/shard_map/jit(dynamic_index_in_dim)/dynamic_slice | solution.py:295
  41.2 4.2 %copy.14 = bf16[64,8,8,512]{3,1,2,0:T(8,128)(2,1)} copy(bf16[64,8,8,512]{3,2,1,0:T(8,128)(2,1)S(1)} %bitcast.33) | data formatting | bytes 8388608
  46.0 3.9 %pack.1 = (bf16[512,384]{1,0:T(8,128)(2,1)}, bf16[512,384]{1,0:T(8,128)(2,1)}, bf16[512,384]{1,0:T(8,128)(2,1)}, bf16[512,384]{1,0:T(8,128)(2,1)}, bf16[512,256]...) custom-call(s32[5]{0:T(128)} %stack.23.place, ...), custom_call_target="tpu_custom_call" | custom-call | bytes 4194304 | tf_op jit(solution)/shard_map/pack/pallas_call | solution.py:58
  51.2 1.3 collective-permute-start.5
  53.8 2.0 %collective-permute-start.1 = (bf16[512,384]{1,0:T(8,128)(2,1)}, bf16[512,384]{1,0:T(8,128)(2,1)S(1)}, u32[]{:S(2)}, u32[]{:S(2)}) collective-permute-start(bf16[512,384]{1,0:T(8,128)(2,1)} %get-tuple-element.18), channel_id=1, source_target_pairs={{0,16},{16,32},{32,48},{48,0},{64,80},{80,96},{96,112},{112,64},{1... | collective-permute-start | bytes 1179656 | tf_op jit(solution)/shard_map/ppermute | solution.py:291
  56.5 6.1 %collective-permute-done.4.refs_4_ = bf16[512,256]{1,0:T(8,128)(2,1)S(1)} collective-permute-done((bf16[512,256]{1,0:T(8,128)(2,1)}, bf16[512,256]{1,0:T(8,128)(2,1)S(1)}, u32[]{:S(2)}, u32[]{:S(2)}) %collective-permute-start.4) | collective-permute-done | bytes 262176 | tf_op jit(solution)/shard_map/ppermute | solution.py:292
  62.6 3.9 %collective-permute-start.2 = (bf16[512,384]{1,0:T(8,128)(2,1)}, bf16[512,384]{1,0:T(8,128)(2,1)S(1)}, u32[]{:S(2)}, u32[]{:S(2)}) collective-permute-start(bf16[512,384]{1,0:T(8,128)(2,1)} %get-tuple-element.19), channel_id=1, source_target_pairs={{0,32},{16,48},{32,0},{48,16},{64,96},{80,112},{96,64},{112,80},{1... | collective-permute-start | bytes 1179656 | tf_op jit(solution)/shard_map/ppermute | solution.py:291
  66.5 5.4 %collective-permute-done.5.refs_5_ = bf16[512,256]{1,0:T(8,128)(2,1)S(1)} collective-permute-done((bf16[512,256]{1,0:T(8,128)(2,1)}, bf16[512,256]{1,0:T(8,128)(2,1)S(1)}, u32[]{:S(2)}, u32[]{:S(2)}) %collective-permute-start.5) | collective-permute-done | bytes 262176 | tf_op jit(solution)/shard_map/ppermute | solution.py:292
  72.2 3.1 %select_add_fusion = s32[2048]{0:T(1024)S(1)} fusion(s32[4096]{0:T(1024)S(1)} %copy-done.3, s32[]{:T(128)S(6)} %select_n.59, s32[]{:T(128)} %get-tuple-element.35, s32[]{:T(128)} %get-tuple-element.36, s32[]{:T(128)} %get-tuple-element.33, s32[]{:T(128)} %get-tuple-element.34, s32[]{:T(128)} %get-tuple-element.32), kind=kLoop, calls=%fused_computation.27 | loop fusion | flops 28672 | bytes 16408 | tf_op jit(solution)/shard_map/add | solution.py:306
  75.3 1.8 collective-permute-done.6.refs_6_
  79.0 10.4 %collective-permute-done.7.refs_7_ = bf16[512,256]{1,0:T(8,128)(2,1)S(1)} collective-permute-done((bf16[512,256]{1,0:T(8,128)(2,1)}, bf16[512,256]{1,0:T(8,128)(2,1)S(1)}, u32[]{:S(2)}, u32[]{:S(2)}) %collective-permute-start.7) | collective-permute-done | bytes 262176 | tf_op jit(solution)/shard_map/ppermute | solution.py:292
  89.4 6.3 %collective-permute-done.3.refs_3_ = bf16[512,384]{1,0:T(8,128)(2,1)S(1)} collective-permute-done((bf16[512,384]{1,0:T(8,128)(2,1)}, bf16[512,384]{1,0:T(8,128)(2,1)S(1)}, u32[]{:S(2)}, u32[]{:S(2)}) %collective-permute-start.3) | collective-permute-done | bytes 393248 | tf_op jit(solution)/shard_map/ppermute | solution.py:291
  96.5 8.2 %attention.1 = (bf16[512,128]{1,0:T(8,128)(2,1)}, bf16[512,128]{1,0:T(8,128)(2,1)}, bf16[512,128]{1,0:T(8,128)(2,1)}, bf16[512,128]{1,0:T(8,128)(2,1)}) custom-call(s32[5]{0:T(128)} %stack.23.place, s32[4]{0:T(128)} %and_select_fusion.low, s32[4,512]{1,0:T(4,128)} %copy-done.4, bf16[512,384]{1,0:T(8,128)(2,1)} %get-tuple-element.17.refs_0_, ...), custom_call_target="tpu_custom_call" | custom-call | flops 4000000000 | bytes 4194304 | tf_op jit(solution)/shard_map/attention/pallas_call | solution.py:126
  105.2 3.6 %collective-permute-start.9 = (bf16[512,128]{1,0:T(8,128)(2,1)}, bf16[512,128]{1,0:T(8,128)(2,1)S(1)}, u32[]{:S(2)}, u32[]{:S(2)}) collective-permute-start(bf16[512,128]{1,0:T(8,128)(2,1)} %get-tuple-element.27), channel_id=1, source_target_pairs={{0,32},{16,48},{32,0},{48,16},{64,96},{80,112},{96,64},{112,80},{1... | collective-permute-start | bytes 393224 | tf_op jit(solution)/shard_map/ppermute | solution.py:311
  109.8 1.4 collective-permute-done.8
  111.2 4.0 %collective-permute-done.9 = bf16[512,128]{1,0:T(8,128)(2,1)S(1)} collective-permute-done((bf16[512,128]{1,0:T(8,128)(2,1)}, bf16[512,128]{1,0:T(8,128)(2,1)S(1)}, u32[]{:S(2)}, u32[]{:S(2)}) %collective-permute-start.9) | collective-permute-done | bytes 131104 | tf_op jit(solution)/shard_map/ppermute | solution.py:311
  115.4 1.9 %collective-permute-done.11.sib_ref = bf16[2048,128]{1,0:T(8,128)(2,1)S(1)} collective-permute-done((bf16[2048,128]{1,0:T(8,128)(2,1)S(1)}, bf16[2048,128]{1,0:T(8,128)(2,1)S(1)}, u32[]{:S(2)}, u32[]{:S(2)}) %collective-permute-start.11) | collective-permute-done | bytes 524320 | tf_op jit(solution)/shard_map/ppermute | solution.py:313
  118.1 6.0 %project.7 = bf16[4,256,512]{2,1,0:T(8,128)(2,1)} custom-call(s32[5]{0:T(128)} %stack.23.place, bf16[2048,128]{1,0:T(8,128)(2,1)} %copy-done, bf16[2048,128]{1,0:T(8,128)(2,1)} %copy-done.1, bf16[512,8192]{1,0:T(8,128)(2,1)} %w_own.7, bf16[512,4096]{1,0:T(8,128)(2,1)} %collective-permute-done.12.w_sib), custom_call_target="tpu_custom_call" | custom-call | flops 1073741824 | bytes 6373376 | tf_op jit(solution)/shard_map/project/pallas_call | solution.py:204
  125.3 8.1 %project.5 = (bf16[2,256,512]{2,1,0:T(8,128)(2,1)}, bf16[2,256,512]{2,1,0:T(8,128)(2,1)}, bf16[2,256,512]{2,1,0:T(8,128)(2,1)}) custom-call(s32[5]{0:T(128)} %stack.23.place, bf16[2048,128]{1,0:T(8,128)(2,1)} %copy-done, bf16[2048,128]{1,0:T(8,128)(2,1)} %copy-done.1, bf16[512,8192]{1,0:T(8,128)(2,1)} %w_own.7, bf16[512,4096]{1,0:T(8,128)(2,1)} %collective-permute-done.12.w_sib), custom_call_target="tpu_custom_call" | custom-call | flops 1610612736 | bytes 9035776 | tf_op jit(solution)/shard_map/project/pallas_call | solution.py:204
  133.3 1.6 collective-permute-start.13
  134.9 2.9 %collective-permute-start.14 = (bf16[2,256,512]{2,1,0:T(8,128)(2,1)}, bf16[2,256,512]{2,1,0:T(8,128)(2,1)S(1)}, u32[]{:S(2)}, u32[]{:S(2)}) collective-permute-start(bf16[2,256,512]{2,1,0:T(8,128)(2,1)} %get-tuple-element.30), channel_id=1, source_target_pairs={{0,8},{1,9},{2,10},{3,11},{4,12},{5,13},{6,14},{7,15},{8,0},{9,1},... | collective-permute-start | bytes 1572872 | tf_op jit(solution)/shard_map/ppermute | solution.py:318
  137.8 1.3 collective-permute-start.15
  140.2 2.0 %collective-permute-start = (bf16[128,512]{1,0:T(8,128)(2,1)S(1)}, bf16[128,512]{1,0:T(8,128)(2,1)S(1)}, u32[]{:S(2)}, u32[]{:S(2)}) collective-permute-start(bf16[128,512]{1,0:T(8,128)(2,1)S(1)} %multiply_convert_fusion), channel_id=1, source_target_pairs={{0,16},{16,32},{32,48},{48,64},{64,80},{80,96},{96,112},{1,17},{17... | collective-permute-start | bytes 393224 | tf_op jit(solution)/shard_map/ppermute | solution.py:299
  142.2 4.1 %project.4 = bf16[2,256,512]{2,1,0:T(8,128)(2,1)} custom-call(s32[5]{0:T(128)} %stack.23.place, bf16[2048,128]{1,0:T(8,128)(2,1)} %copy-done, bf16[2048,128]{1,0:T(8,128)(2,1)} %copy-done.1, bf16[512,8192]{1,0:T(8,128)(2,1)} %w_own.7, bf16[512,4096]{1,0:T(8,128)(2,1)} %collective-permute-done.12.w_sib), custom_call_target="tpu_custom_call" | custom-call | flops 536870912 | bytes 3710976 | tf_op jit(solution)/shard_map/project/pallas_call | solution.py:204
  146.3 6.1 %project.6 = bf16[4,256,512]{2,1,0:T(8,128)(2,1)} custom-call(s32[5]{0:T(128)} %stack.23.place, bf16[2048,128]{1,0:T(8,128)(2,1)} %copy-done, bf16[2048,128]{1,0:T(8,128)(2,1)} %copy-done.1, bf16[512,8192]{1,0:T(8,128)(2,1)} %w_own.7, bf16[512,4096]{1,0:T(8,128)(2,1)} %collective-permute-done.12.w_sib), custom_call_target="tpu_custom_call" | custom-call | flops 1073741824 | bytes 6373376 | tf_op jit(solution)/shard_map/project/pallas_call | solution.py:204
  152.4 8.5 %collective-permute-done.14 = bf16[2,256,512]{2,1,0:T(8,128)(2,1)S(1)} collective-permute-done((bf16[2,256,512]{2,1,0:T(8,128)(2,1)}, bf16[2,256,512]{2,1,0:T(8,128)(2,1)S(1)}, u32[]{:S(2)}, u32[]{:S(2)}) %collective-permute-start.14) | collective-permute-done | bytes 524320 | tf_op jit(solution)/shard_map/ppermute | solution.py:318
  162.0 1.6 fusion.9
  165.0 2.4 %collective-permute-start.19 = (bf16[256,512]{1,0:T(8,128)(2,1)S(1)}, bf16[256,512]{1,0:T(8,128)(2,1)S(1)}, u32[]{:S(2)}, u32[]{:S(2)}) collective-permute-start(bf16[256,512]{1,0:T(8,128)(2,1)S(1)} %get-tuple-element.41), channel_id=1, source_target_pairs={{0,8},{1,9},{2,10},{3,11},{4,12},{5,13},{6,14},{7,15},{8,0},{9,1},... | collective-permute-start | bytes 786440 | tf_op jit(solution)/shard_map/ppermute | solution.py:324
  167.4 1.6 collective-permute-start.20
  169.6 12.9 %hyena.1 = bf16[512,512]{1,0:T(8,128)(2,1)} custom-call(bf16[512,512]{1,0:T(8,128)(2,1)} %q_ref.2, bf16[512,512]{1,0:T(8,128)(2,1)} %k_ref.2, bf16[512,512]{1,0:T(8,128)(2,1)} %v_ref.2, bf16[128,512]{1,0:T(8,128)(2,1)} %copy-done.12, bf16[128,512]{1,0:T(8,128)(2,1)} %f_ref.1), custom_call_target="tpu_custom_call" | custom-call | flops 10000000000 | bytes 3145728 | tf_op jit(solution)/shard_map/hyena/pallas_call | solution.py:255
  182.6 1.4 fusion.6
  (62 shorter events, 15.5 us)
Async XLA Ops:
  41.2 14.6 %copy-start.3 = (s32[4096]{0:T(1024)S(1)}, s32[4096]{0:T(1024)}, u32[]{:S(2)}) copy-start(s32[4096]{0:T(1024)} %param.16) | copy-start | bytes 49156
  45.4 71.9 %collective-permute-start.12 = (bf16[512,4096]{1,0:T(8,128)(2,1)}, bf16[512,4096]{1,0:T(8,128)(2,1)}, u32[]{:S(2)}, u32[]{:S(2)}) collective-permute-start(bf16[512,4096]{1,0:T(8,128)(2,1)} %bitcast.12), channel_id=1, source_target_pairs={{0,1},{1,0},{2,3},{3,2},{4,5},{5,4},{6,7},{7,6},{8,9},{9,8},{10,11... | collective-permute-start | bytes 12582920 | tf_op jit(solution)/shard_map/ppermute | solution.py:296
  49.9 12.7 %collective-permute-start.4 = (bf16[512,256]{1,0:T(8,128)(2,1)}, bf16[512,256]{1,0:T(8,128)(2,1)S(1)}, u32[]{:S(2)}, u32[]{:S(2)}) collective-permute-start(bf16[512,256]{1,0:T(8,128)(2,1)} %get-tuple-element.21), channel_id=1, source_target_pairs={{0,64},{16,80},{32,96},{48,112},{1,65},{17,81},{33,97},{49,113},{2... | collective-permute-start | bytes 786440 | tf_op jit(solution)/shard_map/ppermute | solution.py:292
  51.2 20.7 %collective-permute-start.5 = (bf16[512,256]{1,0:T(8,128)(2,1)}, bf16[512,256]{1,0:T(8,128)(2,1)S(1)}, u32[]{:S(2)}, u32[]{:S(2)}) collective-permute-start(bf16[512,256]{1,0:T(8,128)(2,1)} %get-tuple-element.22), channel_id=1, source_target_pairs={{0,80},{16,96},{32,112},{48,64},{1,81},{17,97},{33,113},{49,65},{2... | collective-permute-start | bytes 786440 | tf_op jit(solution)/shard_map/ppermute | solution.py:292
  52.5 24.5 %collective-permute-start.6 = (bf16[512,256]{1,0:T(8,128)(2,1)}, bf16[512,256]{1,0:T(8,128)(2,1)S(1)}, u32[]{:S(2)}, u32[]{:S(2)}) collective-permute-start(bf16[512,256]{1,0:T(8,128)(2,1)} %get-tuple-element.23), channel_id=1, source_target_pairs={{0,96},{16,112},{32,64},{48,80},{1,97},{17,113},{33,65},{49,81},{2... | collective-permute-start | bytes 786440 | tf_op jit(solution)/shard_map/ppermute | solution.py:292
  53.8 35.6 %collective-permute-start.1 = (bf16[512,384]{1,0:T(8,128)(2,1)}, bf16[512,384]{1,0:T(8,128)(2,1)S(1)}, u32[]{:S(2)}, u32[]{:S(2)}) collective-permute-start(bf16[512,384]{1,0:T(8,128)(2,1)} %get-tuple-element.18), channel_id=1, source_target_pairs={{0,16},{16,32},{32,48},{48,0},{64,80},{80,96},{96,112},{112,64},{1... | collective-permute-start | bytes 1179656 | tf_op jit(solution)/shard_map/ppermute | solution.py:291
  62.6 33.2 %copy-start.8 = (bf16[512,256]{1,0:T(8,128)(2,1)}, bf16[512,256]{1,0:T(8,128)(2,1)S(1)}, u32[]{:S(2)}) copy-start(bf16[512,256]{1,0:T(8,128)(2,1)S(1)} %collective-permute-done.4.refs_4_) | copy-start | bytes 786436
  62.6 26.8 %collective-permute-start.2 = (bf16[512,384]{1,0:T(8,128)(2,1)}, bf16[512,384]{1,0:T(8,128)(2,1)S(1)}, u32[]{:S(2)}, u32[]{:S(2)}) collective-permute-start(bf16[512,384]{1,0:T(8,128)(2,1)} %get-tuple-element.19), channel_id=1, source_target_pairs={{0,32},{16,48},{32,0},{48,16},{64,96},{80,112},{96,64},{112,80},{1... | collective-permute-start | bytes 1179656 | tf_op jit(solution)/shard_map/ppermute | solution.py:291
  71.9 23.8 %copy-start.9 = (bf16[512,256]{1,0:T(8,128)(2,1)}, bf16[512,256]{1,0:T(8,128)(2,1)S(1)}, u32[]{:S(2)}) copy-start(bf16[512,256]{1,0:T(8,128)(2,1)S(1)} %collective-permute-done.5.refs_5_) | copy-start | bytes 786436
  71.9 23.8 %collective-permute-start.3 = (bf16[512,384]{1,0:T(8,128)(2,1)}, bf16[512,384]{1,0:T(8,128)(2,1)S(1)}, u32[]{:S(2)}, u32[]{:S(2)}) collective-permute-start(bf16[512,384]{1,0:T(8,128)(2,1)} %get-tuple-element.20), channel_id=1, source_target_pairs={{0,48},{16,0},{32,16},{48,32},{64,112},{80,64},{96,80},{112,96},{1... | collective-permute-start | bytes 1179656 | tf_op jit(solution)/shard_map/ppermute | solution.py:291
  75.3 20.5 %copy-start.4 = (s32[4,512]{1,0:T(4,128)}, s32[4,512]{1,0:T(4,128)S(1)}, u32[]{:S(2)}) copy-start(s32[4,512]{1,0:T(4,128)S(1)} %reshape.34.start_ref) | copy-start | bytes 24580
  77.0 18.7 %copy-start.10 = (bf16[512,256]{1,0:T(8,128)(2,1)}, bf16[512,256]{1,0:T(8,128)(2,1)S(1)}, u32[]{:S(2)}) copy-start(bf16[512,256]{1,0:T(8,128)(2,1)S(1)} %collective-permute-done.6.refs_6_) | copy-start | bytes 786436
  77.0 12.4 %collective-permute-start.7 = (bf16[512,256]{1,0:T(8,128)(2,1)}, bf16[512,256]{1,0:T(8,128)(2,1)S(1)}, u32[]{:S(2)}, u32[]{:S(2)}) collective-permute-start(bf16[512,256]{1,0:T(8,128)(2,1)} %get-tuple-element.24), channel_id=1, source_target_pairs={{0,112},{16,64},{32,80},{48,96},{1,113},{17,65},{33,81},{49,97},{2... | collective-permute-start | bytes 786440 | tf_op jit(solution)/shard_map/ppermute | solution.py:292
  89.4 6.4 %copy-start.11 = (bf16[512,256]{1,0:T(8,128)(2,1)}, bf16[512,256]{1,0:T(8,128)(2,1)S(1)}, u32[]{:S(2)}) copy-start(bf16[512,256]{1,0:T(8,128)(2,1)S(1)} %collective-permute-done.7.refs_7_) | copy-start | bytes 786436
  89.4 6.4 %copy-start.5 = (bf16[512,384]{1,0:T(8,128)(2,1)}, bf16[512,384]{1,0:T(8,128)(2,1)S(1)}, u32[]{:S(2)}) copy-start(bf16[512,384]{1,0:T(8,128)(2,1)S(1)} %collective-permute-done.1.refs_1_) | copy-start | bytes 1179652
  89.4 6.4 %copy-start.6 = (bf16[512,384]{1,0:T(8,128)(2,1)}, bf16[512,384]{1,0:T(8,128)(2,1)S(1)}, u32[]{:S(2)}) copy-start(bf16[512,384]{1,0:T(8,128)(2,1)S(1)} %collective-permute-done.2.refs_2_) | copy-start | bytes 1179652
  104.7 6.5 %collective-permute-start.8 = (bf16[512,128]{1,0:T(8,128)(2,1)}, bf16[512,128]{1,0:T(8,128)(2,1)S(1)}, u32[]{:S(2)}, u32[]{:S(2)}) collective-permute-start(bf16[512,128]{1,0:T(8,128)(2,1)} %get-tuple-element.26), channel_id=1, source_target_pairs={{0,16},{16,32},{32,48},{48,0},{64,80},{80,96},{96,112},{112,64},{1... | collective-permute-start | bytes 393224 | tf_op jit(solution)/shard_map/ppermute | solution.py:311
  105.2 10.0 %collective-permute-start.9 = (bf16[512,128]{1,0:T(8,128)(2,1)}, bf16[512,128]{1,0:T(8,128)(2,1)S(1)}, u32[]{:S(2)}, u32[]{:S(2)}) collective-permute-start(bf16[512,128]{1,0:T(8,128)(2,1)} %get-tuple-element.27), channel_id=1, source_target_pairs={{0,32},{16,48},{32,0},{48,16},{64,96},{80,112},{96,64},{112,80},{1... | collective-permute-start | bytes 393224 | tf_op jit(solution)/shard_map/ppermute | solution.py:311
  109.7 5.5 %collective-permute-start.10 = (bf16[512,128]{1,0:T(8,128)(2,1)}, bf16[512,128]{1,0:T(8,128)(2,1)S(1)}, u32[]{:S(2)}, u32[]{:S(2)}) collective-permute-start(bf16[512,128]{1,0:T(8,128)(2,1)} %get-tuple-element.28), channel_id=1, source_target_pairs={{0,48},{16,0},{32,16},{48,32},{64,112},{80,64},{96,80},{112,96},{1... | collective-permute-start | bytes 393224 | tf_op jit(solution)/shard_map/ppermute | solution.py:311
  115.3 2.0 %copy-start = (bf16[2048,128]{1,0:T(8,128)(2,1)}, bf16[2048,128]{1,0:T(8,128)(2,1)S(1)}, u32[]{:S(2)}) copy-start(bf16[2048,128]{1,0:T(8,128)(2,1)S(1)} %constant_dynamic-update-slice_fusion.own_ref) | copy-start | bytes 1572868
  115.3 2.0 %collective-permute-start.11 = (bf16[2048,128]{1,0:T(8,128)(2,1)S(1)}, bf16[2048,128]{1,0:T(8,128)(2,1)S(1)}, u32[]{:S(2)}, u32[]{:S(2)}) collective-permute-start(bf16[2048,128]{1,0:T(8,128)(2,1)S(1)} %constant_dynamic-update-slice_fusion.own_ref), channel_id=1, source_target_pairs={{0,1},{1,0},{2,3},{3,2},{4,5},{5,4},{6,7},{7,6},{8,9},{9,8},{10,11... | collective-permute-start | bytes 1572872 | tf_op jit(solution)/shard_map/ppermute | solution.py:313
  117.3 0.8 copy-start.1
  124.1 37.9 %collective-permute-start.17 = (bf16[4,256,512]{2,1,0:T(8,128)(2,1)}, bf16[4,256,512]{2,1,0:T(8,128)(2,1)S(1)}, u32[]{:S(2)}, u32[]{:S(2)}) collective-permute-start(bf16[4,256,512]{2,1,0:T(8,128)(2,1)} %project.7), channel_id=1, source_target_pairs={{0,2},{1,3},{2,0},{3,1},{4,6},{5,7},{6,4},{7,5},{8,10},{9,11},{10,... | collective-permute-start | bytes 3145736 | tf_op jit(solution)/shard_map/ppermute | solution.py:316
  133.3 19.1 %collective-permute-start.13 = (bf16[2,256,512]{2,1,0:T(8,128)(2,1)}, bf16[2,256,512]{2,1,0:T(8,128)(2,1)S(1)}, u32[]{:S(2)}, u32[]{:S(2)}) collective-permute-start(bf16[2,256,512]{2,1,0:T(8,128)(2,1)} %get-tuple-element.29), channel_id=1, source_target_pairs={{0,4},{1,5},{2,6},{3,7},{4,8},{5,9},{6,10},{7,11},{8,12},{9,13},{1... | collective-permute-start | bytes 1572872 | tf_op jit(solution)/shard_map/ppermute | solution.py:318
  134.9 26.0 %collective-permute-start.14 = (bf16[2,256,512]{2,1,0:T(8,128)(2,1)}, bf16[2,256,512]{2,1,0:T(8,128)(2,1)S(1)}, u32[]{:S(2)}, u32[]{:S(2)}) collective-permute-start(bf16[2,256,512]{2,1,0:T(8,128)(2,1)} %get-tuple-element.30), channel_id=1, source_target_pairs={{0,8},{1,9},{2,10},{3,11},{4,12},{5,13},{6,14},{7,15},{8,0},{9,1},... | collective-permute-start | bytes 1572872 | tf_op jit(solution)/shard_map/ppermute | solution.py:318
  137.8 23.1 %collective-permute-start.15 = (bf16[2,256,512]{2,1,0:T(8,128)(2,1)}, bf16[2,256,512]{2,1,0:T(8,128)(2,1)S(1)}, u32[]{:S(2)}, u32[]{:S(2)}) collective-permute-start(bf16[2,256,512]{2,1,0:T(8,128)(2,1)} %get-tuple-element.31), channel_id=1, source_target_pairs={{0,12},{1,13},{2,14},{3,15},{4,0},{5,1},{6,2},{7,3},{8,4},{9,5},{1... | collective-permute-start | bytes 1572872 | tf_op jit(solution)/shard_map/ppermute | solution.py:318
  140.2 28.8 %collective-permute-start = (bf16[128,512]{1,0:T(8,128)(2,1)S(1)}, bf16[128,512]{1,0:T(8,128)(2,1)S(1)}, u32[]{:S(2)}, u32[]{:S(2)}) collective-permute-start(bf16[128,512]{1,0:T(8,128)(2,1)S(1)} %multiply_convert_fusion), channel_id=1, source_target_pairs={{0,16},{16,32},{32,48},{48,64},{64,80},{80,96},{96,112},{1,17},{17... | collective-permute-start | bytes 393224 | tf_op jit(solution)/shard_map/ppermute | solution.py:299
  146.3 14.6 %copy-start.2 = (bf16[2,256,512]{2,1,0:T(8,128)(2,1)S(1)}, bf16[2,256,512]{2,1,0:T(8,128)(2,1)}, u32[]{:S(2)}) copy-start(bf16[2,256,512]{2,1,0:T(8,128)(2,1)} %project.4) | copy-start | bytes 1572868
  161.1 21.5 %collective-permute-start.16 = (bf16[256,512]{1,0:T(8,128)(2,1)S(1)}, bf16[256,512]{1,0:T(8,128)(2,1)S(1)}, u32[]{:S(2)}, u32[]{:S(2)}) collective-permute-start(bf16[256,512]{1,0:T(8,128)(2,1)S(1)} %fusion.7), channel_id=1, source_target_pairs={{0,2},{1,3},{2,0},{3,1},{4,6},{5,7},{6,4},{7,5},{8,10},{9,11},{10,... | collective-permute-start | bytes 786440 | tf_op jit(solution)/shard_map/ppermute | solution.py:332
  163.7 18.8 %collective-permute-start.18 = (bf16[256,512]{1,0:T(8,128)(2,1)S(1)}, bf16[256,512]{1,0:T(8,128)(2,1)S(1)}, u32[]{:S(2)}, u32[]{:S(2)}) collective-permute-start(bf16[256,512]{1,0:T(8,128)(2,1)S(1)} %get-tuple-element.39), channel_id=1, source_target_pairs={{0,4},{1,5},{2,6},{3,7},{4,8},{5,9},{6,10},{7,11},{8,12},{9,13},{1... | collective-permute-start | bytes 786440 | tf_op jit(solution)/shard_map/ppermute | solution.py:324
  165.0 17.6 %collective-permute-start.19 = (bf16[256,512]{1,0:T(8,128)(2,1)S(1)}, bf16[256,512]{1,0:T(8,128)(2,1)S(1)}, u32[]{:S(2)}, u32[]{:S(2)}) collective-permute-start(bf16[256,512]{1,0:T(8,128)(2,1)S(1)} %get-tuple-element.41), channel_id=1, source_target_pairs={{0,8},{1,9},{2,10},{3,11},{4,12},{5,13},{6,14},{7,15},{8,0},{9,1},... | collective-permute-start | bytes 786440 | tf_op jit(solution)/shard_map/ppermute | solution.py:324
  167.4 15.2 %collective-permute-start.20 = (bf16[256,512]{1,0:T(8,128)(2,1)S(1)}, bf16[256,512]{1,0:T(8,128)(2,1)S(1)}, u32[]{:S(2)}, u32[]{:S(2)}) collective-permute-start(bf16[256,512]{1,0:T(8,128)(2,1)S(1)} %get-tuple-element.40), channel_id=1, source_target_pairs={{0,12},{1,13},{2,14},{3,15},{4,0},{5,1},{6,2},{7,3},{8,4},{9,5},{1... | collective-permute-start | bytes 786440 | tf_op jit(solution)/shard_map/ppermute | solution.py:324
  (2 other events, 1.4 us)
where the time goes:
time: 188 us; the launch traced here: 185 us
  Pallas kernels  49.2 us (26%)
  local copies, waits for them, and re-layouts  48.6 us (26%)
  waiting for transfers between devices  45.8 us (24%)
  starting transfers between devices  30.8 us (16%)
  other arithmetic  9.48 us (5%)
    dynamic_slice x1, local copies, waits for them, and re-layouts, on_device(): lax.dynamic_index_in_dim(weight_view, 1 - core, 2, keepdims=False)  26.1 us
    pallas_call x4, Pallas kernels, project(): pl.pallas_call(functools.partial(project_kernel, groups, half), grid_spec...  24.3 us
    ppermute x4, waiting for transfers between devices, on_device(): lax.ppermute(packed[4 + by], 'ctx', cross_pairs(by))  23.7 us
    reshape x1, local copies, waits for them, and re-layouts, on_device(): weight_view = out_weight.reshape(512, 8, 2, 512)  14.5 us
    pallas_call x1, Pallas kernels, hyena(): pl.pallas_call(hyena_kernel, in_specs=vmem_specs(5), out_specs=pl.BlockSp...  12.9 us
    ppermute x3, waiting for transfers between devices, on_device(): a_got = [lax.ppermute(a_send[d - 1], 'head', y_pairs(d)) for d in (1, 2, 3)]  8.52 us
    pallas_call x1, Pallas kernels, attention(): pl.pallas_call(attention_kernel, grid_spec=pltpu.PrefetchScalarGridSpec(n...  8.18 us
    unnamed x30, local copies, waits for them, and re-layouts  7.38 us
  transfers between devices with their start and end apart: 21, of which 9 were waited for; matrix products, arithmetic and copies ran while one was open for 5% of the time, Pallas kernels for 23%

commit v1 on v0

v1 whole, which is shorter than its diff:
```python
import functools
import math

import jax
import jax.numpy as jnp
from jax import lax
from jax.experimental import pallas as pl
from jax.experimental.pallas import tpu as pltpu
from jax.sharding import PartitionSpec as P

HEAD_DIM = 128
ROWS = 512
HALF = 2048
BK = 512
SCALE = HEAD_DIM ** -0.5
LOG2E = math.log2(math.e)
F32 = jnp.float32
BF16 = jnp.bfloat16
MIB = 1024 * 1024


def z_pairs(by):
    return [(i, (i // 4) * 4 + (i % 4 + by) % 4) for i in range(8)]


def cross_pairs(by):
    return [(i, 4 + (i + by) % 4) for i in range(4)]


def y_pairs(by):
    return [(i, ((i // 4 + by) % 4) * 4 + i % 4) for i in range(16)]


def flip_pairs(mask):
    return [(i, i ^ mask) for i in range(16)]


def vmem_specs(count):
    return [pl.BlockSpec(memory_space=pltpu.VMEM)] * count


def pack_kernel(q_ref, k_ref, v_ref, out_ref):
    for to in range(4):
        for i, ref in enumerate((q_ref, k_ref, v_ref)):
            out_ref[to, :, i * 128 : i * 128 + 128] = ref[:, to * 128 : to * 128 + 128]


def pack(q, k, v):
    return pl.pallas_call(
        pack_kernel,
        in_specs=vmem_specs(3),
        out_specs=pl.BlockSpec(memory_space=pltpu.VMEM),
        out_shape=jax.ShapeDtypeStruct((4, ROWS, 384), BF16),
        name="pack",
        compiler_params=pltpu.CompilerParams(vmem_limit_bytes=60 * MIB),
        cost_estimate=pl.CostEstimate(flops=0, bytes_accessed=3 * MIB, transcendentals=0),
    )(q, k, v)


def pack_cross_kernel(place, k_ref, v_ref, *outs):
    for by in range(4):
        cols = pl.ds(pl.multiple_of(lax.rem(place[0] + by, 4) * 128, 128), 128)
        outs[by][:, 0:128] = k_ref[:, cols]
        outs[by][:, 128:256] = v_ref[:, cols]


def pack_cross(place, k, v):
    return pl.pallas_call(
        pack_cross_kernel,
        grid_spec=pltpu.PrefetchScalarGridSpec(
            num_scalar_prefetch=1, grid=(), in_specs=vmem_specs(2), out_specs=vmem_specs(4)
        ),
        out_shape=[jax.ShapeDtypeStruct((ROWS, 256), BF16)] * 4,
        name="pack_cross",
        compiler_params=pltpu.CompilerParams(vmem_limit_bytes=60 * MIB),
        cost_estimate=pl.CostEstimate(flops=0, bytes_accessed=2 * MIB, transcendentals=0),
    )(place, k, v)


def attention_kernel(order, place, ids_ref, *refs):
    own = refs[0]
    cross = refs[1:5]
    outs = refs[5 : 5 + len(order)]
    q_s, k_s, v_s, bound_s, m_s, l_s, acc_s = refs[5 + len(order) :]
    z = place[0]
    shift = place[1]
    for by in range(4):
        row = pl.multiple_of(lax.rem(z + 4 - by, 4) * ROWS, ROWS)
        at = by * ROWS
        q_s[at : at + ROWS, :] = own[by, :, 0:128]
        k_s[HALF + at : HALF + at + ROWS, :] = own[by, :, 128:256]
        v_s[HALF + at : HALF + at + ROWS, :] = own[by, :, 256:384]
        k_s[pl.ds(row, ROWS), :] = cross[by][:, 0:128]
        v_s[pl.ds(row, ROWS), :] = cross[by][:, 128:256]
    ids = ids_ref[...]
    bounds = jnp.full(ids.shape, shift, jnp.int32)
    for value in range(5):
        count = jnp.sum(jnp.where(ids == value, 1.0, 0.0)).astype(jnp.int32)
        bounds = bounds + jnp.where(ids > value, count, 0)
    bound_s[...] = bounds
    key_iota = lax.broadcasted_iota(jnp.int32, (BK, ROWS), 0)
    diff_iota = key_iota - lax.broadcasted_iota(jnp.int32, (BK, ROWS), 1)

    def step(block, query, first, bound, diagonal):
        row = pl.multiple_of(block * BK, BK)
        key = k_s[pl.ds(row, BK), :]
        val = v_s[pl.ds(row, BK), :]
        scores = lax.dot_general(key, query, (((1,), (1,)), ((), ())), preferred_element_type=F32)
        allowed = key_iota >= bound - row
        if diagonal:
            allowed = allowed & (diff_iota <= 0)
        scores = jnp.where(allowed, scores, -1e30)
        top = jnp.max(scores, axis=0, keepdims=True)
        if not first:
            old = m_s[0:1, :]
            top = jnp.maximum(old, top)
        probs = jnp.exp2((scores - top) * (SCALE * LOG2E))
        total = jnp.sum(probs, axis=0, keepdims=True)
        out = lax.dot_general(val, probs.astype(BF16), (((0,), (0,)), ((), ())), preferred_element_type=F32)
        if not first:
            factor = jnp.exp2((old - top) * (SCALE * LOG2E))
            total = total + l_s[0:1, :] * factor
            out = out + acc_s[...] * factor
        m_s[0:1, :] = top
        l_s[0:1, :] = total
        acc_s[...] = out

    for out, by in zip(outs, order):
        block = lax.rem(z + by, 4)
        query = q_s[pl.ds(pl.multiple_of(block * ROWS, ROWS), ROWS), :]
        bound = bound_s[pl.ds(place[5] + block, 1), :]
        low = jnp.min(bound) // BK
        step(4 + block, query, True, bound, True)

        def body(i, carry, block=block, query=query, bound=bound):
            step(3 + block - i, query, False, bound, False)
            return carry

        lax.fori_loop(0, 4 + block - low, body, 0)
        out[...] = jnp.transpose(acc_s[...] / l_s[0:1, :]).astype(BF16)


def attention(order, place, ids, own, cross):
    return pl.pallas_call(
        functools.partial(attention_kernel, order),
        grid_spec=pltpu.PrefetchScalarGridSpec(
            num_scalar_prefetch=1,
            grid=(),
            in_specs=vmem_specs(6),
            out_specs=vmem_specs(len(order)),
            scratch_shapes=[
                pltpu.VMEM((HALF, 128), BF16),
                pltpu.VMEM((2 * HALF, 128), BF16),
                pltpu.VMEM((2 * HALF, 128), BF16),
                pltpu.VMEM((8, ROWS), jnp.int32),
                pltpu.VMEM((8, ROWS), F32),
                pltpu.VMEM((8, ROWS), F32),
                pltpu.VMEM((128, ROWS), F32),
            ],
        ),
        out_shape=[jax.ShapeDtypeStruct((ROWS, 128), BF16)] * len(order),
        name="attention",
        compiler_params=pltpu.CompilerParams(vmem_limit_bytes=20 * MIB),
        cost_estimate=pl.CostEstimate(
            flops=len(order) * 10**9, bytes_accessed=4 * MIB, transcendentals=len(order) * 10**6
        ),
    )(place, ids, own, *cross)


BLOCKS = [(0, 1), (1, 1), (2, 1), (3, 1), (2, 0), (1, 0), (3, 0), (0, 0)]


def project_kernel(place, own_ref, sib_ref, w_own, w_sib, *rest):
    a_refs, b_refs = rest[:4], rest[4:6]
    att, weights, staged, in_sem, out_sem = rest[6:]
    z = place[0]
    copies = []
    for j, (d, e) in enumerate(BLOCKS):
        block = (lax.rem(place[2] + d, 4) * 2 + lax.rem(place[3] + e, 2)) * 2 + place[4]
        cols = pl.ds(pl.multiple_of(block * 512, 512), 512)
        pair = []
        for i, ref in enumerate((w_own, w_sib)):
            pair.append(pltpu.make_async_copy(ref.at[:, cols], weights.at[j, pl.ds(i * 512, 512), :], in_sem.at[j, i]))
            pair[-1].start()
        copies.append(pair)
    for by in range(4):
        col = pl.multiple_of(lax.rem(z + 4 - by, 4) * 128, 128)
        first = by * ROWS
        att[:, pl.ds(col, 128)] = own_ref[first : first + ROWS, :]
        att[:, pl.ds(512 + col, 128)] = sib_ref[first : first + ROWS, :]
    stores = []
    for j, (d, e) in enumerate(BLOCKS):
        for copy in copies[j]:
            copy.wait()
        staged[j] = jnp.dot(att[...], weights[j], preferred_element_type=F32).astype(BF16)
        stores.append(pltpu.make_async_copy(staged.at[j, pl.ds(0, 256), :], a_refs[d].at[e], out_sem.at[j, 0]))
        stores.append(pltpu.make_async_copy(staged.at[j, pl.ds(256, 256), :], b_refs[e].at[d], out_sem.at[j, 1]))
        stores[-2].start()
        stores[-1].start()
    for copy in stores:
        copy.wait()


def project(place, own, sib, w_own, w_sib):
    anywhere = pl.BlockSpec(memory_space=pl.ANY)
    return pl.pallas_call(
        project_kernel,
        grid_spec=pltpu.PrefetchScalarGridSpec(
            num_scalar_prefetch=1,
            grid=(),
            in_specs=vmem_specs(2) + [anywhere] * 2,
            out_specs=[anywhere] * 6,
            scratch_shapes=[
                pltpu.VMEM((ROWS, 1024), BF16),
                pltpu.VMEM((8, 1024, 512), BF16),
                pltpu.VMEM((8, ROWS, 512), BF16),
                pltpu.SemaphoreType.DMA((8, 2)),
                pltpu.SemaphoreType.DMA((8, 2)),
            ],
        ),
        out_shape=[jax.ShapeDtypeStruct((2, 256, 512), BF16)] * 4 + [jax.ShapeDtypeStruct((4, 256, 512), BF16)] * 2,
        name="project",
        compiler_params=pltpu.CompilerParams(vmem_limit_bytes=56 * MIB),
        cost_estimate=pl.CostEstimate(flops=8 * 2 * ROWS * 1024 * 512, bytes_accessed=14 * MIB, transcendentals=0),
    )(place, own, sib, w_own, w_sib)


def hyena_kernel(q_ref, k_ref, v_ref, rim_ref, f_ref, out_ref, sig, shifted, taps):
    for lane in range(4):
        cols = slice(lane * 128, lane * 128 + 128)
        sig[0:128, :] = rim_ref[:, cols].astype(F32)
        product = k_ref[:, cols].astype(F32) * v_ref[:, cols].astype(F32)
        sig[128:640, :] = product.astype(BF16).astype(F32)
        taps[...] = f_ref[:, cols].astype(F32)
        for by in range(8):
            shifted[by, 8:640, :] = sig[8 - by : 640 - by, :]

        def block(b, carry):
            base = 128 + b * 128

            def one_shift(by, acc):
                for high in range(16):
                    tap = taps[pl.ds(high * 8 + by, 1), :]
                    acc = acc + tap * shifted[by, pl.ds(pl.multiple_of(base - high * 8, 8), 128), :]
                return acc

            acc = lax.fori_loop(0, 8, one_shift, jnp.zeros((128, 128), F32))
            rows = pl.ds(pl.multiple_of(b * 128, 128), 128)
            out_ref[rows, cols] = (q_ref[rows, cols].astype(F32) * acc).astype(BF16)
            return carry

        lax.fori_loop(0, 4, block, 0)


def hyena(q, k, v, rim, taps):
    return pl.pallas_call(
        hyena_kernel,
        in_specs=vmem_specs(5),
        out_specs=pl.BlockSpec(memory_space=pltpu.VMEM),
        scratch_shapes=[
            pltpu.VMEM((640, 128), F32),
            pltpu.VMEM((8, 640, 128), F32),
            pltpu.VMEM((128, 128), F32),
        ],
        out_shape=jax.ShapeDtypeStruct((ROWS, 512), BF16),
        name="hyena",
        compiler_params=pltpu.CompilerParams(vmem_limit_bytes=12 * MIB),
        cost_estimate=pl.CostEstimate(flops=10**7, bytes_accessed=3 * 1024, transcendentals=0),
    )(q, k, v, rim, taps)


def on_device(
    hyena_query,
    hyena_key,
    hyena_value,
    hyena_filter,
    attn_query,
    attn_key,
    attn_value,
    segment_ids,
    out_weight,
):
    ctx = lax.axis_index("ctx")
    head = lax.axis_index("head")
    z = ctx % 4
    x_hi = ctx // 4
    core = head % 2
    shift = HALF - x_hi * HALF
    place = jnp.stack([z, shift, head // 4, (head // 2) % 2, core, x_hi * 4]).astype(jnp.int32)

    w_sib = lax.ppermute(out_weight, "head", flip_pairs(1))
    to_cross = pack_cross(place, attn_key, attn_value)
    query, _ = lax.optimization_barrier((attn_query, to_cross[0]))
    packed = pack(query, attn_key, attn_value)
    cross = [lax.ppermute(to_cross[by], "ctx", cross_pairs(by)) for by in range(4)]
    own = lax.all_to_all(packed, "ctx", 0, 0, axis_index_groups=[[0, 1, 2, 3], [4, 5, 6, 7]])

    late_key, late_value, _ = lax.optimization_barrier((hyena_key[384:], hyena_value[384:], w_sib))
    edge = (late_key.astype(F32) * late_value.astype(F32)).astype(BF16)
    rim = lax.ppermute(edge, "ctx", [(i, i + 1) for i in range(7)])
    own, rim = lax.optimization_barrier((own, rim))

    ids = segment_ids.reshape(8, ROWS)
    attended = attention((2, 1, 3), place, ids, own, cross)
    back = [lax.ppermute(part, "ctx", z_pairs(by)) for part, by in zip(attended, (2, 1, 3))]
    (kept,) = attention((0,), place, ids, own, cross)
    mine = jnp.concatenate([kept, back[1], back[0], back[2]], axis=0)
    sib = lax.ppermute(mine, "head", flip_pairs(1))

    *a_terms, b_keep, b_send = project(place, mine, sib, out_weight, w_sib)
    a_keep = a_terms[0]
    b_got = lax.ppermute(b_send, "head", flip_pairs(2))
    a_got = [lax.ppermute(a_terms[d], "head", y_pairs(d)) for d in (2, 1, 3)]
    rim, _ = lax.optimization_barrier((rim, b_keep))
    hyena_out = hyena(hyena_query, hyena_key, hyena_value, rim, hyena_filter)
    hyena_out, b_got = lax.optimization_barrier((hyena_out, b_got))

    b_sum = b_keep.astype(F32) + b_got.astype(F32)
    b_parts = [b_sum[d].astype(BF16) for d in range(4)]
    a_got, _ = lax.optimization_barrier((a_got, b_parts))
    b_terms = [lax.ppermute(b_parts[d], "head", y_pairs(d)) for d in (1, 2, 3)]

    def a_total(e):
        total = a_keep[e].astype(F32)
        for got in a_got:
            total = total + got[e].astype(F32)
        return total

    a_term = lax.ppermute(a_total(1).astype(BF16), "head", flip_pairs(2))
    a_final = a_total(0) + a_term.astype(F32)
    b_final = b_sum[0]
    for term in b_terms:
        b_final = b_final + term.astype(F32)
    stream_a = (hyena_out[:256].astype(F32) + a_final).astype(BF16)
    stream_b = (hyena_out[256:].astype(F32) + b_final).astype(BF16)
    stream = jnp.concatenate([stream_a, stream_b], axis=0)
    return (hyena_out, stream)


def solution(mesh):
    return jax.shard_map(
        on_device,
        mesh=mesh,
        in_specs=(
            P("ctx", "head"),
            P("ctx", "head"),
            P("ctx", "head"),
            P(None, "head"),
            P("ctx", "head"),
            P("ctx", "head"),
            P("ctx", "head"),
            P(),
            P("head", None),
        ),
        out_specs=(P("ctx", "head"), P("ctx", "head")),
        check_vma=False,
    )
```

time: 188 us -> 123 us (0.65); the launches traced: 185 us -> 124 us
  local copies, waits for them, and re-layouts: 48.6 us -> 1.55 us
  Pallas kernels: 49.2 us -> 38.1 us
  other arithmetic: 9.48 us -> 1.82 us
  waiting for transfers between devices: 45.8 us -> 49.1 us
    ppermute x14 -> x11, waiting for transfers between devices: 43.9 us -> 3.21 us  [the longest x3 2.3 us: on_device(): a_got = [lax.ppermute(a_terms[d], 'head', y_pairs(d)) for d in (2, 1, 3)]]
    dynamic_slice x1 -> x0, local copies, waits for them, and re-layouts: 26.1 us -> none  [on_device(): lax.dynamic_index_in_dim(weight_view, 1 - core, 2, keepdims=False)]
    all_to_all x0 -> x1, waiting for transfers between devices: none -> 25.4 us  [on_device(): lax.all_to_all(packed, 'ctx', 0, 0, axis_index_groups=[[0, 1, 2, 3], [4,...]
    reshape x2 -> x1, local copies, waits for them, and re-layouts: 14.5 us -> 0.01 us  [on_device(): ids = segment_ids.reshape(8, ROWS)]
    pallas_call x6 -> x5, Pallas kernels: 36.3 us -> 26.6 us  [the longest x2 10.9 us: attention(): pl.pallas_call(functools.partial(attention_kernel, order), grid_spec=pltp...]
    ppermute x3, waiting for transfers between devices: 0.01 us -> 8.61 us  [on_device(): b_terms = [lax.ppermute(b_parts[d], 'head', y_pairs(d)) for d in (1, 2, 3)]]
    unnamed x30 -> x24, local copies, waits for them, and re-layouts: 7.38 us -> 0.85 us
    ppermute x1, waiting for transfers between devices: 0.01 us -> 6.27 us  [on_device(): b_got = lax.ppermute(b_send, 'head', flip_pairs(2))]
  transfers between devices with their start and end apart: 21 -> 19, of which waited for: 9 -> 12; matrix products, arithmetic and copies ran while one was open for 5% -> 1% of each run, Pallas kernels for 23% -> 17%
where the time goes in v1:
time: 123 us; the launch traced here: 124 us
  waiting for transfers between devices  49.1 us (40%)
  Pallas kernels  38.1 us (31%)
  starting transfers between devices  32.1 us (26%)
  other arithmetic  1.82 us (1%)
  local copies, waits for them, and re-layouts  1.55 us (1%)
    all_to_all x1, waiting for transfers between devices, on_device(): lax.all_to_all(packed, 'ctx', 0, 0, axis_index_groups=[[0, 1, 2, 3], [4,...  25.4 us
    pallas_call x1, Pallas kernels, hyena(): pl.pallas_call(hyena_kernel, in_specs=vmem_specs(5), out_specs=pl.BlockSp...  11.5 us
    pallas_call x2, Pallas kernels, attention(): pl.pallas_call(functools.partial(attention_kernel, order), grid_spec=pltp...  10.9 us
    pallas_call x1, Pallas kernels, project(): pl.pallas_call(project_kernel, grid_spec=pltpu.PrefetchScalarGridSpec(num...  9.88 us
    ppermute x3, waiting for transfers between devices, on_device(): b_terms = [lax.ppermute(b_parts[d], 'head', y_pairs(d)) for d in (1, 2, 3)]  8.61 us
    ppermute x3, starting transfers between devices, on_device(): a_got = [lax.ppermute(a_terms[d], 'head', y_pairs(d)) for d in (2, 1, 3)]  6.42 us
    ppermute x1, waiting for transfers between devices, on_device(): b_got = lax.ppermute(b_send, 'head', flip_pairs(2))  6.27 us
    all_to_all x1, starting transfers between devices, on_device(): lax.all_to_all(packed, 'ctx', 0, 0, axis_index_groups=[[0, 1, 2, 3], [4,...  5.45 us
  transfers between devices with their start and end apart: 19, of which 12 were waited for; matrix products, arithmetic and copies ran while one was open for 1% of the time, Pallas kernels for 17%

profile of v1, /device:TPU:4, one launch (start us, length us, event | category | flops | bytes accessed | tf_op | source)
XLA Modules:
  0.0 123.6 jit_solution(2274131881058831657)
XLA Ops:
  1.4 3.0 %pack_cross.1 = (bf16[512,256]{1,0:T(8,128)(2,1)}, bf16[512,256]{1,0:T(8,128)(2,1)}, bf16[512,256]{1,0:T(8,128)(2,1)}, bf16[512,256]{1,0:T(8,128)(2,1)}) custom-call(s32[6]{0:T(128)} %stack.27.place, bf16[512,512]{1,0:T(8,128)(2,1)} %k_ref.4, bf16[512,512]{1,0:T(8,128)(2,1)} %v_ref.4), custom_call_target="tpu_custom_call" | custom-call | bytes 2097152 | tf_op jit(solution)/shard_map/pack_cross/pallas_call | solution.py:68
  4.4 2.8 %pack.1 = bf16[4,512,384]{2,1,0:T(8,128)(2,1)} custom-call(bf16[512,512]{1,0:T(8,128)(2,1)} %q_ref.1, bf16[512,512]{1,0:T(8,128)(2,1)} %k_ref.4, bf16[512,512]{1,0:T(8,128)(2,1)} %v_ref.4), custom_call_target="tpu_custom_call" | custom-call | bytes 3145728 | tf_op jit(solution)/shard_map/pack/pallas_call | solution.py:49
  7.2 5.5 %all-to-all-start = ((bf16[4,512,384]{2,1,0:T(8,128)(2,1)}), bf16[4,512,384]{2,1,0:T(8,128)(2,1)S(1)}, u32[]{:S(2)}, u32[]{:S(2)}) async-start(bf16[4,512,384]{2,1,0:T(8,128)(2,1)} %pack.1), calls=%async_computation | async-start | bytes 3145728 | tf_op jit(solution)/shard_map/all_to_all | solution.py:296
  12.7 1.3 %collective-permute-start.2 = (bf16[512,256]{1,0:T(8,128)(2,1)S(1)}, bf16[512,256]{1,0:T(8,128)(2,1)S(1)}, u32[]{:S(2)}, u32[]{:S(2)}) collective-permute-start(bf16[512,256]{1,0:T(8,128)(2,1)S(1)} %copy-done.11), channel_id=1, source_target_pairs={{0,64},{16,80},{32,96},{48,112},{1,65},{17,81},{33,97},{49,113},{2... | collective-permute-start | bytes 786440 | tf_op jit(solution)/shard_map/ppermute | solution.py:295
  14.0 1.3 %collective-permute-start.3 = (bf16[512,256]{1,0:T(8,128)(2,1)}, bf16[512,256]{1,0:T(8,128)(2,1)S(1)}, u32[]{:S(2)}, u32[]{:S(2)}) collective-permute-start(bf16[512,256]{1,0:T(8,128)(2,1)} %get-tuple-element.32), channel_id=1, source_target_pairs={{0,80},{16,96},{32,112},{48,64},{1,81},{17,97},{33,113},{49,65},{2... | collective-permute-start | bytes 786440 | tf_op jit(solution)/shard_map/ppermute | solution.py:295
  15.3 1.3 %collective-permute-start.4 = (bf16[512,256]{1,0:T(8,128)(2,1)}, bf16[512,256]{1,0:T(8,128)(2,1)S(1)}, u32[]{:S(2)}, u32[]{:S(2)}) collective-permute-start(bf16[512,256]{1,0:T(8,128)(2,1)} %get-tuple-element.33), channel_id=1, source_target_pairs={{0,96},{16,112},{32,64},{48,80},{1,97},{17,113},{33,65},{49,81},{2... | collective-permute-start | bytes 786440 | tf_op jit(solution)/shard_map/ppermute | solution.py:295
  16.6 1.3 %collective-permute-start.5 = (bf16[512,256]{1,0:T(8,128)(2,1)}, bf16[512,256]{1,0:T(8,128)(2,1)S(1)}, u32[]{:S(2)}, u32[]{:S(2)}) collective-permute-start(bf16[512,256]{1,0:T(8,128)(2,1)} %get-tuple-element.34), channel_id=1, source_target_pairs={{0,112},{16,64},{32,80},{48,96},{1,113},{17,65},{33,81},{49,97},{2... | collective-permute-start | bytes 786440 | tf_op jit(solution)/shard_map/ppermute | solution.py:295
  17.9 3.9 %collective-permute-start.1 = (bf16[128,512]{1,0:T(8,128)(2,1)S(1)}, bf16[128,512]{1,0:T(8,128)(2,1)S(1)}, u32[]{:S(2)}, u32[]{:S(2)}) collective-permute-start(bf16[128,512]{1,0:T(8,128)(2,1)S(1)} %multiply_convert_fusion), channel_id=1, source_target_pairs={{0,16},{16,32},{32,48},{48,64},{64,80},{80,96},{96,112},{1,17},{17... | collective-permute-start | bytes 393224 | tf_op jit(solution)/shard_map/ppermute | solution.py:300
  21.9 25.4 %all-to-all-done.refs_0_ = bf16[4,512,384]{2,1,0:T(8,128)(2,1)S(1)} async-done(((bf16[4,512,384]{2,1,0:T(8,128)(2,1)}), bf16[4,512,384]{2,1,0:T(8,128)(2,1)S(1)}, u32[]{:S(2)}, u32[]{:S(2)}) %all-to-all-start) | async-done | bytes 1572896 | tf_op jit(solution)/shard_map/all_to_all | solution.py:296
  48.1 7.1 %attention.3 = (bf16[512,128]{1,0:T(8,128)(2,1)S(1)}, bf16[512,128]{1,0:T(8,128)(2,1)S(1)}, bf16[512,128]{1,0:T(8,128)(2,1)S(1)}) custom-call(s32[6]{0:T(128)S(1)} %copy-done.4, s32[8,512]{1,0:T(8,128)S(1)} %reshape.25.ids_ref, bf16[4,512,384]{2,1,0:T(8,128)(2,1)S(1)} %all-to-all-done.refs_0_, bf16[512,256]{1,0:T(8,128)(2,1)S(1)} %collective-permute-done.2.refs_1_, ...), custom_call_target="tpu_custom_call" | custom-call | flops 3000000000 | bytes 4194304 | tf_op jit(solution)/shard_map/attention/pallas_call | solution.py:144
  55.3 3.7 %collective-permute-start.7 = (bf16[512,128]{1,0:T(8,128)(2,1)S(1)}, bf16[512,128]{1,0:T(8,128)(2,1)S(1)}, u32[]{:S(2)}, u32[]{:S(2)}) collective-permute-start(bf16[512,128]{1,0:T(8,128)(2,1)S(1)} %get-tuple-element.36), channel_id=1, source_target_pairs={{0,32},{16,48},{32,0},{48,16},{64,96},{80,112},{96,64},{112,80},{1... | collective-permute-start | bytes 393224 | tf_op jit(solution)/shard_map/ppermute | solution.py:305
  59.0 0.9 collective-permute-start.8
  59.9 3.8 %attention.2 = bf16[512,128]{1,0:T(8,128)(2,1)S(1)} custom-call(s32[6]{0:T(128)S(1)} %copy-done.4, s32[8,512]{1,0:T(8,128)S(1)} %reshape.25.ids_ref, bf16[4,512,384]{2,1,0:T(8,128)(2,1)S(1)} %all-to-all-done.refs_0_, bf16[512,256]{1,0:T(8,128)(2,1)S(1)} %collective-permute-done.2.refs_1_, bf16[512,256]{1,0:T(8,128)(2,1)S(1)} %collective-permute-done.3.refs_2_, ...), custom_call_target="tpu_custom_call" | custom-call | flops 1000000000 | bytes 4194304 | tf_op jit(solution)/shard_map/attention/pallas_call | solution.py:144
  63.7 0.8 collective-permute-done.7
  64.8 1.9 %collective-permute-done.9.sib_ref = bf16[2048,128]{1,0:T(8,128)(2,1)S(1)} collective-permute-done((bf16[2048,128]{1,0:T(8,128)(2,1)S(1)}, bf16[2048,128]{1,0:T(8,128)(2,1)S(1)}, u32[]{:S(2)}, u32[]{:S(2)}) %collective-permute-start.9) | collective-permute-done | bytes 524320 | tf_op jit(solution)/shard_map/ppermute | solution.py:308
  66.7 0.8 copy-done.9
  67.5 9.9 %project.1 = (bf16[2,256,512]{2,1,0:T(8,128)(2,1)}, bf16[2,256,512]{2,1,0:T(8,128)(2,1)}, bf16[2,256,512]{2,1,0:T(8,128)(2,1)}, bf16[2,256,512]{2,1,0:T(8,128)(2...) custom-call(s32[6]{0:T(128)} %stack.27.place, bf16[2048,128]{1,0:T(8,128)(2,1)} %copy-done.5, ...), custom_call_target="tpu_custom_call" | custom-call | flops 4294967296 | bytes 14680064 | tf_op jit(solution)/shard_map/project/pallas_call | solution.py:206
  77.4 1.3 %collective-permute-start.10 = (bf16[4,256,512]{2,1,0:T(8,128)(2,1)}, bf16[4,256,512]{2,1,0:T(8,128)(2,1)S(1)}, u32[]{:S(2)}, u32[]{:S(2)}) collective-permute-start(bf16[4,256,512]{2,1,0:T(8,128)(2,1)} %get-tuple-element.40), channel_id=1, source_target_pairs={{0,2},{1,3},{2,0},{3,1},{4,6},{5,7},{6,4},{7,5},{8,10},{9,11},{10,... | collective-permute-start | bytes 3145736 | tf_op jit(solution)/shard_map/ppermute | solution.py:312
  78.7 3.2 %collective-permute-start.11 = (bf16[2,256,512]{2,1,0:T(8,128)(2,1)}, bf16[2,256,512]{2,1,0:T(8,128)(2,1)S(1)}, u32[]{:S(2)}, u32[]{:S(2)}) collective-permute-start(bf16[2,256,512]{2,1,0:T(8,128)(2,1)} %get-tuple-element.43), channel_id=1, source_target_pairs={{0,8},{1,9},{2,10},{3,11},{4,12},{5,13},{6,14},{7,15},{8,0},{9,1},... | collective-permute-start | bytes 1572872 | tf_op jit(solution)/shard_map/ppermute | solution.py:313
  82.5 2.6 %collective-permute-start.13 = (bf16[2,256,512]{2,1,0:T(8,128)(2,1)}, bf16[2,256,512]{2,1,0:T(8,128)(2,1)S(1)}, u32[]{:S(2)}, u32[]{:S(2)}) collective-permute-start(bf16[2,256,512]{2,1,0:T(8,128)(2,1)} %get-tuple-element.45), channel_id=1, source_target_pairs={{0,12},{1,13},{2,14},{3,15},{4,0},{5,1},{6,2},{7,3},{8,4},{9,5},{1... | collective-permute-start | bytes 1572872 | tf_op jit(solution)/shard_map/ppermute | solution.py:313
  85.1 11.5 %hyena.1 = bf16[512,512]{1,0:T(8,128)(2,1)} custom-call(bf16[512,512]{1,0:T(8,128)(2,1)S(1)} %copy-done.2, bf16[512,512]{1,0:T(8,128)(2,1)S(1)} %copy-done, bf16[512,512]{1,0:T(8,128)(2,1)S(1)} %copy-done.1, bf16[128,512]{1,0:T(8,128)(2,1)S(1)} %collective-permute-done.1.rim_ref, bf16[128,512]{1,0:T(8,128)(2,1)S(1)} %copy-done.3), custom_call_target="tpu_custom_call" | custom-call | flops 10000000 | bytes 3072 | tf_op jit(solution)/shard_map/hyena/pallas_call | solution.py:256
  96.6 6.3 %collective-permute-done.10 = bf16[4,256,512]{2,1,0:T(8,128)(2,1)S(1)} collective-permute-done((bf16[4,256,512]{2,1,0:T(8,128)(2,1)}, bf16[4,256,512]{2,1,0:T(8,128)(2,1)S(1)}, u32[]{:S(2)}, u32[]{:S(2)}) %collective-permute-start.10) | collective-permute-done | bytes 1048608 | tf_op jit(solution)/shard_map/ppermute | solution.py:312
  103.4 1.9 %collective-permute-done.12 = bf16[2,256,512]{2,1,0:T(8,128)(2,1)S(1)} collective-permute-done((bf16[2,256,512]{2,1,0:T(8,128)(2,1)}, bf16[2,256,512]{2,1,0:T(8,128)(2,1)S(1)}, u32[]{:S(2)}, u32[]{:S(2)}) %collective-permute-start.12) | collective-permute-done | bytes 524320 | tf_op jit(solution)/shard_map/ppermute | solution.py:313
  105.8 0.9 collective-permute-start.14
  106.7 1.4 %collective-permute-start.15 = (bf16[256,512]{1,0:T(8,128)(2,1)S(1)}, bf16[256,512]{1,0:T(8,128)(2,1)S(1)}, u32[]{:S(2)}, u32[]{:S(2)}) collective-permute-start(bf16[256,512]{1,0:T(8,128)(2,1)S(1)} %get-tuple-element.52), channel_id=1, source_target_pairs={{0,4},{1,5},{2,6},{3,7},{4,8},{5,9},{6,10},{7,11},{8,12},{9,13},{1... | collective-permute-start | bytes 786440 | tf_op jit(solution)/shard_map/ppermute | solution.py:321
  108.1 1.9 %collective-permute-start.17 = (bf16[256,512]{1,0:T(8,128)(2,1)S(1)}, bf16[256,512]{1,0:T(8,128)(2,1)S(1)}, u32[]{:S(2)}, u32[]{:S(2)}) collective-permute-start(bf16[256,512]{1,0:T(8,128)(2,1)S(1)} %get-tuple-element.53), channel_id=1, source_target_pairs={{0,12},{1,13},{2,14},{3,15},{4,0},{5,1},{6,2},{7,3},{8,4},{9,5},{1... | collective-permute-start | bytes 786440 | tf_op jit(solution)/shard_map/ppermute | solution.py:321
  110.0 0.9 collective-permute-start.16
  110.8 2.9 %collective-permute-done.14 = bf16[256,512]{1,0:T(8,128)(2,1)S(1)} collective-permute-done((bf16[256,512]{1,0:T(8,128)(2,1)S(1)}, bf16[256,512]{1,0:T(8,128)(2,1)S(1)}, u32[]{:S(2)}, u32[]{:S(2)}) %collective-permute-start.14) | collective-permute-done | bytes 262176 | tf_op jit(solution)/shard_map/ppermute | solution.py:329
  113.8 1.9 %collective-permute-done.15 = bf16[256,512]{1,0:T(8,128)(2,1)S(1)} collective-permute-done((bf16[256,512]{1,0:T(8,128)(2,1)S(1)}, bf16[256,512]{1,0:T(8,128)(2,1)S(1)}, u32[]{:S(2)}, u32[]{:S(2)}) %collective-permute-start.15) | collective-permute-done | bytes 262176 | tf_op jit(solution)/shard_map/ppermute | solution.py:321
  115.7 1.7 %collective-permute-done.17 = bf16[256,512]{1,0:T(8,128)(2,1)S(1)} collective-permute-done((bf16[256,512]{1,0:T(8,128)(2,1)S(1)}, bf16[256,512]{1,0:T(8,128)(2,1)S(1)}, u32[]{:S(2)}, u32[]{:S(2)}) %collective-permute-start.17) | collective-permute-done | bytes 262176 | tf_op jit(solution)/shard_map/ppermute | solution.py:321
  117.3 5.0 %collective-permute-done.16 = bf16[256,512]{1,0:T(8,128)(2,1)S(1)} collective-permute-done((bf16[256,512]{1,0:T(8,128)(2,1)S(1)}, bf16[256,512]{1,0:T(8,128)(2,1)S(1)}, u32[]{:S(2)}, u32[]{:S(2)}) %collective-permute-start.16) | collective-permute-done | bytes 262176 | tf_op jit(solution)/shard_map/ppermute | solution.py:321
  122.8 0.8 pad_maximum_fusion.1
  (49 shorter events, 3.8 us)
Async XLA Ops:
  0.6 17.2 %collective-permute-start = (bf16[512,8192]{1,0:T(8,128)(2,1)}, bf16[512,8192]{1,0:T(8,128)(2,1)}, u32[]{:S(2)}, u32[]{:S(2)}) collective-permute-start(bf16[512,8192]{1,0:T(8,128)(2,1)} %w_own.1), channel_id=1, source_target_pairs={{0,1},{1,0},{2,3},{3,2},{4,5},{5,4},{6,7},{7,6},{8,9},{9,8},{10,11... | collective-permute-start | bytes 25165832 | tf_op jit(solution)/shard_map/ppermute | solution.py:291
  7.2 5.5 %copy-start.11 = (bf16[512,256]{1,0:T(8,128)(2,1)S(1)}, bf16[512,256]{1,0:T(8,128)(2,1)}, u32[]{:S(2)}) copy-start(bf16[512,256]{1,0:T(8,128)(2,1)} %get-tuple-element.26) | copy-start | bytes 786436
  7.2 10.7 %slice-start = ((bf16[512,512]{1,0:T(8,128)(2,1)}), bf16[128,512]{1,0:T(8,128)(2,1)S(1)}, s32[]{:S(2)}) async-start(bf16[512,512]{1,0:T(8,128)(2,1)} %k_ref.5), calls=%async_computation.1 | async-start | bytes 262144 | tf_op jit(solution)/shard_map/slice | solution.py:298
  7.2 10.7 %slice-start.1 = ((bf16[512,512]{1,0:T(8,128)(2,1)}), bf16[128,512]{1,0:T(8,128)(2,1)S(1)}, s32[]{:S(2)}) async-start(bf16[512,512]{1,0:T(8,128)(2,1)} %v_ref.5), calls=%async_computation.2 | async-start | bytes 262144 | tf_op jit(solution)/shard_map/slice | solution.py:298
  7.2 14.7 %copy-start.10 = (s32[4096]{0:T(1024)S(1)}, s32[4096]{0:T(1024)}, u32[]{:S(2)}) copy-start(s32[4096]{0:T(1024)} %param.16) | copy-start | bytes 49156
  7.2 40.9 %copy-start.4 = (s32[6]{0:T(128)S(1)}, s32[6]{0:T(128)}, u32[]{:S(2)}) copy-start(s32[6]{0:T(128)} %stack.27.place) | copy-start | bytes 76
  7.2 40.1 %all-to-all-start = ((bf16[4,512,384]{2,1,0:T(8,128)(2,1)}), bf16[4,512,384]{2,1,0:T(8,128)(2,1)S(1)}, u32[]{:S(2)}, u32[]{:S(2)}) async-start(bf16[4,512,384]{2,1,0:T(8,128)(2,1)} %pack.1), calls=%async_computation | async-start | bytes 3145728 | tf_op jit(solution)/shard_map/all_to_all | solution.py:296
  12.7 35.4 %collective-permute-start.2 = (bf16[512,256]{1,0:T(8,128)(2,1)S(1)}, bf16[512,256]{1,0:T(8,128)(2,1)S(1)}, u32[]{:S(2)}, u32[]{:S(2)}) collective-permute-start(bf16[512,256]{1,0:T(8,128)(2,1)S(1)} %copy-done.11), channel_id=1, source_target_pairs={{0,64},{16,80},{32,96},{48,112},{1,65},{17,81},{33,97},{49,113},{2... | collective-permute-start | bytes 786440 | tf_op jit(solution)/shard_map/ppermute | solution.py:295
  14.0 34.1 %collective-permute-start.3 = (bf16[512,256]{1,0:T(8,128)(2,1)}, bf16[512,256]{1,0:T(8,128)(2,1)S(1)}, u32[]{:S(2)}, u32[]{:S(2)}) collective-permute-start(bf16[512,256]{1,0:T(8,128)(2,1)} %get-tuple-element.32), channel_id=1, source_target_pairs={{0,80},{16,96},{32,112},{48,64},{1,81},{17,97},{33,113},{49,65},{2... | collective-permute-start | bytes 786440 | tf_op jit(solution)/shard_map/ppermute | solution.py:295
  15.3 32.8 %collective-permute-start.4 = (bf16[512,256]{1,0:T(8,128)(2,1)}, bf16[512,256]{1,0:T(8,128)(2,1)S(1)}, u32[]{:S(2)}, u32[]{:S(2)}) collective-permute-start(bf16[512,256]{1,0:T(8,128)(2,1)} %get-tuple-element.33), channel_id=1, source_target_pairs={{0,96},{16,112},{32,64},{48,80},{1,97},{17,113},{33,65},{49,81},{2... | collective-permute-start | bytes 786440 | tf_op jit(solution)/shard_map/ppermute | solution.py:295
  16.6 31.5 %collective-permute-start.5 = (bf16[512,256]{1,0:T(8,128)(2,1)}, bf16[512,256]{1,0:T(8,128)(2,1)S(1)}, u32[]{:S(2)}, u32[]{:S(2)}) collective-permute-start(bf16[512,256]{1,0:T(8,128)(2,1)} %get-tuple-element.34), channel_id=1, source_target_pairs={{0,112},{16,64},{32,80},{48,96},{1,113},{17,65},{33,81},{49,97},{2... | collective-permute-start | bytes 786440 | tf_op jit(solution)/shard_map/ppermute | solution.py:295
  17.9 30.1 %collective-permute-start.1 = (bf16[128,512]{1,0:T(8,128)(2,1)S(1)}, bf16[128,512]{1,0:T(8,128)(2,1)S(1)}, u32[]{:S(2)}, u32[]{:S(2)}) collective-permute-start(bf16[128,512]{1,0:T(8,128)(2,1)S(1)} %multiply_convert_fusion), channel_id=1, source_target_pairs={{0,16},{16,32},{32,48},{48,64},{64,80},{80,96},{96,112},{1,17},{17... | collective-permute-start | bytes 393224 | tf_op jit(solution)/shard_map/ppermute | solution.py:300
  55.2 8.5 %collective-permute-start.6 = (bf16[512,128]{1,0:T(8,128)(2,1)S(1)}, bf16[512,128]{1,0:T(8,128)(2,1)S(1)}, u32[]{:S(2)}, u32[]{:S(2)}) collective-permute-start(bf16[512,128]{1,0:T(8,128)(2,1)S(1)} %get-tuple-element.35), channel_id=1, source_target_pairs={{0,16},{16,32},{32,48},{48,0},{64,80},{80,96},{96,112},{112,64},{1... | collective-permute-start | bytes 393224 | tf_op jit(solution)/shard_map/ppermute | solution.py:305
  55.3 9.3 %collective-permute-start.7 = (bf16[512,128]{1,0:T(8,128)(2,1)S(1)}, bf16[512,128]{1,0:T(8,128)(2,1)S(1)}, u32[]{:S(2)}, u32[]{:S(2)}) collective-permute-start(bf16[512,128]{1,0:T(8,128)(2,1)S(1)} %get-tuple-element.36), channel_id=1, source_target_pairs={{0,32},{16,48},{32,0},{48,16},{64,96},{80,112},{96,64},{112,80},{1... | collective-permute-start | bytes 393224 | tf_op jit(solution)/shard_map/ppermute | solution.py:305
  59.0 5.6 %collective-permute-start.8 = (bf16[512,128]{1,0:T(8,128)(2,1)S(1)}, bf16[512,128]{1,0:T(8,128)(2,1)S(1)}, u32[]{:S(2)}, u32[]{:S(2)}) collective-permute-start(bf16[512,128]{1,0:T(8,128)(2,1)S(1)} %get-tuple-element.37), channel_id=1, source_target_pairs={{0,48},{16,0},{32,16},{48,32},{64,112},{80,64},{96,80},{112,96},{1... | collective-permute-start | bytes 393224 | tf_op jit(solution)/shard_map/ppermute | solution.py:305
  64.7 2.1 %copy-start.5 = (bf16[2048,128]{1,0:T(8,128)(2,1)}, bf16[2048,128]{1,0:T(8,128)(2,1)S(1)}, u32[]{:S(2)}) copy-start(bf16[2048,128]{1,0:T(8,128)(2,1)S(1)} %pad_maximum_fusion.own_ref) | copy-start | bytes 1572868
  64.7 20.4 %copy-start = (bf16[512,512]{1,0:T(8,128)(2,1)S(1)}, bf16[512,512]{1,0:T(8,128)(2,1)}, u32[]{:S(2)}) copy-start(bf16[512,512]{1,0:T(8,128)(2,1)} %k_ref.5) | copy-start | bytes 1572868
  64.7 20.4 %copy-start.1 = (bf16[512,512]{1,0:T(8,128)(2,1)S(1)}, bf16[512,512]{1,0:T(8,128)(2,1)}, u32[]{:S(2)}) copy-start(bf16[512,512]{1,0:T(8,128)(2,1)} %v_ref.5) | copy-start | bytes 1572868
  64.7 20.4 %copy-start.2 = (bf16[512,512]{1,0:T(8,128)(2,1)S(1)}, bf16[512,512]{1,0:T(8,128)(2,1)}, u32[]{:S(2)}) copy-start(bf16[512,512]{1,0:T(8,128)(2,1)} %q_ref.2) | copy-start | bytes 1572868
  64.7 20.4 %copy-start.3 = (bf16[128,512]{1,0:T(8,128)(2,1)S(1)}, bf16[128,512]{1,0:T(8,128)(2,1)}, u32[]{:S(2)}) copy-start(bf16[128,512]{1,0:T(8,128)(2,1)} %f_ref.1) | copy-start | bytes 393220
  64.7 2.0 %collective-permute-start.9 = (bf16[2048,128]{1,0:T(8,128)(2,1)S(1)}, bf16[2048,128]{1,0:T(8,128)(2,1)S(1)}, u32[]{:S(2)}, u32[]{:S(2)}) collective-permute-start(bf16[2048,128]{1,0:T(8,128)(2,1)S(1)} %pad_maximum_fusion.own_ref), channel_id=1, source_target_pairs={{0,1},{1,0},{2,3},{3,2},{4,5},{5,4},{6,7},{7,6},{8,9},{9,8},{10,11... | collective-permute-start | bytes 1572872 | tf_op jit(solution)/shard_map/ppermute | solution.py:308
  77.4 25.5 %copy-start.7 = (bf16[4,256,512]{2,1,0:T(8,128)(2,1)S(1)}, bf16[4,256,512]{2,1,0:T(8,128)(2,1)}, u32[]{:S(2)}) copy-start(bf16[4,256,512]{2,1,0:T(8,128)(2,1)} %get-tuple-element.38) | copy-start | bytes 3145732
  77.4 25.5 %collective-permute-start.10 = (bf16[4,256,512]{2,1,0:T(8,128)(2,1)}, bf16[4,256,512]{2,1,0:T(8,128)(2,1)S(1)}, u32[]{:S(2)}, u32[]{:S(2)}) collective-permute-start(bf16[4,256,512]{2,1,0:T(8,128)(2,1)} %get-tuple-element.40), channel_id=1, source_target_pairs={{0,2},{1,3},{2,0},{3,1},{4,6},{5,7},{6,4},{7,5},{8,10},{9,11},{10,... | collective-permute-start | bytes 3145736 | tf_op jit(solution)/shard_map/ppermute | solution.py:312
  78.7 24.7 %collective-permute-start.11 = (bf16[2,256,512]{2,1,0:T(8,128)(2,1)}, bf16[2,256,512]{2,1,0:T(8,128)(2,1)S(1)}, u32[]{:S(2)}, u32[]{:S(2)}) collective-permute-start(bf16[2,256,512]{2,1,0:T(8,128)(2,1)} %get-tuple-element.43), channel_id=1, source_target_pairs={{0,8},{1,9},{2,10},{3,11},{4,12},{5,13},{6,14},{7,15},{8,0},{9,1},... | collective-permute-start | bytes 1572872 | tf_op jit(solution)/shard_map/ppermute | solution.py:313
  81.9 23.4 %collective-permute-start.12 = (bf16[2,256,512]{2,1,0:T(8,128)(2,1)}, bf16[2,256,512]{2,1,0:T(8,128)(2,1)S(1)}, u32[]{:S(2)}, u32[]{:S(2)}) collective-permute-start(bf16[2,256,512]{2,1,0:T(8,128)(2,1)} %get-tuple-element.44), channel_id=1, source_target_pairs={{0,4},{1,5},{2,6},{3,7},{4,8},{5,9},{6,10},{7,11},{8,12},{9,13},{1... | collective-permute-start | bytes 1572872 | tf_op jit(solution)/shard_map/ppermute | solution.py:313
  82.5 23.1 %collective-permute-start.13 = (bf16[2,256,512]{2,1,0:T(8,128)(2,1)}, bf16[2,256,512]{2,1,0:T(8,128)(2,1)S(1)}, u32[]{:S(2)}, u32[]{:S(2)}) collective-permute-start(bf16[2,256,512]{2,1,0:T(8,128)(2,1)} %get-tuple-element.45), channel_id=1, source_target_pairs={{0,12},{1,13},{2,14},{3,15},{4,0},{5,1},{6,2},{7,3},{8,4},{9,5},{1... | collective-permute-start | bytes 1572872 | tf_op jit(solution)/shard_map/ppermute | solution.py:313
  96.6 9.1 %copy-start.8 = (bf16[2,256,512]{2,1,0:T(8,128)(2,1)S(1)}, bf16[2,256,512]{2,1,0:T(8,128)(2,1)}, u32[]{:S(2)}) copy-start(bf16[2,256,512]{2,1,0:T(8,128)(2,1)} %get-tuple-element.42) | copy-start | bytes 1572868
  103.3 19.1 %copy-start.6 = (bf16[512,512]{1,0:T(8,128)(2,1)S(1)}, bf16[512,512]{1,0:T(8,128)(2,1)}, u32[]{:S(2)}) copy-start(bf16[512,512]{1,0:T(8,128)(2,1)} %hyena.1) | copy-start | bytes 1572868
  105.8 7.9 %collective-permute-start.14 = (bf16[256,512]{1,0:T(8,128)(2,1)S(1)}, bf16[256,512]{1,0:T(8,128)(2,1)S(1)}, u32[]{:S(2)}, u32[]{:S(2)}) collective-permute-start(bf16[256,512]{1,0:T(8,128)(2,1)S(1)} %fusion.7), channel_id=1, source_target_pairs={{0,2},{1,3},{2,0},{3,1},{4,6},{5,7},{6,4},{7,5},{8,10},{9,11},{10,... | collective-permute-start | bytes 786440 | tf_op jit(solution)/shard_map/ppermute | solution.py:329
  106.7 8.9 %collective-permute-start.15 = (bf16[256,512]{1,0:T(8,128)(2,1)S(1)}, bf16[256,512]{1,0:T(8,128)(2,1)S(1)}, u32[]{:S(2)}, u32[]{:S(2)}) collective-permute-start(bf16[256,512]{1,0:T(8,128)(2,1)S(1)} %get-tuple-element.52), channel_id=1, source_target_pairs={{0,4},{1,5},{2,6},{3,7},{4,8},{5,9},{6,10},{7,11},{8,12},{9,13},{1... | collective-permute-start | bytes 786440 | tf_op jit(solution)/shard_map/ppermute | solution.py:321
  108.1 9.2 %collective-permute-start.17 = (bf16[256,512]{1,0:T(8,128)(2,1)S(1)}, bf16[256,512]{1,0:T(8,128)(2,1)S(1)}, u32[]{:S(2)}, u32[]{:S(2)}) collective-permute-start(bf16[256,512]{1,0:T(8,128)(2,1)S(1)} %get-tuple-element.53), channel_id=1, source_target_pairs={{0,12},{1,13},{2,14},{3,15},{4,0},{5,1},{6,2},{7,3},{8,4},{9,5},{1... | collective-permute-start | bytes 786440 | tf_op jit(solution)/shard_map/ppermute | solution.py:321
  110.0 12.4 %collective-permute-start.16 = (bf16[256,512]{1,0:T(8,128)(2,1)S(1)}, bf16[256,512]{1,0:T(8,128)(2,1)S(1)}, u32[]{:S(2)}, u32[]{:S(2)}) collective-permute-start(bf16[256,512]{1,0:T(8,128)(2,1)S(1)} %get-tuple-element.54), channel_id=1, source_target_pairs={{0,8},{1,9},{2,10},{3,11},{4,12},{5,13},{6,14},{7,15},{8,0},{9,1},... | collective-permute-start | bytes 786440 | tf_op jit(solution)/shard_map/ppermute | solution.py:321
  (1 other events, 0.8 us)

commit v2 on v1

v2 whole, which is shorter than its diff:
```python
import functools
import math

import jax
import jax.numpy as jnp
from jax import lax
from jax.experimental import pallas as pl
from jax.experimental.pallas import tpu as pltpu
from jax.sharding import PartitionSpec as P

HEAD_DIM = 128
ROWS = 512
A_ROWS = 288
B_ROWS = ROWS - A_ROWS
HALF = 2048
BK = 512
SCALE = HEAD_DIM ** -0.5
LOG2E = math.log2(math.e)
F32 = jnp.float32
BF16 = jnp.bfloat16
MIB = 1024 * 1024


def z_pairs(by):
    return [(i, (i // 4) * 4 + (i % 4 + by) % 4) for i in range(8)]


def cross_pairs(by):
    return [(i, 4 + (i + by) % 4) for i in range(4)]


def y_pairs(by):
    return [(i, ((i // 4 + by) % 4) * 4 + i % 4) for i in range(16)]


def flip_pairs(mask):
    return [(i, i ^ mask) for i in range(16)]


def vmem_specs(count):
    return [pl.BlockSpec(memory_space=pltpu.VMEM)] * count


DIRECT = (0, 1, 3)


def pack_kernel(q_ref, k_ref, v_ref, all_ref, *outs):
    for to in range(4):
        for i, ref in enumerate((q_ref, k_ref, v_ref)):
            all_ref[to, :, i * 128 : i * 128 + 128] = ref[:, to * 128 : to * 128 + 128]
    z = lax.rem(lax.axis_index("ctx"), 4)
    for out, by in zip(outs, DIRECT):
        cols = pl.ds(pl.multiple_of(lax.rem(z + by, 4) * 128, 128), 128)
        out[:, 0:128] = k_ref[:, cols]
        out[:, 128:256] = v_ref[:, cols]


def pack(q, k, v):
    return pl.pallas_call(
        pack_kernel,
        in_specs=vmem_specs(3),
        out_specs=vmem_specs(4),
        out_shape=[jax.ShapeDtypeStruct((4, ROWS, 384), BF16)] + [jax.ShapeDtypeStruct((ROWS, 256), BF16)] * 3,
        name="pack",
        compiler_params=pltpu.CompilerParams(vmem_limit_bytes=60 * MIB),
        cost_estimate=pl.CostEstimate(flops=0, bytes_accessed=4 * MIB, transcendentals=0),
    )(q, k, v)


def document_starts(ids):
    starts = jnp.zeros(ids.shape, jnp.int32)
    for value in range(5):
        count = jnp.sum(jnp.where(ids == value, 1.0, 0.0)).astype(jnp.int32)
        starts = starts + jnp.where(ids > value, count, 0)
    return starts


def softmax_step(query, key, val, allowed, before):
    scores = lax.dot_general(key, query, (((1,), (1,)), ((), ())), preferred_element_type=F32)
    scores = jnp.where(allowed, scores, -1e30)
    top = jnp.max(scores, axis=0, keepdims=True)
    if before is not None:
        top = jnp.maximum(before[0], top)
    probs = jnp.exp2((scores - top) * (SCALE * LOG2E))
    total = jnp.sum(probs, axis=0, keepdims=True)
    out = lax.dot_general(val, probs.astype(BF16), (((0,), (0,)), ((), ())), preferred_element_type=F32)
    if before is not None:
        factor = jnp.exp2((before[0] - top) * (SCALE * LOG2E))
        total = total + before[1] * factor
        out = out + before[2] * factor
    return top, total, out


def attend_own_kernel(place, ids_ref, qkv_ref, acc_ref, stat_ref, start_s):
    start_s[...] = document_starts(ids_ref[...]) - place[1] * HALF
    key_iota = lax.broadcasted_iota(jnp.int32, (BK, ROWS), 0)
    diff_iota = key_iota - lax.broadcasted_iota(jnp.int32, (BK, ROWS), 1)
    for at in range(4):
        query = qkv_ref[at, :, 0:128]
        bound = start_s[pl.ds(place[1] * 4 + at, 1), :]

        def put(result, at=at):
            stat_ref[at, 0:1, :], stat_ref[at, 8:9, :], acc_ref[at] = result

        allowed = (key_iota >= bound - at * BK) & (diff_iota <= 0)
        put(softmax_step(query, qkv_ref[at, :, 128:256], qkv_ref[at, :, 256:384], allowed, None))

        def body(i, carry, at=at, query=query, bound=bound, put=put):
            block = at - 1 - i
            before = (stat_ref[at, 0:1, :], stat_ref[at, 8:9, :], acc_ref[at])
            key, val = qkv_ref[block, :, 128:256], qkv_ref[block, :, 256:384]
            put(softmax_step(query, key, val, key_iota >= bound - block * BK, before))
            return carry

        lax.fori_loop(0, at - jnp.maximum(jnp.min(bound), 0) // BK, body, 0)


def attend_own(place, ids, qkv):
    return pl.pallas_call(
        attend_own_kernel,
        grid_spec=pltpu.PrefetchScalarGridSpec(
            num_scalar_prefetch=1,
            grid=(),
            in_specs=vmem_specs(2),
            out_specs=vmem_specs(2),
            scratch_shapes=[pltpu.VMEM((8, ROWS), jnp.int32)],
        ),
        out_shape=[jax.ShapeDtypeStruct((4, 128, ROWS), F32), jax.ShapeDtypeStruct((4, 16, ROWS), F32)],
        name="attend_own",
        compiler_params=pltpu.CompilerParams(vmem_limit_bytes=16 * MIB),
        cost_estimate=pl.CostEstimate(flops=4 * 10**9, bytes_accessed=4 * MIB, transcendentals=4 * 10**6),
    )(place, ids, qkv)


def attend_earlier_kernel(order, place, ids_ref, qkv_ref, *rest):
    cross, (acc_ref, stat_ref) = rest[:4], rest[4:6]
    outs = rest[6 : 6 + len(order)]
    kv_s, start_s, stat_s, acc_s = rest[6 + len(order) :]
    for by in range(4):
        kv_s[lax.rem(place[0] + 4 - by, 4)] = cross[by][...]
    start_s[...] = document_starts(ids_ref[...])
    key_iota = lax.broadcasted_iota(jnp.int32, (BK, ROWS), 0)
    for out, by in zip(outs, order):
        at = lax.rem(place[0] + by, 4)
        query = qkv_ref[at, :, 0:128]
        bound = start_s[pl.ds(place[1] * 4 + at, 1), :]
        stat_s[...] = stat_ref[at]
        acc_s[...] = acc_ref[at]

        def body(i, carry, query=query, bound=bound):
            block = 3 - i
            before = (stat_s[0:1, :], stat_s[8:9, :], acc_s[...])
            result = softmax_step(query, kv_s[block, :, 0:128], kv_s[block, :, 128:256], key_iota >= bound - block * BK, before)
            stat_s[0:1, :], stat_s[8:9, :], acc_s[...] = result
            return carry

        lax.fori_loop(0, place[1] * jnp.maximum(4 - jnp.min(bound) // BK, 0), body, 0)
        out[...] = jnp.transpose(acc_s[...] / stat_s[8:9, :]).astype(BF16)


def attend_earlier(order, place, ids, qkv, cross, acc, stat):
    return pl.pallas_call(
        functools.partial(attend_earlier_kernel, order),
        grid_spec=pltpu.PrefetchScalarGridSpec(
            num_scalar_prefetch=1,
            grid=(),
            in_specs=vmem_specs(8),
            out_specs=vmem_specs(len(order)),
            scratch_shapes=[
                pltpu.VMEM((4, ROWS, 256), BF16),
                pltpu.VMEM((8, ROWS), jnp.int32),
                pltpu.VMEM((16, ROWS), F32),
                pltpu.VMEM((128, ROWS), F32),
            ],
        ),
        out_shape=[jax.ShapeDtypeStruct((ROWS, 128), BF16)] * len(order),
        name="attend_earlier",
        compiler_params=pltpu.CompilerParams(vmem_limit_bytes=16 * MIB),
        cost_estimate=pl.CostEstimate(
            flops=len(order) * 10**9, bytes_accessed=4 * MIB, transcendentals=len(order) * 10**6
        ),
    )(place, ids, qkv, *cross, acc, stat)


BLOCKS = [(0, 1), (1, 1), (2, 1), (3, 1), (2, 0), (1, 0), (3, 0), (0, 0)]


def project_kernel(place, own_ref, sib_ref, w_own, w_sib, *rest):
    a_refs, b_refs = rest[:4], rest[4:6]
    att, weights, staged, in_sem, out_sem, att_sem = rest[6:]
    z = place[0]
    copies = []
    for j, (d, e) in enumerate(BLOCKS):
        block = (lax.rem(place[2] + d, 4) * 2 + lax.rem(place[3] + e, 2)) * 2 + place[4]
        cols = pl.ds(pl.multiple_of(block * 512, 512), 512)
        pair = []
        for i, ref in enumerate((w_own, w_sib)):
            pair.append(pltpu.make_async_copy(ref.at[:, cols], weights.at[j, pl.ds(i * 512, 512), :], in_sem.at[j, i]))
        copies.append(pair)
    loads = []
    for by in range(4):
        col = pl.multiple_of(lax.rem(z + 4 - by, 4) * 128, 128)
        rows = pl.ds(by * ROWS, ROWS)
        for i, ref in enumerate((own_ref, sib_ref)):
            loads.append(pltpu.make_async_copy(ref.at[rows, :], att.at[:, pl.ds(i * 512 + col, 128)], att_sem.at[by, i]))
    for copy in copies[0] + loads + copies[1]:
        copy.start()
    for copy in loads:
        copy.wait()
    stores = []
    for j, (d, e) in enumerate(BLOCKS):
        for copy in copies[j]:
            copy.wait()
        if j + 2 < len(BLOCKS):
            for copy in copies[j + 2]:
                copy.start()
        staged[j] = jnp.dot(att[...], weights[j], preferred_element_type=F32).astype(BF16)
        stores.append(pltpu.make_async_copy(staged.at[j, pl.ds(0, A_ROWS), :], a_refs[d].at[e], out_sem.at[j, 0]))
        stores.append(pltpu.make_async_copy(staged.at[j, pl.ds(A_ROWS, B_ROWS), :], b_refs[e].at[d], out_sem.at[j, 1]))
        stores[-2].start()
        stores[-1].start()
    for copy in stores:
        copy.wait()


def project(place, own, sib, w_own, w_sib):
    anywhere = pl.BlockSpec(memory_space=pl.ANY)
    return pl.pallas_call(
        project_kernel,
        grid_spec=pltpu.PrefetchScalarGridSpec(
            num_scalar_prefetch=1,
            grid=(),
            in_specs=[anywhere] * 4,
            out_specs=[anywhere] * 6,
            scratch_shapes=[
                pltpu.VMEM((ROWS, 1024), BF16),
                pltpu.VMEM((8, 1024, 512), BF16),
                pltpu.VMEM((8, ROWS, 512), BF16),
                pltpu.SemaphoreType.DMA((8, 2)),
                pltpu.SemaphoreType.DMA((8, 2)),
                pltpu.SemaphoreType.DMA((4, 2)),
            ],
        ),
        out_shape=[jax.ShapeDtypeStruct((2, A_ROWS, 512), BF16)] * 4 + [jax.ShapeDtypeStruct((4, B_ROWS, 512), BF16)] * 2,
        name="project",
        compiler_params=pltpu.CompilerParams(vmem_limit_bytes=56 * MIB),
        cost_estimate=pl.CostEstimate(flops=8 * 2 * ROWS * 1024 * 512, bytes_accessed=14 * MIB, transcendentals=0),
    )(place, own, sib, w_own, w_sib)


def hyena_kernel(q_ref, k_ref, v_ref, rim_ref, f_ref, out_ref, sig, shifted, taps):
    for lane in range(4):
        cols = slice(lane * 128, lane * 128 + 128)
        sig[0:128, :] = rim_ref[:, cols].astype(F32)
        product = k_ref[:, cols].astype(F32) * v_ref[:, cols].astype(F32)
        sig[128:640, :] = product.astype(BF16).astype(F32)
        taps[...] = f_ref[:, cols].astype(F32)
        for by in range(8):
            shifted[by, 8:640, :] = sig[8 - by : 640 - by, :]

        def block(b, carry):
            base = 128 + b * 128

            def one_shift(by, acc):
                for high in range(16):
                    tap = taps[pl.ds(high * 8 + by, 1), :]
                    acc = acc + tap * shifted[by, pl.ds(pl.multiple_of(base - high * 8, 8), 128), :]
                return acc

            acc = lax.fori_loop(0, 8, one_shift, jnp.zeros((128, 128), F32))
            rows = pl.ds(pl.multiple_of(b * 128, 128), 128)
            out_ref[rows, cols] = (q_ref[rows, cols].astype(F32) * acc).astype(BF16)
            return carry

        lax.fori_loop(0, 4, block, 0)


def hyena(q, k, v, rim, taps):
    return pl.pallas_call(
        hyena_kernel,
        in_specs=vmem_specs(5),
        out_specs=pl.BlockSpec(memory_space=pltpu.VMEM),
        scratch_shapes=[
            pltpu.VMEM((640, 128), F32),
            pltpu.VMEM((8, 640, 128), F32),
            pltpu.VMEM((128, 128), F32),
        ],
        out_shape=jax.ShapeDtypeStruct((ROWS, 512), BF16),
        name="hyena",
        compiler_params=pltpu.CompilerParams(vmem_limit_bytes=12 * MIB),
        cost_estimate=pl.CostEstimate(flops=10**7, bytes_accessed=3 * 1024, transcendentals=0),
    )(q, k, v, rim, taps)


def add_kernel(keep_ref, one_ref, two_ref, three_ref, send_ref, mine_ref):
    for e, out in ((1, send_ref), (0, mine_ref)):
        total = keep_ref[e].astype(F32) + one_ref[e].astype(F32)
        total = total + two_ref[e].astype(F32) + three_ref[e].astype(F32)
        out[...] = total.astype(out.dtype)


def add_terms(keep, got):
    return pl.pallas_call(
        add_kernel,
        in_specs=vmem_specs(4),
        out_specs=vmem_specs(2),
        out_shape=[jax.ShapeDtypeStruct((A_ROWS, 512), BF16), jax.ShapeDtypeStruct((A_ROWS, 512), F32)],
        name="add_terms",
        compiler_params=pltpu.CompilerParams(vmem_limit_bytes=12 * MIB),
        cost_estimate=pl.CostEstimate(flops=10**10, bytes_accessed=3 * MIB, transcendentals=0),
    )(keep, *got)


def on_device(
    hyena_query,
    hyena_key,
    hyena_value,
    hyena_filter,
    attn_query,
    attn_key,
    attn_value,
    segment_ids,
    out_weight,
):
    ctx = lax.axis_index("ctx")
    head = lax.axis_index("head")
    z = ctx % 4
    x_hi = ctx // 4
    core = head % 2
    place = jnp.stack([z, x_hi, head // 4, (head // 2) % 2, core]).astype(jnp.int32)

    w_sib = lax.ppermute(out_weight, "head", flip_pairs(1))
    packed, *to_cross = pack(attn_query, attn_key, attn_value)
    cross = [lax.ppermute(part, "ctx", cross_pairs(by)) for part, by in zip(to_cross, DIRECT)]
    own = lax.all_to_all(packed, "ctx", 0, 0, axis_index_groups=[[0, 1, 2, 3], [4, 5, 6, 7]])
    forwarded = lax.dynamic_index_in_dim(own, (z + 2) % 4, 0, keepdims=False)[:, 128:]
    cross.insert(2, lax.ppermute(forwarded, "ctx", cross_pairs(0)))

    ids = segment_ids.reshape(8, ROWS)
    late_key, late_value, _ = lax.optimization_barrier((hyena_key[384:], hyena_value[384:], w_sib))
    edge = (late_key.astype(F32) * late_value.astype(F32)).astype(BF16)
    rim = lax.ppermute(edge, "ctx", [(i, i + 1) for i in range(7)])
    acc, stat = attend_own(place, ids, own)
    acc, rim = lax.optimization_barrier((acc, rim))
    attended = attend_earlier((2, 1, 3), place, ids, own, cross, acc, stat)
    back = [lax.ppermute(part, "ctx", z_pairs(by)) for part, by in zip(attended, (2, 1, 3))]
    (kept,) = attend_earlier((0,), place, ids, own, cross, acc, stat)
    mine = jnp.concatenate([kept, back[1], back[0], back[2]], axis=0)
    sib = lax.ppermute(mine, "head", flip_pairs(1))

    *a_terms, b_keep, b_send = project(place, mine, sib, out_weight, w_sib)
    a_keep = a_terms[0]
    b_got = lax.ppermute(b_send, "head", flip_pairs(2))
    a_got = [lax.ppermute(a_terms[d], "head", y_pairs(d)) for d in (2, 1, 3)]
    late_query, _ = lax.optimization_barrier((hyena_query, b_keep))
    hyena_out = hyena(late_query, hyena_key, hyena_value, rim, hyena_filter)
    hyena_out, b_got = lax.optimization_barrier((hyena_out, b_got))

    b_sum = b_keep.astype(F32) + b_got.astype(F32)
    b_parts = [b_sum[d].astype(BF16) for d in range(4)]
    a_got, _ = lax.optimization_barrier((a_got, b_parts))
    b_terms = [lax.ppermute(b_parts[d], "head", y_pairs(d)) for d in (1, 2, 3)]

    a_part, a_mine = add_terms(a_keep, a_got)
    a_term = lax.ppermute(a_part, "head", flip_pairs(2))
    a_final = a_mine + a_term.astype(F32)
    b_final = b_sum[0]
    for term in b_terms:
        b_final = b_final + term.astype(F32)
    stream_a = (hyena_out[:A_ROWS].astype(F32) + a_final).astype(BF16)
    stream_b = (hyena_out[A_ROWS:].astype(F32) + b_final).astype(BF16)
    stream = jnp.concatenate([stream_a, stream_b], axis=0)
    return (hyena_out, stream)


def solution(mesh):
    return jax.shard_map(
        on_device,
        mesh=mesh,
        in_specs=(
            P("ctx", "head"),
            P("ctx", "head"),
            P("ctx", "head"),
            P(None, "head"),
            P("ctx", "head"),
            P("ctx", "head"),
            P("ctx", "head"),
            P(),
            P("head", None),
        ),
        out_specs=(P("ctx", "head"), P("ctx", "head")),
        check_vma=False,
    )
```

time: 123 us -> 117 us (0.951)
  waiting for transfers between devices: 49.1 us -> 46.1 us
  starting transfers between devices: 32.1 us -> 30.6 us
    ppermute x5, waiting for transfers between devices: 2.93 us -> 0.01 us  [the longest x3 0.01 us: on_device(): lax.ppermute(part, 'ctx', cross_pairs(by))]
    ppermute x1, waiting for transfers between devices: 6.27 us -> 3.46 us  [on_device(): b_got = lax.ppermute(b_send, 'head', flip_pairs(2))]
    ppermute x1, waiting for transfers between devices: 0.71 us -> 3.45 us  [on_device(): rim = lax.ppermute(edge, 'ctx', [(i, i + 1) for i in range(7)])]
    ppermute x3, waiting for transfers between devices: 0.9 us -> 3.5 us  [on_device(): lax.ppermute(part, 'ctx', z_pairs(by))]
    all_to_all x1, waiting for transfers between devices: 25.4 us -> 22.8 us  [on_device(): lax.all_to_all(packed, 'ctx', 0, 0, axis_index_groups=[[0, 1, 2, 3], [4,...]
    ppermute x3, waiting for transfers between devices: 2.3 us -> 3.83 us  [on_device(): a_got = [lax.ppermute(a_terms[d], 'head', y_pairs(d)) for d in (2, 1, 3)]]
    ppermute x3, waiting for transfers between devices: 8.61 us -> 7.14 us  [on_device(): b_terms = [lax.ppermute(b_parts[d], 'head', y_pairs(d)) for d in (1, 2, 3)]]
    ppermute x1, starting transfers between devices: 3.93 us -> 2.47 us  [on_device(): rim = lax.ppermute(edge, 'ctx', [(i, i + 1) for i in range(7)])]
  transfers between devices with their start and end apart: 19 -> 19, of which waited for: 12 -> 11; matrix products, arithmetic and copies ran while one was open for 1% -> 1% of each run, Pallas kernels for 17% -> 20%
where the time goes in v2:
time: 117 us
  waiting for transfers between devices  46.1 us (39%)
  Pallas kernels  36.9 us (32%)
  starting transfers between devices  30.6 us (26%)
  other arithmetic  1.56 us (1%)
    all_to_all x1, waiting for transfers between devices, on_device(): lax.all_to_all(packed, 'ctx', 0, 0, axis_index_groups=[[0, 1, 2, 3], [4,...  22.8 us
    pallas_call x1, Pallas kernels, hyena(): pl.pallas_call(hyena_kernel, in_specs=vmem_specs(5), out_specs=pl.BlockSp...  11.5 us
    pallas_call x1, Pallas kernels, project(): pl.pallas_call(project_kernel, grid_spec=pltpu.PrefetchScalarGridSpec(num...  9.45 us
    ppermute x3, waiting for transfers between devices, on_device(): b_terms = [lax.ppermute(b_parts[d], 'head', y_pairs(d)) for d in (1, 2, 3)]  7.14 us
    pallas_call x1, Pallas kernels, attend_own(): pl.pallas_call(attend_own_kernel, grid_spec=pltpu.PrefetchScalarGridSpec(...  7.11 us
    ppermute x3, starting transfers between devices, on_device(): a_got = [lax.ppermute(a_terms[d], 'head', y_pairs(d)) for d in (2, 1, 3)]  6.43 us
    all_to_all x1, starting transfers between devices, on_device(): lax.all_to_all(packed, 'ctx', 0, 0, axis_index_groups=[[0, 1, 2, 3], [4,...  5.45 us
    pallas_call x2, Pallas kernels, attend_earlier(): pl.pallas_call(functools.partial(attend_earlier_kernel, order), grid_spec...  5.34 us
  transfers between devices with their start and end apart: 19, of which 11 were waited for; matrix products, arithmetic and copies ran while one was open for 1% of the time, Pallas kernels for 20%

profile of v2, /device:TPU:4, one launch (start us, length us, event | category | flops | bytes accessed | tf_op | source)
XLA Modules:
  0.0 117.3 jit_solution(7531649055102691854)
XLA Ops:
  0.7 3.2 %pack.1 = (bf16[4,512,384]{2,1,0:T(8,128)(2,1)}, bf16[512,256]{1,0:T(8,128)(2,1)}, bf16[512,256]{1,0:T(8,128)(2,1)}, bf16[512,256]{1,0:T(8,128)(2,1)}) custom-call(bf16[512,512]{1,0:T(8,128)(2,1)} %q_ref.1, bf16[512,512]{1,0:T(8,128)(2,1)} %k_ref.2, bf16[512,512]{1,0:T(8,128)(2,1)} %v_ref.2), custom_call_target="tpu_custom_call" | custom-call | bytes 4194304 | tf_op jit(solution)/shard_map/pack/pallas_call | solution.py:59
  4.0 5.5 %all-to-all-start = ((bf16[4,512,384]{2,1,0:T(8,128)(2,1)}), bf16[4,512,384]{2,1,0:T(8,128)(2,1)S(1)}, u32[]{:S(2)}, u32[]{:S(2)}) async-start(bf16[4,512,384]{2,1,0:T(8,128)(2,1)} %get-tuple-element.29), calls=%async_computation | async-start | bytes 3145728 | tf_op jit(solution)/shard_map/all_to_all | solution.py:335
  9.4 1.3 %collective-permute-start = (bf16[512,256]{1,0:T(8,128)(2,1)S(1)}, bf16[512,256]{1,0:T(8,128)(2,1)S(1)}, u32[]{:S(2)}, u32[]{:S(2)}) collective-permute-start(bf16[512,256]{1,0:T(8,128)(2,1)S(1)} %copy-done.13), channel_id=1, source_target_pairs={{0,64},{16,80},{32,96},{48,112},{1,65},{17,81},{33,97},{49,113},{2... | collective-permute-start | bytes 786440 | tf_op jit(solution)/shard_map/ppermute | solution.py:334
  10.7 1.3 %collective-permute-start.1 = (bf16[512,256]{1,0:T(8,128)(2,1)S(1)}, bf16[512,256]{1,0:T(8,128)(2,1)S(1)}, u32[]{:S(2)}, u32[]{:S(2)}) collective-permute-start(bf16[512,256]{1,0:T(8,128)(2,1)S(1)} %copy-done.12), channel_id=1, source_target_pairs={{0,80},{16,96},{32,112},{48,64},{1,81},{17,97},{33,113},{49,65},{2... | collective-permute-start | bytes 786440 | tf_op jit(solution)/shard_map/ppermute | solution.py:334
  12.0 1.3 %collective-permute-start.3 = (bf16[512,256]{1,0:T(8,128)(2,1)S(1)}, bf16[512,256]{1,0:T(8,128)(2,1)S(1)}, u32[]{:S(2)}, u32[]{:S(2)}) collective-permute-start(bf16[512,256]{1,0:T(8,128)(2,1)S(1)} %copy-done.11), channel_id=1, source_target_pairs={{0,112},{16,64},{32,80},{48,96},{1,113},{17,65},{33,81},{49,97},{2... | collective-permute-start | bytes 786440 | tf_op jit(solution)/shard_map/ppermute | solution.py:334
  13.5 22.8 %all-to-all-done.qkv_ref = bf16[4,512,384]{2,1,0:T(8,128)(2,1)S(1)} async-done(((bf16[4,512,384]{2,1,0:T(8,128)(2,1)}), bf16[4,512,384]{2,1,0:T(8,128)(2,1)S(1)}, u32[]{:S(2)}, u32[]{:S(2)}) %all-to-all-start) | async-done | bytes 1572896 | tf_op jit(solution)/shard_map/all_to_all | solution.py:335
  36.5 1.3 %collective-permute-start.2 = (bf16[512,256]{1,0:T(8,128)(2,1)S(1)}, bf16[512,256]{1,0:T(8,128)(2,1)S(1)}, u32[]{:S(2)}, u32[]{:S(2)}) collective-permute-start(bf16[512,256]{1,0:T(8,128)(2,1)S(1)} %slice.40), channel_id=1, source_target_pairs={{0,64},{16,80},{32,96},{48,112},{1,65},{17,81},{33,97},{49,113},{2... | collective-permute-start | bytes 786440 | tf_op jit(solution)/shard_map/ppermute | solution.py:337
  37.8 2.5 %collective-permute-start.5 = (bf16[128,512]{1,0:T(8,128)(2,1)S(1)}, bf16[128,512]{1,0:T(8,128)(2,1)S(1)}, u32[]{:S(2)}, u32[]{:S(2)}) collective-permute-start(bf16[128,512]{1,0:T(8,128)(2,1)S(1)} %multiply_convert_fusion), channel_id=1, source_target_pairs={{0,16},{16,32},{32,48},{48,64},{64,80},{80,96},{96,112},{1,17},{17... | collective-permute-start | bytes 393224 | tf_op jit(solution)/shard_map/ppermute | solution.py:342
  40.3 7.1 %attend_own.1 = (f32[4,128,512]{2,1,0:T(8,128)S(1)}, f32[4,16,512]{2,1,0:T(8,128)S(1)}) custom-call(s32[5]{0:T(128)S(1)} %stack.23.place, s32[8,512]{1,0:T(8,128)S(1)} %reshape.10.ids_ref, bf16[4,512,384]{2,1,0:T(8,128)(2,1)S(1)} %all-to-all-done.qkv_ref), custom_call_target="tpu_custom_call" | custom-call | flops 4000000000 | bytes 4194304 | tf_op jit(solution)/shard_map/attend_own/pallas_call | solution.py:119
  47.4 3.4 %collective-permute-done.5.rim_ref = bf16[128,512]{1,0:T(8,128)(2,1)S(1)} collective-permute-done((bf16[128,512]{1,0:T(8,128)(2,1)S(1)}, bf16[128,512]{1,0:T(8,128)(2,1)S(1)}, u32[]{:S(2)}, u32[]{:S(2)}) %collective-permute-start.5) | collective-permute-done | bytes 131104 | tf_op jit(solution)/shard_map/ppermute | solution.py:342
  50.9 3.6 %attend_earlier.3 = (bf16[512,128]{1,0:T(8,128)(2,1)S(1)}, bf16[512,128]{1,0:T(8,128)(2,1)S(1)}, bf16[512,128]{1,0:T(8,128)(2,1)S(1)}) custom-call(s32[5]{0:T(128)S(1)} %stack.23.place, s32[8,512]{1,0:T(8,128)S(1)} %reshape.10.ids_ref, bf16[4,512,384]{2,1,0:T(8,128)(2,1)S(1)} %all-to-all-done.qkv_ref, bf16[512,256]{1,0:T(8,128)(2,1)S(1)} %collective-permute-done.rest_0_, ...), custom_call_target="tpu_custom_call" | custom-call | flops 3000000000 | bytes 4194304 | tf_op jit(solution)/shard_map/attend_earlier/pallas_call | solution.py:162
  55.2 2.6 %collective-permute-start.8 = (bf16[512,128]{1,0:T(8,128)(2,1)S(1)}, bf16[512,128]{1,0:T(8,128)(2,1)S(1)}, u32[]{:S(2)}, u32[]{:S(2)}) collective-permute-start(bf16[512,128]{1,0:T(8,128)(2,1)S(1)} %get-tuple-element.40), channel_id=1, source_target_pairs={{0,48},{16,0},{32,16},{48,32},{64,112},{80,64},{96,80},{112,96},{1... | collective-permute-start | bytes 393224 | tf_op jit(solution)/shard_map/ppermute | solution.py:346
  57.8 1.7 %attend_earlier.2 = bf16[512,128]{1,0:T(8,128)(2,1)S(1)} custom-call(s32[5]{0:T(128)S(1)} %stack.23.place, s32[8,512]{1,0:T(8,128)S(1)} %reshape.10.ids_ref, bf16[4,512,384]{2,1,0:T(8,128)(2,1)S(1)} %all-to-all-done.qkv_ref, bf16[512,256]{1,0:T(8,128)(2,1)S(1)} %collective-permute-done.rest_0_, bf16[512,256]{1,0:T(8,128)(2,1)S(1)} %collective-permute-done.1.rest_1_, ...), custom_call_target="tpu_custom_call" | custom-call | flops 1000000000 | bytes 4194304 | tf_op jit(solution)/shard_map/attend_earlier/pallas_call | solution.py:162
  59.6 2.8 %collective-permute-done.6 = bf16[512,128]{1,0:T(8,128)(2,1)S(1)} collective-permute-done((bf16[512,128]{1,0:T(8,128)(2,1)S(1)}, bf16[512,128]{1,0:T(8,128)(2,1)S(1)}, u32[]{:S(2)}, u32[]{:S(2)}) %collective-permute-start.6) | collective-permute-done | bytes 131104 | tf_op jit(solution)/shard_map/ppermute | solution.py:346
  62.3 0.7 collective-permute-done.8
  63.4 1.9 %collective-permute-done.9.sib_ref = bf16[2048,128]{1,0:T(8,128)(2,1)S(1)} collective-permute-done((bf16[2048,128]{1,0:T(8,128)(2,1)S(1)}, bf16[2048,128]{1,0:T(8,128)(2,1)S(1)}, u32[]{:S(2)}, u32[]{:S(2)}) %collective-permute-start.9) | collective-permute-done | bytes 524320 | tf_op jit(solution)/shard_map/ppermute | solution.py:349
  65.3 0.8 copy-done.9
  66.1 9.4 %project.1 = (bf16[2,288,512]{2,1,0:T(8,128)(2,1)}, bf16[2,288,512]{2,1,0:T(8,128)(2,1)}, bf16[2,288,512]{2,1,0:T(8,128)(2,1)}, bf16[2,288,512]{2,1,0:T(8,128)(2...) custom-call(s32[5]{0:T(128)} %copy-done.4, bf16[2048,128]{1,0:T(8,128)(2,1)} %copy-done.6, ...), custom_call_target="tpu_custom_call" | custom-call | flops 4294967296 | bytes 14680064 | tf_op jit(solution)/shard_map/project/pallas_call | solution.py:228
  75.6 1.3 %collective-permute-start.10 = (bf16[4,224,512]{2,1,0:T(8,128)(2,1)}, bf16[4,224,512]{2,1,0:T(8,128)(2,1)S(1)}, u32[]{:S(2)}, u32[]{:S(2)}) collective-permute-start(bf16[4,224,512]{2,1,0:T(8,128)(2,1)} %get-tuple-element.44), channel_id=1, source_target_pairs={{0,2},{1,3},{2,0},{3,1},{4,6},{5,7},{6,4},{7,5},{8,10},{9,11},{10,... | collective-permute-start | bytes 2752520 | tf_op jit(solution)/shard_map/ppermute | solution.py:353
  76.9 3.2 %collective-permute-start.11 = (bf16[2,288,512]{2,1,0:T(8,128)(2,1)}, bf16[2,288,512]{2,1,0:T(8,128)(2,1)S(1)}, u32[]{:S(2)}, u32[]{:S(2)}) collective-permute-start(bf16[2,288,512]{2,1,0:T(8,128)(2,1)} %get-tuple-element.47), channel_id=1, source_target_pairs={{0,8},{1,9},{2,10},{3,11},{4,12},{5,13},{6,14},{7,15},{8,0},{9,1},... | collective-permute-start | bytes 1769480 | tf_op jit(solution)/shard_map/ppermute | solution.py:354
  80.7 2.6 %collective-permute-start.13 = (bf16[2,288,512]{2,1,0:T(8,128)(2,1)}, bf16[2,288,512]{2,1,0:T(8,128)(2,1)S(1)}, u32[]{:S(2)}, u32[]{:S(2)}) collective-permute-start(bf16[2,288,512]{2,1,0:T(8,128)(2,1)} %get-tuple-element.49), channel_id=1, source_target_pairs={{0,12},{1,13},{2,14},{3,15},{4,0},{5,1},{6,2},{7,3},{8,4},{9,5},{1... | collective-permute-start | bytes 1769480 | tf_op jit(solution)/shard_map/ppermute | solution.py:354
  83.3 11.5 %hyena.1 = bf16[512,512]{1,0:T(8,128)(2,1)} custom-call(bf16[512,512]{1,0:T(8,128)(2,1)S(1)} %copy-done.2, bf16[512,512]{1,0:T(8,128)(2,1)S(1)} %copy-done, bf16[512,512]{1,0:T(8,128)(2,1)S(1)} %copy-done.1, bf16[128,512]{1,0:T(8,128)(2,1)S(1)} %collective-permute-done.5.rim_ref, bf16[128,512]{1,0:T(8,128)(2,1)S(1)} %copy-done.3), custom_call_target="tpu_custom_call" | custom-call | flops 10000000 | bytes 3072 | tf_op jit(solution)/shard_map/hyena/pallas_call | solution.py:279
  94.8 3.5 %collective-permute-done.10 = bf16[4,224,512]{2,1,0:T(8,128)(2,1)S(1)} collective-permute-done((bf16[4,224,512]{2,1,0:T(8,128)(2,1)}, bf16[4,224,512]{2,1,0:T(8,128)(2,1)S(1)}, u32[]{:S(2)}, u32[]{:S(2)}) %collective-permute-start.10) | collective-permute-done | bytes 917536 | tf_op jit(solution)/shard_map/ppermute | solution.py:353
  98.7 1.6 %collective-permute-start.15 = (bf16[224,512]{1,0:T(8,128)(2,1)S(1)}, bf16[224,512]{1,0:T(8,128)(2,1)S(1)}, u32[]{:S(2)}, u32[]{:S(2)}) collective-permute-start(bf16[224,512]{1,0:T(8,128)(2,1)S(1)} %get-tuple-element.58), channel_id=1, source_target_pairs={{0,4},{1,5},{2,6},{3,7},{4,8},{5,9},{6,10},{7,11},{8,12},{9,13},{1... | collective-permute-start | bytes 688136 | tf_op jit(solution)/shard_map/ppermute | solution.py:362
  100.4 1.7 %collective-permute-start.17 = (bf16[224,512]{1,0:T(8,128)(2,1)S(1)}, bf16[224,512]{1,0:T(8,128)(2,1)S(1)}, u32[]{:S(2)}, u32[]{:S(2)}) collective-permute-start(bf16[224,512]{1,0:T(8,128)(2,1)S(1)} %get-tuple-element.59), channel_id=1, source_target_pairs={{0,12},{1,13},{2,14},{3,15},{4,0},{5,1},{6,2},{7,3},{8,4},{9,5},{1... | collective-permute-start | bytes 688136 | tf_op jit(solution)/shard_map/ppermute | solution.py:362
  102.0 2.0 %collective-permute-start.16 = (bf16[224,512]{1,0:T(8,128)(2,1)S(1)}, bf16[224,512]{1,0:T(8,128)(2,1)S(1)}, u32[]{:S(2)}, u32[]{:S(2)}) collective-permute-start(bf16[224,512]{1,0:T(8,128)(2,1)S(1)} %get-tuple-element.60), channel_id=1, source_target_pairs={{0,8},{1,9},{2,10},{3,11},{4,12},{5,13},{6,14},{7,15},{8,0},{9,1},... | collective-permute-start | bytes 688136 | tf_op jit(solution)/shard_map/ppermute | solution.py:362
  104.0 2.7 %collective-permute-done.12.two_ref = bf16[2,288,512]{2,1,0:T(8,128)(2,1)S(1)} collective-permute-done((bf16[2,288,512]{2,1,0:T(8,128)(2,1)}, bf16[2,288,512]{2,1,0:T(8,128)(2,1)S(1)}, u32[]{:S(2)}, u32[]{:S(2)}) %collective-permute-start.12) | collective-permute-done | bytes 589856 | tf_op jit(solution)/shard_map/ppermute | solution.py:354
  106.8 1.1 collective-permute-done.13.three_ref
  108.1 0.9 collective-permute-start.14
  109.0 3.3 %collective-permute-done.15 = bf16[224,512]{1,0:T(8,128)(2,1)S(1)} collective-permute-done((bf16[224,512]{1,0:T(8,128)(2,1)S(1)}, bf16[224,512]{1,0:T(8,128)(2,1)S(1)}, u32[]{:S(2)}, u32[]{:S(2)}) %collective-permute-start.15) | collective-permute-done | bytes 229408 | tf_op jit(solution)/shard_map/ppermute | solution.py:362
  112.7 3.4 %collective-permute-done.16 = bf16[224,512]{1,0:T(8,128)(2,1)S(1)} collective-permute-done((bf16[224,512]{1,0:T(8,128)(2,1)S(1)}, bf16[224,512]{1,0:T(8,128)(2,1)S(1)}, u32[]{:S(2)}, u32[]{:S(2)}) %collective-permute-start.16) | collective-permute-done | bytes 229408 | tf_op jit(solution)/shard_map/ppermute | solution.py:362
  116.5 0.8 pad_maximum_fusion.1
  (56 shorter events, 3.5 us)
Async XLA Ops:
  0.6 37.1 %collective-permute-start.4 = (bf16[512,8192]{1,0:T(8,128)(2,1)}, bf16[512,8192]{1,0:T(8,128)(2,1)}, u32[]{:S(2)}, u32[]{:S(2)}) collective-permute-start(bf16[512,8192]{1,0:T(8,128)(2,1)} %w_own.1), channel_id=1, source_target_pairs={{0,1},{1,0},{2,3},{3,2},{4,5},{5,4},{6,7},{7,6},{8,9},{9,8},{10,11... | collective-permute-start | bytes 25165832 | tf_op jit(solution)/shard_map/ppermute | solution.py:332
  3.9 6.8 %copy-start.12 = (bf16[512,256]{1,0:T(8,128)(2,1)S(1)}, bf16[512,256]{1,0:T(8,128)(2,1)}, u32[]{:S(2)}) copy-start(bf16[512,256]{1,0:T(8,128)(2,1)} %get-tuple-element.31) | copy-start | bytes 786436
  3.9 8.1 %copy-start.11 = (bf16[512,256]{1,0:T(8,128)(2,1)S(1)}, bf16[512,256]{1,0:T(8,128)(2,1)}, u32[]{:S(2)}) copy-start(bf16[512,256]{1,0:T(8,128)(2,1)} %get-tuple-element.32) | copy-start | bytes 786436
  3.9 9.5 %copy-start.10 = (s32[4096]{0:T(1024)S(1)}, s32[4096]{0:T(1024)}, u32[]{:S(2)}) copy-start(s32[4096]{0:T(1024)} %param.16) | copy-start | bytes 49156
  3.9 33.8 %slice-start = ((bf16[512,512]{1,0:T(8,128)(2,1)}), bf16[128,512]{1,0:T(8,128)(2,1)S(1)}, s32[]{:S(2)}) async-start(bf16[512,512]{1,0:T(8,128)(2,1)} %k_ref.3), calls=%async_computation.1 | async-start | bytes 262144 | tf_op jit(solution)/shard_map/slice | solution.py:340
  3.9 33.8 %slice-start.1 = ((bf16[512,512]{1,0:T(8,128)(2,1)}), bf16[128,512]{1,0:T(8,128)(2,1)S(1)}, s32[]{:S(2)}) async-start(bf16[512,512]{1,0:T(8,128)(2,1)} %v_ref.3), calls=%async_computation.2 | async-start | bytes 262144 | tf_op jit(solution)/shard_map/slice | solution.py:340
  4.0 32.4 %all-to-all-start = ((bf16[4,512,384]{2,1,0:T(8,128)(2,1)}), bf16[4,512,384]{2,1,0:T(8,128)(2,1)S(1)}, u32[]{:S(2)}, u32[]{:S(2)}) async-start(bf16[4,512,384]{2,1,0:T(8,128)(2,1)} %get-tuple-element.29), calls=%async_computation | async-start | bytes 3145728 | tf_op jit(solution)/shard_map/all_to_all | solution.py:335
  9.4 41.5 %collective-permute-start = (bf16[512,256]{1,0:T(8,128)(2,1)S(1)}, bf16[512,256]{1,0:T(8,128)(2,1)S(1)}, u32[]{:S(2)}, u32[]{:S(2)}) collective-permute-start(bf16[512,256]{1,0:T(8,128)(2,1)S(1)} %copy-done.13), channel_id=1, source_target_pairs={{0,64},{16,80},{32,96},{48,112},{1,65},{17,81},{33,97},{49,113},{2... | collective-permute-start | bytes 786440 | tf_op jit(solution)/shard_map/ppermute | solution.py:334
  10.7 40.2 %collective-permute-start.1 = (bf16[512,256]{1,0:T(8,128)(2,1)S(1)}, bf16[512,256]{1,0:T(8,128)(2,1)S(1)}, u32[]{:S(2)}, u32[]{:S(2)}) collective-permute-start(bf16[512,256]{1,0:T(8,128)(2,1)S(1)} %copy-done.12), channel_id=1, source_target_pairs={{0,80},{16,96},{32,112},{48,64},{1,81},{17,97},{33,113},{49,65},{2... | collective-permute-start | bytes 786440 | tf_op jit(solution)/shard_map/ppermute | solution.py:334
  12.0 38.9 %collective-permute-start.3 = (bf16[512,256]{1,0:T(8,128)(2,1)S(1)}, bf16[512,256]{1,0:T(8,128)(2,1)S(1)}, u32[]{:S(2)}, u32[]{:S(2)}) collective-permute-start(bf16[512,256]{1,0:T(8,128)(2,1)S(1)} %copy-done.11), channel_id=1, source_target_pairs={{0,112},{16,64},{32,80},{48,96},{1,113},{17,65},{33,81},{49,97},{2... | collective-permute-start | bytes 786440 | tf_op jit(solution)/shard_map/ppermute | solution.py:334
  13.5 44.3 %copy-start.4 = (s32[5]{0:T(128)}, s32[5]{0:T(128)S(1)}, u32[]{:S(2)}) copy-start(s32[5]{0:T(128)S(1)} %stack.23.place) | copy-start | bytes 64
  36.5 14.4 %collective-permute-start.2 = (bf16[512,256]{1,0:T(8,128)(2,1)S(1)}, bf16[512,256]{1,0:T(8,128)(2,1)S(1)}, u32[]{:S(2)}, u32[]{:S(2)}) collective-permute-start(bf16[512,256]{1,0:T(8,128)(2,1)S(1)} %slice.40), channel_id=1, source_target_pairs={{0,64},{16,80},{32,96},{48,112},{1,65},{17,81},{33,97},{49,113},{2... | collective-permute-start | bytes 786440 | tf_op jit(solution)/shard_map/ppermute | solution.py:337
  37.8 13.0 %collective-permute-start.5 = (bf16[128,512]{1,0:T(8,128)(2,1)S(1)}, bf16[128,512]{1,0:T(8,128)(2,1)S(1)}, u32[]{:S(2)}, u32[]{:S(2)}) collective-permute-start(bf16[128,512]{1,0:T(8,128)(2,1)S(1)} %multiply_convert_fusion), channel_id=1, source_target_pairs={{0,16},{16,32},{32,48},{48,64},{64,80},{80,96},{96,112},{1,17},{17... | collective-permute-start | bytes 393224 | tf_op jit(solution)/shard_map/ppermute | solution.py:342
  54.5 7.8 %collective-permute-start.6 = (bf16[512,128]{1,0:T(8,128)(2,1)S(1)}, bf16[512,128]{1,0:T(8,128)(2,1)S(1)}, u32[]{:S(2)}, u32[]{:S(2)}) collective-permute-start(bf16[512,128]{1,0:T(8,128)(2,1)S(1)} %get-tuple-element.38), channel_id=1, source_target_pairs={{0,16},{16,32},{32,48},{48,0},{64,80},{80,96},{96,112},{112,64},{1... | collective-permute-start | bytes 393224 | tf_op jit(solution)/shard_map/ppermute | solution.py:346
  54.6 7.7 %collective-permute-start.7 = (bf16[512,128]{1,0:T(8,128)(2,1)S(1)}, bf16[512,128]{1,0:T(8,128)(2,1)S(1)}, u32[]{:S(2)}, u32[]{:S(2)}) collective-permute-start(bf16[512,128]{1,0:T(8,128)(2,1)S(1)} %get-tuple-element.39), channel_id=1, source_target_pairs={{0,32},{16,48},{32,0},{48,16},{64,96},{80,112},{96,64},{112,80},{1... | collective-permute-start | bytes 393224 | tf_op jit(solution)/shard_map/ppermute | solution.py:346
  55.2 7.9 %collective-permute-start.8 = (bf16[512,128]{1,0:T(8,128)(2,1)S(1)}, bf16[512,128]{1,0:T(8,128)(2,1)S(1)}, u32[]{:S(2)}, u32[]{:S(2)}) collective-permute-start(bf16[512,128]{1,0:T(8,128)(2,1)S(1)} %get-tuple-element.40), channel_id=1, source_target_pairs={{0,48},{16,0},{32,16},{48,32},{64,112},{80,64},{96,80},{112,96},{1... | collective-permute-start | bytes 393224 | tf_op jit(solution)/shard_map/ppermute | solution.py:346
  63.1 20.2 %copy-start = (bf16[512,512]{1,0:T(8,128)(2,1)S(1)}, bf16[512,512]{1,0:T(8,128)(2,1)}, u32[]{:S(2)}) copy-start(bf16[512,512]{1,0:T(8,128)(2,1)} %k_ref.3) | copy-start | bytes 1572868
  63.1 20.2 %copy-start.1 = (bf16[512,512]{1,0:T(8,128)(2,1)S(1)}, bf16[512,512]{1,0:T(8,128)(2,1)}, u32[]{:S(2)}) copy-start(bf16[512,512]{1,0:T(8,128)(2,1)} %v_ref.3) | copy-start | bytes 1572868
  63.1 20.2 %copy-start.2 = (bf16[512,512]{1,0:T(8,128)(2,1)S(1)}, bf16[512,512]{1,0:T(8,128)(2,1)}, u32[]{:S(2)}) copy-start(bf16[512,512]{1,0:T(8,128)(2,1)} %q_ref.2) | copy-start | bytes 1572868
  63.1 20.2 %copy-start.3 = (bf16[128,512]{1,0:T(8,128)(2,1)S(1)}, bf16[128,512]{1,0:T(8,128)(2,1)}, u32[]{:S(2)}) copy-start(bf16[128,512]{1,0:T(8,128)(2,1)} %f_ref.1) | copy-start | bytes 393220
  63.2 2.2 %collective-permute-start.9 = (bf16[2048,128]{1,0:T(8,128)(2,1)S(1)}, bf16[2048,128]{1,0:T(8,128)(2,1)S(1)}, u32[]{:S(2)}, u32[]{:S(2)}) collective-permute-start(bf16[2048,128]{1,0:T(8,128)(2,1)S(1)} %pad_maximum_fusion.own_ref), channel_id=1, source_target_pairs={{0,1},{1,0},{2,3},{3,2},{4,5},{5,4},{6,7},{7,6},{8,9},{9,8},{10,11... | collective-permute-start | bytes 1572872 | tf_op jit(solution)/shard_map/ppermute | solution.py:349
  75.6 22.7 %copy-start.8 = (bf16[4,224,512]{2,1,0:T(8,128)(2,1)S(1)}, bf16[4,224,512]{2,1,0:T(8,128)(2,1)}, u32[]{:S(2)}) copy-start(bf16[4,224,512]{2,1,0:T(8,128)(2,1)} %get-tuple-element.41) | copy-start | bytes 2752516
  75.6 22.7 %collective-permute-start.10 = (bf16[4,224,512]{2,1,0:T(8,128)(2,1)}, bf16[4,224,512]{2,1,0:T(8,128)(2,1)S(1)}, u32[]{:S(2)}, u32[]{:S(2)}) collective-permute-start(bf16[4,224,512]{2,1,0:T(8,128)(2,1)} %get-tuple-element.44), channel_id=1, source_target_pairs={{0,2},{1,3},{2,0},{3,1},{4,6},{5,7},{6,4},{7,5},{8,10},{9,11},{10,... | collective-permute-start | bytes 2752520 | tf_op jit(solution)/shard_map/ppermute | solution.py:353
  76.9 25.1 %collective-permute-start.11 = (bf16[2,288,512]{2,1,0:T(8,128)(2,1)}, bf16[2,288,512]{2,1,0:T(8,128)(2,1)S(1)}, u32[]{:S(2)}, u32[]{:S(2)}) collective-permute-start(bf16[2,288,512]{2,1,0:T(8,128)(2,1)} %get-tuple-element.47), channel_id=1, source_target_pairs={{0,8},{1,9},{2,10},{3,11},{4,12},{5,13},{6,14},{7,15},{8,0},{9,1},... | collective-permute-start | bytes 1769480 | tf_op jit(solution)/shard_map/ppermute | solution.py:354
  80.1 26.7 %collective-permute-start.12 = (bf16[2,288,512]{2,1,0:T(8,128)(2,1)}, bf16[2,288,512]{2,1,0:T(8,128)(2,1)S(1)}, u32[]{:S(2)}, u32[]{:S(2)}) collective-permute-start(bf16[2,288,512]{2,1,0:T(8,128)(2,1)} %get-tuple-element.48), channel_id=1, source_target_pairs={{0,4},{1,5},{2,6},{3,7},{4,8},{5,9},{6,10},{7,11},{8,12},{9,13},{1... | collective-permute-start | bytes 1769480 | tf_op jit(solution)/shard_map/ppermute | solution.py:354
  80.7 27.1 %collective-permute-start.13 = (bf16[2,288,512]{2,1,0:T(8,128)(2,1)}, bf16[2,288,512]{2,1,0:T(8,128)(2,1)S(1)}, u32[]{:S(2)}, u32[]{:S(2)}) collective-permute-start(bf16[2,288,512]{2,1,0:T(8,128)(2,1)} %get-tuple-element.49), channel_id=1, source_target_pairs={{0,12},{1,13},{2,14},{3,15},{4,0},{5,1},{6,2},{7,3},{8,4},{9,5},{1... | collective-permute-start | bytes 1769480 | tf_op jit(solution)/shard_map/ppermute | solution.py:354
  94.8 13.0 %copy-start.5 = (bf16[2,288,512]{2,1,0:T(8,128)(2,1)S(1)}, bf16[2,288,512]{2,1,0:T(8,128)(2,1)}, u32[]{:S(2)}) copy-start(bf16[2,288,512]{2,1,0:T(8,128)(2,1)} %get-tuple-element.46.keep_ref) | copy-start | bytes 1769476
  98.7 13.6 %collective-permute-start.15 = (bf16[224,512]{1,0:T(8,128)(2,1)S(1)}, bf16[224,512]{1,0:T(8,128)(2,1)S(1)}, u32[]{:S(2)}, u32[]{:S(2)}) collective-permute-start(bf16[224,512]{1,0:T(8,128)(2,1)S(1)} %get-tuple-element.58), channel_id=1, source_target_pairs={{0,4},{1,5},{2,6},{3,7},{4,8},{5,9},{6,10},{7,11},{8,12},{9,13},{1... | collective-permute-start | bytes 688136 | tf_op jit(solution)/shard_map/ppermute | solution.py:362
  100.4 12.4 %collective-permute-start.17 = (bf16[224,512]{1,0:T(8,128)(2,1)S(1)}, bf16[224,512]{1,0:T(8,128)(2,1)S(1)}, u32[]{:S(2)}, u32[]{:S(2)}) collective-permute-start(bf16[224,512]{1,0:T(8,128)(2,1)S(1)} %get-tuple-element.59), channel_id=1, source_target_pairs={{0,12},{1,13},{2,14},{3,15},{4,0},{5,1},{6,2},{7,3},{8,4},{9,5},{1... | collective-permute-start | bytes 688136 | tf_op jit(solution)/shard_map/ppermute | solution.py:362
  102.0 14.2 %collective-permute-start.16 = (bf16[224,512]{1,0:T(8,128)(2,1)S(1)}, bf16[224,512]{1,0:T(8,128)(2,1)S(1)}, u32[]{:S(2)}, u32[]{:S(2)}) collective-permute-start(bf16[224,512]{1,0:T(8,128)(2,1)S(1)} %get-tuple-element.60), channel_id=1, source_target_pairs={{0,8},{1,9},{2,10},{3,11},{4,12},{5,13},{6,14},{7,15},{8,0},{9,1},... | collective-permute-start | bytes 688136 | tf_op jit(solution)/shard_map/ppermute | solution.py:362
  107.8 8.4 %copy-start.7 = (bf16[512,512]{1,0:T(8,128)(2,1)S(1)}, bf16[512,512]{1,0:T(8,128)(2,1)}, u32[]{:S(2)}) copy-start(bf16[512,512]{1,0:T(8,128)(2,1)} %hyena.1) | copy-start | bytes 1572868
  108.1 8.2 %collective-permute-start.14 = (bf16[288,512]{1,0:T(8,128)(2,1)S(1)}, bf16[288,512]{1,0:T(8,128)(2,1)S(1)}, u32[]{:S(2)}, u32[]{:S(2)}) collective-permute-start(bf16[288,512]{1,0:T(8,128)(2,1)S(1)} %get-tuple-element.55), channel_id=1, source_target_pairs={{0,2},{1,3},{2,0},{3,1},{4,6},{5,7},{6,4},{7,5},{8,10},{9,11},{10,... | collective-permute-start | bytes 884744 | tf_op jit(solution)/shard_map/ppermute | solution.py:365
  (3 other events, 8.5 us)

commit v3 on v2

--- a/solution.py
+++ b/solution.py
@@ -10,7 +10,7 @@
 
 HEAD_DIM = 128
 ROWS = 512
-A_ROWS = 288
+A_ROWS = 272
 B_ROWS = ROWS - A_ROWS
 HALF = 2048
 BK = 512
@@ -91,74 +91,89 @@
     return top, total, out
 
 
-def attend_own_kernel(place, ids_ref, qkv_ref, acc_ref, stat_ref, start_s):
+AWAY, HERE = (2, 1, 3), (0,)
+
+
+def attend_own_kernel(place, ids_ref, qkv_ref, *rest):
+    outs, start_s = (rest[0:3], rest[3:6]), rest[6]
     start_s[...] = document_starts(ids_ref[...]) - place[1] * HALF
     key_iota = lax.broadcasted_iota(jnp.int32, (BK, ROWS), 0)
     diff_iota = key_iota - lax.broadcasted_iota(jnp.int32, (BK, ROWS), 1)
-    for at in range(4):
-        query = qkv_ref[at, :, 0:128]
-        bound = start_s[pl.ds(place[1] * 4 + at, 1), :]
-
-        def put(result, at=at):
-            stat_ref[at, 0:1, :], stat_ref[at, 8:9, :], acc_ref[at] = result
-
-        allowed = (key_iota >= bound - at * BK) & (diff_iota <= 0)
-        put(softmax_step(query, qkv_ref[at, :, 128:256], qkv_ref[at, :, 256:384], allowed, None))
-
-        def body(i, carry, at=at, query=query, bound=bound, put=put):
-            block = at - 1 - i
-            before = (stat_ref[at, 0:1, :], stat_ref[at, 8:9, :], acc_ref[at])
-            key, val = qkv_ref[block, :, 128:256], qkv_ref[block, :, 256:384]
-            put(softmax_step(query, key, val, key_iota >= bound - block * BK, before))
-            return carry
-
-        lax.fori_loop(0, at - jnp.maximum(jnp.min(bound), 0) // BK, body, 0)
+    for order, (q_ref, acc_ref, stat_ref) in zip((AWAY, HERE), outs):
+        for i, by in enumerate(order):
+            at = lax.rem(place[0] + by, 4)
+            query = qkv_ref[at, :, 0:128]
+            q_ref[i] = query
+            bound = start_s[pl.ds(place[1] * 4 + at, 1), :]
+
+            def put(result, i=i, acc_ref=acc_ref, stat_ref=stat_ref):
+                stat_ref[i, 0:1, :], stat_ref[i, 8:9, :], acc_ref[i] = result
+
+            allowed = (key_iota >= bound - at * BK) & (diff_iota <= 0)
+            put(softmax_step(query, qkv_ref[at, :, 128:256], qkv_ref[at, :, 256:384], allowed, None))
+
+            def body(step, carry, i=i, at=at, query=query, bound=bound, put=put, acc_ref=acc_ref, stat_ref=stat_ref):
+                block = at - 1 - step
+                before = (stat_ref[i, 0:1, :], stat_ref[i, 8:9, :], acc_ref[i])
+                key, val = qkv_ref[block, :, 128:256], qkv_ref[block, :, 256:384]
+                put(softmax_step(query, key, val, key_iota >= bound - block * BK, before))
+                return carry
+
+            lax.fori_loop(0, at - jnp.maximum(jnp.min(bound), 0) // BK, body, 0)
 
 
 def attend_own(place, ids, qkv):
-    return pl.pallas_call(
+    shapes = []
+    for order in (AWAY, HERE):
+        count = len(order)
+        shapes.append(jax.ShapeDtypeStruct((count, ROWS, 128), BF16))
+        shapes.append(jax.ShapeDtypeStruct((count, 128, ROWS), F32))
+        shapes.append(jax.ShapeDtypeStruct((count, 16, ROWS), F32))
+    outs = pl.pallas_call(
         attend_own_kernel,
         grid_spec=pltpu.PrefetchScalarGridSpec(
             num_scalar_prefetch=1,
             grid=(),
             in_specs=vmem_specs(2),
-            out_specs=vmem_specs(2),
+            out_specs=vmem_specs(6),
             scratch_shapes=[pltpu.VMEM((8, ROWS), jnp.int32)],
         ),
-        out_shape=[jax.ShapeDtypeStruct((4, 128, ROWS), F32), jax.ShapeDtypeStruct((4, 16, ROWS), F32)],
+        out_shape=shapes,
         name="attend_own",
         compiler_params=pltpu.CompilerParams(vmem_limit_bytes=16 * MIB),
         cost_estimate=pl.CostEstimate(flops=4 * 10**9, bytes_accessed=4 * MIB, transcendentals=4 * 10**6),
     )(place, ids, qkv)
-
-
-def attend_earlier_kernel(order, place, ids_ref, qkv_ref, *rest):
-    cross, (acc_ref, stat_ref) = rest[:4], rest[4:6]
-    outs = rest[6 : 6 + len(order)]
-    kv_s, start_s, stat_s, acc_s = rest[6 + len(order) :]
+    return outs[0:3], outs[3:6]
+
+
+def attend_earlier_kernel(order, place, ids_ref, *rest):
+    cross, (q_ref, acc_ref, stat_ref) = rest[:4], rest[4:7]
+    outs = rest[7 : 7 + len(order)]
+    kv_s, start_s, stat_s, acc_s = rest[7 + len(order) :]
     for by in range(4):
         kv_s[lax.rem(place[0] + 4 - by, 4)] = cross[by][...]
     start_s[...] = document_starts(ids_ref[...])
     key_iota = lax.broadcasted_iota(jnp.int32, (BK, ROWS), 0)
-    for out, by in zip(outs, order):
+    for i, by in enumerate(order):
         at = lax.rem(place[0] + by, 4)
-        query = qkv_ref[at, :, 0:128]
+        query = q_ref[i]
         bound = start_s[pl.ds(place[1] * 4 + at, 1), :]
-        stat_s[...] = stat_ref[at]
-        acc_s[...] = acc_ref[at]
-
-        def body(i, carry, query=query, bound=bound):
-            block = 3 - i
+        stat_s[...] = stat_ref[i]
+        acc_s[...] = acc_ref[i]
+
+        def body(step, carry, query=query, bound=bound):
+            block = 3 - step
             before = (stat_s[0:1, :], stat_s[8:9, :], acc_s[...])
-            result = softmax_step(query, kv_s[block, :, 0:128], kv_s[block, :, 128:256], key_iota >= bound - block * BK, before)
+            key, val = kv_s[block, :, 0:128], kv_s[block, :, 128:256]
+            result = softmax_step(query, key, val, key_iota >= bound - block * BK, before)
             stat_s[0:1, :], stat_s[8:9, :], acc_s[...] = result
             return carry
 
         lax.fori_loop(0, place[1] * jnp.maximum(4 - jnp.min(bound) // BK, 0), body, 0)
-        out[...] = jnp.transpose(acc_s[...] / stat_s[8:9, :]).astype(BF16)
-
-
-def attend_earlier(order, place, ids, qkv, cross, acc, stat):
+        outs[i][...] = jnp.transpose(acc_s[...] / stat_s[8:9, :]).astype(BF16)
+
+
+def attend_earlier(order, place, ids, cross, state):
     return pl.pallas_call(
         functools.partial(attend_earlier_kernel, order),
         grid_spec=pltpu.PrefetchScalarGridSpec(
@@ -176,10 +191,8 @@
         out_shape=[jax.ShapeDtypeStruct((ROWS, 128), BF16)] * len(order),
         name="attend_earlier",
         compiler_params=pltpu.CompilerParams(vmem_limit_bytes=16 * MIB),
-        cost_estimate=pl.CostEstimate(
-            flops=len(order) * 10**9, bytes_accessed=4 * MIB, transcendentals=len(order) * 10**6
-        ),
-    )(place, ids, qkv, *cross, acc, stat)
+        cost_estimate=pl.CostEstimate(flops=len(order) * 10**6, bytes_accessed=4096, transcendentals=0),
+    )(place, ids, *cross, *state)
 
 
 BLOCKS = [(0, 1), (1, 1), (2, 1), (3, 1), (2, 0), (1, 0), (3, 0), (0, 0)]
@@ -243,7 +256,7 @@
         ),
         out_shape=[jax.ShapeDtypeStruct((2, A_ROWS, 512), BF16)] * 4 + [jax.ShapeDtypeStruct((4, B_ROWS, 512), BF16)] * 2,
         name="project",
-        compiler_params=pltpu.CompilerParams(vmem_limit_bytes=56 * MIB),
+        compiler_params=pltpu.CompilerParams(vmem_limit_bytes=52 * MIB),
         cost_estimate=pl.CostEstimate(flops=8 * 2 * ROWS * 1024 * 512, bytes_accessed=14 * MIB, transcendentals=0),
     )(place, own, sib, w_own, w_sib)
 
@@ -340,11 +353,11 @@
     late_key, late_value, _ = lax.optimization_barrier((hyena_key[384:], hyena_value[384:], w_sib))
     edge = (late_key.astype(F32) * late_value.astype(F32)).astype(BF16)
     rim = lax.ppermute(edge, "ctx", [(i, i + 1) for i in range(7)])
-    acc, stat = attend_own(place, ids, own)
-    acc, rim = lax.optimization_barrier((acc, rim))
-    attended = attend_earlier((2, 1, 3), place, ids, own, cross, acc, stat)
-    back = [lax.ppermute(part, "ctx", z_pairs(by)) for part, by in zip(attended, (2, 1, 3))]
-    (kept,) = attend_earlier((0,), place, ids, own, cross, acc, stat)
+    away, here = attend_own(place, ids, own)
+    attended = attend_earlier(AWAY, place, ids, cross, away)
+    back = [lax.ppermute(part, "ctx", z_pairs(by)) for part, by in zip(attended, AWAY)]
+    (kept,) = attend_earlier(HERE, place, ids, cross, here)
+    kept, rim = lax.optimization_barrier((kept, rim))
     mine = jnp.concatenate([kept, back[1], back[0], back[2]], axis=0)
     sib = lax.ppermute(mine, "head", flip_pairs(1))
 

time: 117 us -> 114 us (0.974); the launches traced: 117 us -> 113 us
  waiting for transfers between devices: 46.1 us -> 41.6 us
  starting transfers between devices: 30.6 us -> 34.3 us
  Pallas kernels: 36.9 us -> 34 us
    ppermute x3, starting transfers between devices: 3.3 us -> 6.95 us  [on_device(): lax.ppermute(part, 'ctx', z_pairs(by))]
    ppermute x1, waiting for transfers between devices: 3.45 us -> 0.01 us  [on_device(): rim = lax.ppermute(edge, 'ctx', [(i, i + 1) for i in range(7)])]
    ppermute x3, waiting for transfers between devices: 3.83 us -> 0.99 us  [on_device(): a_got = [lax.ppermute(a_terms[d], 'head', y_pairs(d)) for d in (2, 1, 3)]]
    ppermute x3, waiting for transfers between devices: 3.5 us -> 1.03 us  [on_device(): lax.ppermute(part, 'ctx', z_pairs(by))]
    ppermute x1, waiting for transfers between devices: 0.01 us -> 2.12 us  [on_device(): cross.insert(2, lax.ppermute(forwarded, 'ctx', cross_pairs(0)))]
    pallas_call x1, Pallas kernels: 7.11 us -> 5 us  [attend_own(): pl.pallas_call(attend_own_kernel, grid_spec=pltpu.PrefetchScalarGridSpec(...]
    ppermute x1, waiting for transfers between devices: 3.46 us -> 4.84 us  [on_device(): b_got = lax.ppermute(b_send, 'head', flip_pairs(2))]
  transfers between devices with their start and end apart: 19 -> 19, of which waited for: 11 -> 10; matrix products, arithmetic and copies ran while one was open for 1% -> 1% of each run, Pallas kernels for 20% -> 22%
where the time goes in v3:
time: 114 us; the launch traced here: 113 us
  waiting for transfers between devices  41.6 us (36%)
  starting transfers between devices  34.3 us (30%)
  Pallas kernels  34 us (30%)
  other arithmetic  1.55 us (1%)
    all_to_all x1, waiting for transfers between devices, on_device(): lax.all_to_all(packed, 'ctx', 0, 0, axis_index_groups=[[0, 1, 2, 3], [4,...  22.8 us
    pallas_call x1, Pallas kernels, hyena(): pl.pallas_call(hyena_kernel, in_specs=vmem_specs(5), out_specs=pl.BlockSp...  11.5 us
    pallas_call x1, Pallas kernels, project(): pl.pallas_call(project_kernel, grid_spec=pltpu.PrefetchScalarGridSpec(num...  8.71 us
    ppermute x3, waiting for transfers between devices, on_device(): b_terms = [lax.ppermute(b_parts[d], 'head', y_pairs(d)) for d in (1, 2, 3)]  7.89 us
    ppermute x3, starting transfers between devices, on_device(): lax.ppermute(part, 'ctx', z_pairs(by))  6.95 us
    ppermute x3, starting transfers between devices, on_device(): a_got = [lax.ppermute(a_terms[d], 'head', y_pairs(d)) for d in (2, 1, 3)]  6.44 us
    all_to_all x1, starting transfers between devices, on_device(): lax.all_to_all(packed, 'ctx', 0, 0, axis_index_groups=[[0, 1, 2, 3], [4,...  5.45 us
    pallas_call x2, Pallas kernels, attend_earlier(): pl.pallas_call(functools.partial(attend_earlier_kernel, order), grid_spec...  5.3 us
  transfers between devices with their start and end apart: 19, of which 10 were waited for; matrix products, arithmetic and copies ran while one was open for 1% of the time, Pallas kernels for 22%

profile of v3, /device:TPU:4, one launch (start us, length us, event | category | flops | bytes accessed | tf_op | source)
XLA Modules:
  0.0 112.8 jit_solution(7605785263291320321)
XLA Ops:
  0.7 3.2 %pack.1 = (bf16[4,512,384]{2,1,0:T(8,128)(2,1)}, bf16[512,256]{1,0:T(8,128)(2,1)}, bf16[512,256]{1,0:T(8,128)(2,1)}, bf16[512,256]{1,0:T(8,128)(2,1)}) custom-call(bf16[512,512]{1,0:T(8,128)(2,1)} %q_ref.1, bf16[512,512]{1,0:T(8,128)(2,1)} %k_ref.2, bf16[512,512]{1,0:T(8,128)(2,1)} %v_ref.2), custom_call_target="tpu_custom_call" | custom-call | bytes 4194304 | tf_op jit(solution)/shard_map/pack/pallas_call | solution.py:59
  3.9 5.5 %all-to-all-start = ((bf16[4,512,384]{2,1,0:T(8,128)(2,1)}), bf16[4,512,384]{2,1,0:T(8,128)(2,1)S(1)}, u32[]{:S(2)}, u32[]{:S(2)}) async-start(bf16[4,512,384]{2,1,0:T(8,128)(2,1)} %get-tuple-element.35), calls=%async_computation | async-start | bytes 3145728 | tf_op jit(solution)/shard_map/all_to_all | solution.py:348
  9.4 1.3 %collective-permute-start = (bf16[512,256]{1,0:T(8,128)(2,1)S(1)}, bf16[512,256]{1,0:T(8,128)(2,1)S(1)}, u32[]{:S(2)}, u32[]{:S(2)}) collective-permute-start(bf16[512,256]{1,0:T(8,128)(2,1)S(1)} %copy-done.9), channel_id=1, source_target_pairs={{0,64},{16,80},{32,96},{48,112},{1,65},{17,81},{33,97},{49,113},{2... | collective-permute-start | bytes 786440 | tf_op jit(solution)/shard_map/ppermute | solution.py:347
  10.7 1.3 %collective-permute-start.1 = (bf16[512,256]{1,0:T(8,128)(2,1)S(1)}, bf16[512,256]{1,0:T(8,128)(2,1)S(1)}, u32[]{:S(2)}, u32[]{:S(2)}) collective-permute-start(bf16[512,256]{1,0:T(8,128)(2,1)S(1)} %copy-done.8), channel_id=1, source_target_pairs={{0,80},{16,96},{32,112},{48,64},{1,81},{17,97},{33,113},{49,65},{2... | collective-permute-start | bytes 786440 | tf_op jit(solution)/shard_map/ppermute | solution.py:347
  12.0 1.3 %collective-permute-start.3 = (bf16[512,256]{1,0:T(8,128)(2,1)S(1)}, bf16[512,256]{1,0:T(8,128)(2,1)S(1)}, u32[]{:S(2)}, u32[]{:S(2)}) collective-permute-start(bf16[512,256]{1,0:T(8,128)(2,1)S(1)} %copy-done.7), channel_id=1, source_target_pairs={{0,112},{16,64},{32,80},{48,96},{1,113},{17,65},{33,81},{49,97},{2... | collective-permute-start | bytes 786440 | tf_op jit(solution)/shard_map/ppermute | solution.py:347
  13.5 22.8 %all-to-all-done.qkv_ref = bf16[4,512,384]{2,1,0:T(8,128)(2,1)S(1)} async-done(((bf16[4,512,384]{2,1,0:T(8,128)(2,1)}), bf16[4,512,384]{2,1,0:T(8,128)(2,1)S(1)}, u32[]{:S(2)}, u32[]{:S(2)}) %all-to-all-start) | async-done | bytes 1572896 | tf_op jit(solution)/shard_map/all_to_all | solution.py:348
  36.5 1.3 %collective-permute-start.2 = (bf16[512,256]{1,0:T(8,128)(2,1)S(1)}, bf16[512,256]{1,0:T(8,128)(2,1)S(1)}, u32[]{:S(2)}, u32[]{:S(2)}) collective-permute-start(bf16[512,256]{1,0:T(8,128)(2,1)S(1)} %slice.40), channel_id=1, source_target_pairs={{0,64},{16,80},{32,96},{48,112},{1,65},{17,81},{33,97},{49,113},{2... | collective-permute-start | bytes 786440 | tf_op jit(solution)/shard_map/ppermute | solution.py:350
  37.8 2.5 %collective-permute-start.5 = (bf16[128,512]{1,0:T(8,128)(2,1)S(1)}, bf16[128,512]{1,0:T(8,128)(2,1)S(1)}, u32[]{:S(2)}, u32[]{:S(2)}) collective-permute-start(bf16[128,512]{1,0:T(8,128)(2,1)S(1)} %multiply_convert_fusion), channel_id=1, source_target_pairs={{0,16},{16,32},{32,48},{48,64},{64,80},{80,96},{96,112},{1,17},{17... | collective-permute-start | bytes 393224 | tf_op jit(solution)/shard_map/ppermute | solution.py:355
  40.3 5.0 %attend_own.1 = (bf16[3,512,128]{2,1,0:T(8,128)(2,1)S(1)}, f32[3,128,512]{2,1,0:T(8,128)S(1)}, f32[3,16,512]{2,1,0:T(8,128)S(1)}, bf16[1,512,128]{2,1,0:T(8,128)...) custom-call(s32[5]{0:T(128)S(1)} %stack.23.place, s32[8,512]{1,0:T(8,128)S(1)} %reshape.10.ids_ref, ...), custom_call_target="tpu_custom_call" | custom-call | flops 4000000000 | bytes 4194304 | tf_op jit(solution)/shard_map/attend_own/pallas_call | solution.py:132
  45.3 2.1 %collective-permute-done.2.rest_2_ = bf16[512,256]{1,0:T(8,128)(2,1)S(1)} collective-permute-done((bf16[512,256]{1,0:T(8,128)(2,1)S(1)}, bf16[512,256]{1,0:T(8,128)(2,1)S(1)}, u32[]{:S(2)}, u32[]{:S(2)}) %collective-permute-start.2) | collective-permute-done | bytes 262176 | tf_op jit(solution)/shard_map/ppermute | solution.py:350
  47.5 1.5 %attend_earlier.3 = (bf16[512,128]{1,0:T(8,128)(2,1)S(1)}, bf16[512,128]{1,0:T(8,128)(2,1)S(1)}, bf16[512,128]{1,0:T(8,128)(2,1)S(1)}) custom-call(s32[5]{0:T(128)S(1)} %stack.23.place, s32[8,512]{1,0:T(8,128)S(1)} %reshape.10.ids_ref, bf16[512,256]{1,0:T(8,128)(2,1)S(1)} %collective-permute-done.rest_0_, ...), custom_call_target="tpu_custom_call" | custom-call | flops 3000000 | bytes 4096 | tf_op jit(solution)/shard_map/attend_earlier/pallas_call | solution.py:177
  48.9 3.5 %collective-permute-start.6 = (bf16[512,128]{1,0:T(8,128)(2,1)S(1)}, bf16[512,128]{1,0:T(8,128)(2,1)S(1)}, u32[]{:S(2)}, u32[]{:S(2)}) collective-permute-start(bf16[512,128]{1,0:T(8,128)(2,1)S(1)} %get-tuple-element.46), channel_id=1, source_target_pairs={{0,16},{16,32},{32,48},{48,0},{64,80},{80,96},{96,112},{112,64},{1... | collective-permute-start | bytes 393224 | tf_op jit(solution)/shard_map/ppermute | solution.py:358
  52.4 3.5 %collective-permute-start.7 = (bf16[512,128]{1,0:T(8,128)(2,1)S(1)}, bf16[512,128]{1,0:T(8,128)(2,1)S(1)}, u32[]{:S(2)}, u32[]{:S(2)}) collective-permute-start(bf16[512,128]{1,0:T(8,128)(2,1)S(1)} %get-tuple-element.47), channel_id=1, source_target_pairs={{0,32},{16,48},{32,0},{48,16},{64,96},{80,112},{96,64},{112,80},{1... | collective-permute-start | bytes 393224 | tf_op jit(solution)/shard_map/ppermute | solution.py:358
  55.9 3.8 %attend_earlier.2 = bf16[512,128]{1,0:T(8,128)(2,1)S(1)} custom-call(s32[5]{0:T(128)S(1)} %stack.23.place, s32[8,512]{1,0:T(8,128)S(1)} %reshape.10.ids_ref, bf16[512,256]{1,0:T(8,128)(2,1)S(1)} %collective-permute-done.rest_0_, bf16[512,256]{1,0:T(8,128)(2,1)S(1)} %collective-permute-done.1.rest_1_, bf16[512,256]{1,0:T(8,128)(2,1)S(1)} %collective-permute-done.2.rest_2_, ...), custom_call_target="tpu_custom_call" | custom-call | flops 1000000 | bytes 4096 | tf_op jit(solution)/shard_map/attend_earlier/pallas_call | solution.py:177
  59.8 0.4 collective-permute-done.7
  60.2 0.6 collective-permute-done.8
  61.2 1.9 %collective-permute-done.9.sib_ref = bf16[2048,128]{1,0:T(8,128)(2,1)S(1)} collective-permute-done((bf16[2048,128]{1,0:T(8,128)(2,1)S(1)}, bf16[2048,128]{1,0:T(8,128)(2,1)S(1)}, u32[]{:S(2)}, u32[]{:S(2)}) %collective-permute-start.9) | collective-permute-done | bytes 524320 | tf_op jit(solution)/shard_map/ppermute | solution.py:362
  63.1 8.7 %project.1 = (bf16[2,272,512]{2,1,0:T(8,128)(2,1)S(1)}, bf16[2,272,512]{2,1,0:T(8,128)(2,1)}, bf16[2,272,512]{2,1,0:T(8,128)(2,1)}, bf16[2,272,512]{2,1,0:T(8,12...) custom-call(s32[5]{0:T(128)S(1)} %stack.23.place, ...), custom_call_target="tpu_custom_call" | custom-call | flops 4294967296 | bytes 14680064 | tf_op jit(solution)/shard_map/project/pallas_call | solution.py:241
  71.8 1.3 %collective-permute-start.10 = (bf16[4,240,512]{2,1,0:T(8,128)(2,1)}, bf16[4,240,512]{2,1,0:T(8,128)(2,1)S(1)}, u32[]{:S(2)}, u32[]{:S(2)}) collective-permute-start(bf16[4,240,512]{2,1,0:T(8,128)(2,1)} %get-tuple-element.52), channel_id=1, source_target_pairs={{0,2},{1,3},{2,0},{3,1},{4,6},{5,7},{6,4},{7,5},{8,10},{9,11},{10,... | collective-permute-start | bytes 2949128 | tf_op jit(solution)/shard_map/ppermute | solution.py:366
  73.1 3.2 %collective-permute-start.11 = (bf16[2,272,512]{2,1,0:T(8,128)(2,1)}, bf16[2,272,512]{2,1,0:T(8,128)(2,1)S(1)}, u32[]{:S(2)}, u32[]{:S(2)}) collective-permute-start(bf16[2,272,512]{2,1,0:T(8,128)(2,1)} %get-tuple-element.55), channel_id=1, source_target_pairs={{0,8},{1,9},{2,10},{3,11},{4,12},{5,13},{6,14},{7,15},{8,0},{9,1},... | collective-permute-start | bytes 1671176 | tf_op jit(solution)/shard_map/ppermute | solution.py:367
  76.3 0.7 collective-permute-start.12
  77.0 2.6 %collective-permute-start.13 = (bf16[2,272,512]{2,1,0:T(8,128)(2,1)}, bf16[2,272,512]{2,1,0:T(8,128)(2,1)S(1)}, u32[]{:S(2)}, u32[]{:S(2)}) collective-permute-start(bf16[2,272,512]{2,1,0:T(8,128)(2,1)} %get-tuple-element.57), channel_id=1, source_target_pairs={{0,12},{1,13},{2,14},{3,15},{4,0},{5,1},{6,2},{7,3},{8,4},{9,5},{1... | collective-permute-start | bytes 1671176 | tf_op jit(solution)/shard_map/ppermute | solution.py:367
  79.5 11.5 %hyena.1 = bf16[512,512]{1,0:T(8,128)(2,1)} custom-call(bf16[512,512]{1,0:T(8,128)(2,1)S(1)} %copy-done.2, bf16[512,512]{1,0:T(8,128)(2,1)S(1)} %copy-done, bf16[512,512]{1,0:T(8,128)(2,1)S(1)} %copy-done.1, bf16[128,512]{1,0:T(8,128)(2,1)S(1)} %collective-permute-done.5.rim_ref, bf16[128,512]{1,0:T(8,128)(2,1)S(1)} %copy-done.3), custom_call_target="tpu_custom_call" | custom-call | flops 10000000 | bytes 3072 | tf_op jit(solution)/shard_map/hyena/pallas_call | solution.py:292
  91.1 4.8 %collective-permute-done.10 = bf16[4,240,512]{2,1,0:T(8,128)(2,1)S(1)} collective-permute-done((bf16[4,240,512]{2,1,0:T(8,128)(2,1)}, bf16[4,240,512]{2,1,0:T(8,128)(2,1)S(1)}, u32[]{:S(2)}, u32[]{:S(2)}) %collective-permute-start.10) | collective-permute-done | bytes 983072 | tf_op jit(solution)/shard_map/ppermute | solution.py:366
  96.4 1.6 %collective-permute-start.15 = (bf16[240,512]{1,0:T(8,128)(2,1)S(1)}, bf16[240,512]{1,0:T(8,128)(2,1)S(1)}, u32[]{:S(2)}, u32[]{:S(2)}) collective-permute-start(bf16[240,512]{1,0:T(8,128)(2,1)S(1)} %get-tuple-element.66), channel_id=1, source_target_pairs={{0,4},{1,5},{2,6},{3,7},{4,8},{5,9},{6,10},{7,11},{8,12},{9,13},{1... | collective-permute-start | bytes 737288 | tf_op jit(solution)/shard_map/ppermute | solution.py:375
  98.0 1.7 %collective-permute-start.17 = (bf16[240,512]{1,0:T(8,128)(2,1)S(1)}, bf16[240,512]{1,0:T(8,128)(2,1)S(1)}, u32[]{:S(2)}, u32[]{:S(2)}) collective-permute-start(bf16[240,512]{1,0:T(8,128)(2,1)S(1)} %get-tuple-element.67), channel_id=1, source_target_pairs={{0,12},{1,13},{2,14},{3,15},{4,0},{5,1},{6,2},{7,3},{8,4},{9,5},{1... | collective-permute-start | bytes 737288 | tf_op jit(solution)/shard_map/ppermute | solution.py:375
  99.7 2.0 %collective-permute-start.16 = (bf16[240,512]{1,0:T(8,128)(2,1)S(1)}, bf16[240,512]{1,0:T(8,128)(2,1)S(1)}, u32[]{:S(2)}, u32[]{:S(2)}) collective-permute-start(bf16[240,512]{1,0:T(8,128)(2,1)S(1)} %get-tuple-element.68), channel_id=1, source_target_pairs={{0,8},{1,9},{2,10},{3,11},{4,12},{5,13},{6,14},{7,15},{8,0},{9,1},... | collective-permute-start | bytes 737288 | tf_op jit(solution)/shard_map/ppermute | solution.py:375
  101.6 1.0 collective-permute-done.13.three_ref
  102.9 0.9 collective-permute-start.14
  103.8 3.9 %collective-permute-done.15 = bf16[240,512]{1,0:T(8,128)(2,1)S(1)} collective-permute-done((bf16[240,512]{1,0:T(8,128)(2,1)S(1)}, bf16[240,512]{1,0:T(8,128)(2,1)S(1)}, u32[]{:S(2)}, u32[]{:S(2)}) %collective-permute-start.15) | collective-permute-done | bytes 245792 | tf_op jit(solution)/shard_map/ppermute | solution.py:375
  107.9 3.8 %collective-permute-done.16 = bf16[240,512]{1,0:T(8,128)(2,1)S(1)} collective-permute-done((bf16[240,512]{1,0:T(8,128)(2,1)S(1)}, bf16[240,512]{1,0:T(8,128)(2,1)S(1)}, u32[]{:S(2)}, u32[]{:S(2)}) %collective-permute-start.16) | collective-permute-done | bytes 245792 | tf_op jit(solution)/shard_map/ppermute | solution.py:375
  112.0 0.8 pad_maximum_fusion
  (51 shorter events, 1.9 us)
Async XLA Ops:
  0.6 37.1 %collective-permute-start.4 = (bf16[512,8192]{1,0:T(8,128)(2,1)}, bf16[512,8192]{1,0:T(8,128)(2,1)}, u32[]{:S(2)}, u32[]{:S(2)}) collective-permute-start(bf16[512,8192]{1,0:T(8,128)(2,1)} %w_own.1), channel_id=1, source_target_pairs={{0,1},{1,0},{2,3},{3,2},{4,5},{5,4},{6,7},{7,6},{8,9},{9,8},{10,11... | collective-permute-start | bytes 25165832 | tf_op jit(solution)/shard_map/ppermute | solution.py:345
  3.9 5.5 %copy-start.9 = (bf16[512,256]{1,0:T(8,128)(2,1)S(1)}, bf16[512,256]{1,0:T(8,128)(2,1)}, u32[]{:S(2)}) copy-start(bf16[512,256]{1,0:T(8,128)(2,1)} %get-tuple-element.33) | copy-start | bytes 786436
  3.9 6.8 %copy-start.8 = (bf16[512,256]{1,0:T(8,128)(2,1)S(1)}, bf16[512,256]{1,0:T(8,128)(2,1)}, u32[]{:S(2)}) copy-start(bf16[512,256]{1,0:T(8,128)(2,1)} %get-tuple-element.34) | copy-start | bytes 786436
  3.9 8.1 %copy-start.7 = (bf16[512,256]{1,0:T(8,128)(2,1)S(1)}, bf16[512,256]{1,0:T(8,128)(2,1)}, u32[]{:S(2)}) copy-start(bf16[512,256]{1,0:T(8,128)(2,1)} %get-tuple-element.36) | copy-start | bytes 786436
  3.9 9.5 %copy-start.6 = (s32[4096]{0:T(1024)S(1)}, s32[4096]{0:T(1024)}, u32[]{:S(2)}) copy-start(s32[4096]{0:T(1024)} %param.16) | copy-start | bytes 49156
  3.9 33.8 %slice-start = ((bf16[512,512]{1,0:T(8,128)(2,1)}), bf16[128,512]{1,0:T(8,128)(2,1)S(1)}, s32[]{:S(2)}) async-start(bf16[512,512]{1,0:T(8,128)(2,1)} %k_ref.3), calls=%async_computation.1 | async-start | bytes 262144 | tf_op jit(solution)/shard_map/slice | solution.py:353
  3.9 33.8 %slice-start.1 = ((bf16[512,512]{1,0:T(8,128)(2,1)}), bf16[128,512]{1,0:T(8,128)(2,1)S(1)}, s32[]{:S(2)}) async-start(bf16[512,512]{1,0:T(8,128)(2,1)} %v_ref.3), calls=%async_computation.2 | async-start | bytes 262144 | tf_op jit(solution)/shard_map/slice | solution.py:353
  3.9 32.4 %all-to-all-start = ((bf16[4,512,384]{2,1,0:T(8,128)(2,1)}), bf16[4,512,384]{2,1,0:T(8,128)(2,1)S(1)}, u32[]{:S(2)}, u32[]{:S(2)}) async-start(bf16[4,512,384]{2,1,0:T(8,128)(2,1)} %get-tuple-element.35), calls=%async_computation | async-start | bytes 3145728 | tf_op jit(solution)/shard_map/all_to_all | solution.py:348
  9.4 35.9 %collective-permute-start = (bf16[512,256]{1,0:T(8,128)(2,1)S(1)}, bf16[512,256]{1,0:T(8,128)(2,1)S(1)}, u32[]{:S(2)}, u32[]{:S(2)}) collective-permute-start(bf16[512,256]{1,0:T(8,128)(2,1)S(1)} %copy-done.9), channel_id=1, source_target_pairs={{0,64},{16,80},{32,96},{48,112},{1,65},{17,81},{33,97},{49,113},{2... | collective-permute-start | bytes 786440 | tf_op jit(solution)/shard_map/ppermute | solution.py:347
  10.7 34.6 %collective-permute-start.1 = (bf16[512,256]{1,0:T(8,128)(2,1)S(1)}, bf16[512,256]{1,0:T(8,128)(2,1)S(1)}, u32[]{:S(2)}, u32[]{:S(2)}) collective-permute-start(bf16[512,256]{1,0:T(8,128)(2,1)S(1)} %copy-done.8), channel_id=1, source_target_pairs={{0,80},{16,96},{32,112},{48,64},{1,81},{17,97},{33,113},{49,65},{2... | collective-permute-start | bytes 786440 | tf_op jit(solution)/shard_map/ppermute | solution.py:347
  12.0 33.3 %collective-permute-start.3 = (bf16[512,256]{1,0:T(8,128)(2,1)S(1)}, bf16[512,256]{1,0:T(8,128)(2,1)S(1)}, u32[]{:S(2)}, u32[]{:S(2)}) collective-permute-start(bf16[512,256]{1,0:T(8,128)(2,1)S(1)} %copy-done.7), channel_id=1, source_target_pairs={{0,112},{16,64},{32,80},{48,96},{1,113},{17,65},{33,81},{49,97},{2... | collective-permute-start | bytes 786440 | tf_op jit(solution)/shard_map/ppermute | solution.py:347
  36.5 11.0 %collective-permute-start.2 = (bf16[512,256]{1,0:T(8,128)(2,1)S(1)}, bf16[512,256]{1,0:T(8,128)(2,1)S(1)}, u32[]{:S(2)}, u32[]{:S(2)}) collective-permute-start(bf16[512,256]{1,0:T(8,128)(2,1)S(1)} %slice.40), channel_id=1, source_target_pairs={{0,64},{16,80},{32,96},{48,112},{1,65},{17,81},{33,97},{49,113},{2... | collective-permute-start | bytes 786440 | tf_op jit(solution)/shard_map/ppermute | solution.py:350
  37.8 21.9 %collective-permute-start.5 = (bf16[128,512]{1,0:T(8,128)(2,1)S(1)}, bf16[128,512]{1,0:T(8,128)(2,1)S(1)}, u32[]{:S(2)}, u32[]{:S(2)}) collective-permute-start(bf16[128,512]{1,0:T(8,128)(2,1)S(1)} %multiply_convert_fusion), channel_id=1, source_target_pairs={{0,16},{16,32},{32,48},{48,64},{64,80},{80,96},{96,112},{1,17},{17... | collective-permute-start | bytes 393224 | tf_op jit(solution)/shard_map/ppermute | solution.py:355
  48.9 10.8 %collective-permute-start.6 = (bf16[512,128]{1,0:T(8,128)(2,1)S(1)}, bf16[512,128]{1,0:T(8,128)(2,1)S(1)}, u32[]{:S(2)}, u32[]{:S(2)}) collective-permute-start(bf16[512,128]{1,0:T(8,128)(2,1)S(1)} %get-tuple-element.46), channel_id=1, source_target_pairs={{0,16},{16,32},{32,48},{48,0},{64,80},{80,96},{96,112},{112,64},{1... | collective-permute-start | bytes 393224 | tf_op jit(solution)/shard_map/ppermute | solution.py:358
  52.4 7.8 %collective-permute-start.7 = (bf16[512,128]{1,0:T(8,128)(2,1)S(1)}, bf16[512,128]{1,0:T(8,128)(2,1)S(1)}, u32[]{:S(2)}, u32[]{:S(2)}) collective-permute-start(bf16[512,128]{1,0:T(8,128)(2,1)S(1)} %get-tuple-element.47), channel_id=1, source_target_pairs={{0,32},{16,48},{32,0},{48,16},{64,96},{80,112},{96,64},{112,80},{1... | collective-permute-start | bytes 393224 | tf_op jit(solution)/shard_map/ppermute | solution.py:358
  55.9 5.0 %collective-permute-start.8 = (bf16[512,128]{1,0:T(8,128)(2,1)S(1)}, bf16[512,128]{1,0:T(8,128)(2,1)S(1)}, u32[]{:S(2)}, u32[]{:S(2)}) collective-permute-start(bf16[512,128]{1,0:T(8,128)(2,1)S(1)} %get-tuple-element.48), channel_id=1, source_target_pairs={{0,48},{16,0},{32,16},{48,32},{64,112},{80,64},{96,80},{112,96},{1... | collective-permute-start | bytes 393224 | tf_op jit(solution)/shard_map/ppermute | solution.py:358
  60.9 18.7 %copy-start = (bf16[512,512]{1,0:T(8,128)(2,1)S(1)}, bf16[512,512]{1,0:T(8,128)(2,1)}, u32[]{:S(2)}) copy-start(bf16[512,512]{1,0:T(8,128)(2,1)} %k_ref.3) | copy-start | bytes 1572868
  60.9 18.7 %copy-start.1 = (bf16[512,512]{1,0:T(8,128)(2,1)S(1)}, bf16[512,512]{1,0:T(8,128)(2,1)}, u32[]{:S(2)}) copy-start(bf16[512,512]{1,0:T(8,128)(2,1)} %v_ref.3) | copy-start | bytes 1572868
  60.9 18.6 %copy-start.2 = (bf16[512,512]{1,0:T(8,128)(2,1)S(1)}, bf16[512,512]{1,0:T(8,128)(2,1)}, u32[]{:S(2)}) copy-start(bf16[512,512]{1,0:T(8,128)(2,1)} %q_ref.2) | copy-start | bytes 1572868
  60.9 18.6 %copy-start.3 = (bf16[128,512]{1,0:T(8,128)(2,1)S(1)}, bf16[128,512]{1,0:T(8,128)(2,1)}, u32[]{:S(2)}) copy-start(bf16[128,512]{1,0:T(8,128)(2,1)} %f_ref.1) | copy-start | bytes 393220
  60.9 2.2 %collective-permute-start.9 = (bf16[2048,128]{1,0:T(8,128)(2,1)S(1)}, bf16[2048,128]{1,0:T(8,128)(2,1)S(1)}, u32[]{:S(2)}, u32[]{:S(2)}) collective-permute-start(bf16[2048,128]{1,0:T(8,128)(2,1)S(1)} %constant_dynamic-update-slice_fusion.own_ref), channel_id=1, source_target_pairs={{0,1},{1,0},{2,3},{3,2},{4,5},{5,4},{6,7},{7,6},{8,9},{9,8},{10,11... | collective-permute-start | bytes 1572872 | tf_op jit(solution)/shard_map/ppermute | solution.py:362
  71.8 24.1 %copy-start.5 = (bf16[4,240,512]{2,1,0:T(8,128)(2,1)S(1)}, bf16[4,240,512]{2,1,0:T(8,128)(2,1)}, u32[]{:S(2)}) copy-start(bf16[4,240,512]{2,1,0:T(8,128)(2,1)} %get-tuple-element.49) | copy-start | bytes 2949124
  71.8 24.1 %collective-permute-start.10 = (bf16[4,240,512]{2,1,0:T(8,128)(2,1)}, bf16[4,240,512]{2,1,0:T(8,128)(2,1)S(1)}, u32[]{:S(2)}, u32[]{:S(2)}) collective-permute-start(bf16[4,240,512]{2,1,0:T(8,128)(2,1)} %get-tuple-element.52), channel_id=1, source_target_pairs={{0,2},{1,3},{2,0},{3,1},{4,6},{5,7},{6,4},{7,5},{8,10},{9,11},{10,... | collective-permute-start | bytes 2949128 | tf_op jit(solution)/shard_map/ppermute | solution.py:366
  73.1 26.6 %collective-permute-start.11 = (bf16[2,272,512]{2,1,0:T(8,128)(2,1)}, bf16[2,272,512]{2,1,0:T(8,128)(2,1)S(1)}, u32[]{:S(2)}, u32[]{:S(2)}) collective-permute-start(bf16[2,272,512]{2,1,0:T(8,128)(2,1)} %get-tuple-element.55), channel_id=1, source_target_pairs={{0,8},{1,9},{2,10},{3,11},{4,12},{5,13},{6,14},{7,15},{8,0},{9,1},... | collective-permute-start | bytes 1671176 | tf_op jit(solution)/shard_map/ppermute | solution.py:367
  76.3 25.4 %collective-permute-start.12 = (bf16[2,272,512]{2,1,0:T(8,128)(2,1)}, bf16[2,272,512]{2,1,0:T(8,128)(2,1)S(1)}, u32[]{:S(2)}, u32[]{:S(2)}) collective-permute-start(bf16[2,272,512]{2,1,0:T(8,128)(2,1)} %get-tuple-element.56), channel_id=1, source_target_pairs={{0,4},{1,5},{2,6},{3,7},{4,8},{5,9},{6,10},{7,11},{8,12},{9,13},{1... | collective-permute-start | bytes 1671176 | tf_op jit(solution)/shard_map/ppermute | solution.py:367
  77.0 25.7 %collective-permute-start.13 = (bf16[2,272,512]{2,1,0:T(8,128)(2,1)}, bf16[2,272,512]{2,1,0:T(8,128)(2,1)S(1)}, u32[]{:S(2)}, u32[]{:S(2)}) collective-permute-start(bf16[2,272,512]{2,1,0:T(8,128)(2,1)} %get-tuple-element.57), channel_id=1, source_target_pairs={{0,12},{1,13},{2,14},{3,15},{4,0},{5,1},{6,2},{7,3},{8,4},{9,5},{1... | collective-permute-start | bytes 1671176 | tf_op jit(solution)/shard_map/ppermute | solution.py:367
  96.4 11.3 %collective-permute-start.15 = (bf16[240,512]{1,0:T(8,128)(2,1)S(1)}, bf16[240,512]{1,0:T(8,128)(2,1)S(1)}, u32[]{:S(2)}, u32[]{:S(2)}) collective-permute-start(bf16[240,512]{1,0:T(8,128)(2,1)S(1)} %get-tuple-element.66), channel_id=1, source_target_pairs={{0,4},{1,5},{2,6},{3,7},{4,8},{5,9},{6,10},{7,11},{8,12},{9,13},{1... | collective-permute-start | bytes 737288 | tf_op jit(solution)/shard_map/ppermute | solution.py:375
  98.0 9.9 %collective-permute-start.17 = (bf16[240,512]{1,0:T(8,128)(2,1)S(1)}, bf16[240,512]{1,0:T(8,128)(2,1)S(1)}, u32[]{:S(2)}, u32[]{:S(2)}) collective-permute-start(bf16[240,512]{1,0:T(8,128)(2,1)S(1)} %get-tuple-element.67), channel_id=1, source_target_pairs={{0,12},{1,13},{2,14},{3,15},{4,0},{5,1},{6,2},{7,3},{8,4},{9,5},{1... | collective-permute-start | bytes 737288 | tf_op jit(solution)/shard_map/ppermute | solution.py:375
  99.7 12.0 %collective-permute-start.16 = (bf16[240,512]{1,0:T(8,128)(2,1)S(1)}, bf16[240,512]{1,0:T(8,128)(2,1)S(1)}, u32[]{:S(2)}, u32[]{:S(2)}) collective-permute-start(bf16[240,512]{1,0:T(8,128)(2,1)S(1)} %get-tuple-element.68), channel_id=1, source_target_pairs={{0,8},{1,9},{2,10},{3,11},{4,12},{5,13},{6,14},{7,15},{8,0},{9,1},... | collective-permute-start | bytes 737288 | tf_op jit(solution)/shard_map/ppermute | solution.py:375
  102.6 9.1 %copy-start.4 = (bf16[512,512]{1,0:T(8,128)(2,1)S(1)}, bf16[512,512]{1,0:T(8,128)(2,1)}, u32[]{:S(2)}) copy-start(bf16[512,512]{1,0:T(8,128)(2,1)} %hyena.1) | copy-start | bytes 1572868
  102.9 9.0 %collective-permute-start.14 = (bf16[272,512]{1,0:T(8,128)(2,1)S(1)}, bf16[272,512]{1,0:T(8,128)(2,1)S(1)}, u32[]{:S(2)}, u32[]{:S(2)}) collective-permute-start(bf16[272,512]{1,0:T(8,128)(2,1)S(1)} %get-tuple-element.63), channel_id=1, source_target_pairs={{0,2},{1,3},{2,0},{3,1},{4,6},{5,7},{6,4},{7,5},{8,10},{9,11},{10,... | collective-permute-start | bytes 835592 | tf_op jit(solution)/shard_map/ppermute | solution.py:378

commit v4 on v3

--- a/solution.py
+++ b/solution.py
@@ -41,15 +41,12 @@
     return [pl.BlockSpec(memory_space=pltpu.VMEM)] * count
 
 
-DIRECT = (0, 1, 3)
-
-
 def pack_kernel(q_ref, k_ref, v_ref, all_ref, *outs):
     for to in range(4):
         for i, ref in enumerate((q_ref, k_ref, v_ref)):
             all_ref[to, :, i * 128 : i * 128 + 128] = ref[:, to * 128 : to * 128 + 128]
     z = lax.rem(lax.axis_index("ctx"), 4)
-    for out, by in zip(outs, DIRECT):
+    for out, by in zip(outs, (2, 0, 1, 3)):
         cols = pl.ds(pl.multiple_of(lax.rem(z + by, 4) * 128, 128), 128)
         out[:, 0:128] = k_ref[:, cols]
         out[:, 128:256] = v_ref[:, cols]
@@ -59,8 +56,8 @@
     return pl.pallas_call(
         pack_kernel,
         in_specs=vmem_specs(3),
-        out_specs=vmem_specs(4),
-        out_shape=[jax.ShapeDtypeStruct((4, ROWS, 384), BF16)] + [jax.ShapeDtypeStruct((ROWS, 256), BF16)] * 3,
+        out_specs=vmem_specs(5),
+        out_shape=[jax.ShapeDtypeStruct((4, ROWS, 384), BF16)] + [jax.ShapeDtypeStruct((ROWS, 256), BF16)] * 4,
         name="pack",
         compiler_params=pltpu.CompilerParams(vmem_limit_bytes=60 * MIB),
         cost_estimate=pl.CostEstimate(flops=0, bytes_accessed=4 * MIB, transcendentals=0),
@@ -170,7 +167,7 @@
             return carry
 
         lax.fori_loop(0, place[1] * jnp.maximum(4 - jnp.min(bound) // BK, 0), body, 0)
-        outs[i][...] = jnp.transpose(acc_s[...] / stat_s[8:9, :]).astype(BF16)
+        outs[i][...] = jnp.transpose(acc_s[...] * (1.0 / stat_s[8:9, :])).astype(BF16)
 
 
 def attend_earlier(order, place, ids, cross, state):
@@ -343,11 +340,11 @@
     place = jnp.stack([z, x_hi, head // 4, (head // 2) % 2, core]).astype(jnp.int32)
 
     w_sib = lax.ppermute(out_weight, "head", flip_pairs(1))
-    packed, *to_cross = pack(attn_query, attn_key, attn_value)
-    cross = [lax.ppermute(part, "ctx", cross_pairs(by)) for part, by in zip(to_cross, DIRECT)]
+    packed, far, *near = pack(attn_query, attn_key, attn_value)
+    far = lax.ppermute(far, "ctx", [(i, (i + 2) % 4) for i in range(4)])
+    cross = [lax.ppermute(part, "ctx", cross_pairs(by)) for part, by in zip(near, (0, 1, 3))]
     own = lax.all_to_all(packed, "ctx", 0, 0, axis_index_groups=[[0, 1, 2, 3], [4, 5, 6, 7]])
-    forwarded = lax.dynamic_index_in_dim(own, (z + 2) % 4, 0, keepdims=False)[:, 128:]
-    cross.insert(2, lax.ppermute(forwarded, "ctx", cross_pairs(0)))
+    cross.insert(2, lax.ppermute(far, "ctx", cross_pairs(0)))
 
     ids = segment_ids.reshape(8, ROWS)
     late_key, late_value, _ = lax.optimization_barrier((hyena_key[384:], hyena_value[384:], w_sib))

time: 114 us -> 111 us (0.974)
  waiting for transfers between devices: 41.6 us -> 36.4 us
  starting transfers between devices: 34.3 us -> 37.3 us
    all_to_all x1, waiting for transfers between devices: 22.8 us -> 16.9 us  [on_device(): lax.all_to_all(packed, 'ctx', 0, 0, axis_index_groups=[[0, 1, 2, 3], [4,...]
    ppermute x1, starting transfers between devices: 2.47 us -> 3.93 us  [on_device(): rim = lax.ppermute(edge, 'ctx', [(i, i + 1) for i in range(7)])]
    ppermute x1 -> x2, starting transfers between devices: 1.29 us -> 2.64 us  [the longest x1 1.36 us: on_device(): far = lax.ppermute(far, 'ctx', [(i, (i + 2) % 4) for i in range(4)])]
  transfers between devices with their start and end apart: 19 -> 20, of which waited for: 10 -> 11; matrix products, arithmetic and copies ran while one was open for 1% -> 1% of each run, Pallas kernels for 22% -> 23%
where the time goes in v4:
time: 111 us
  starting transfers between devices  37.3 us (34%)
  waiting for transfers between devices  36.4 us (33%)
  Pallas kernels  34.1 us (31%)
  other arithmetic  1.55 us (1%)
    all_to_all x1, waiting for transfers between devices, on_device(): lax.all_to_all(packed, 'ctx', 0, 0, axis_index_groups=[[0, 1, 2, 3], [4,...  16.9 us
    pallas_call x1, Pallas kernels, hyena(): pl.pallas_call(hyena_kernel, in_specs=vmem_specs(5), out_specs=pl.BlockSp...  11.5 us
    pallas_call x1, Pallas kernels, project(): pl.pallas_call(project_kernel, grid_spec=pltpu.PrefetchScalarGridSpec(num...  8.72 us
    ppermute x3, waiting for transfers between devices, on_device(): b_terms = [lax.ppermute(b_parts[d], 'head', y_pairs(d)) for d in (1, 2, 3)]  8.47 us
    ppermute x3, starting transfers between devices, on_device(): lax.ppermute(part, 'ctx', z_pairs(by))  6.86 us
    ppermute x3, starting transfers between devices, on_device(): a_got = [lax.ppermute(a_terms[d], 'head', y_pairs(d)) for d in (2, 1, 3)]  6.45 us
    all_to_all x1, starting transfers between devices, on_device(): lax.all_to_all(packed, 'ctx', 0, 0, axis_index_groups=[[0, 1, 2, 3], [4,...  5.45 us
    ppermute x3, starting transfers between devices, on_device(): b_terms = [lax.ppermute(b_parts[d], 'head', y_pairs(d)) for d in (1, 2, 3)]  5.31 us
  transfers between devices with their start and end apart: 20, of which 11 were waited for; matrix products, arithmetic and copies ran while one was open for 1% of the time, Pallas kernels for 23%

profile of v4, /device:TPU:4, one launch (start us, length us, event | category | flops | bytes accessed | tf_op | source)
XLA Modules:
  0.0 110.6 jit_solution(4757221084457988603)
XLA Ops:
  0.7 3.3 %pack.1 = (bf16[4,512,384]{2,1,0:T(8,128)(2,1)}, bf16[512,256]{1,0:T(8,128)(2,1)}, bf16[512,256]{1,0:T(8,128)(2,1)}, bf16[512,256]{1,0:T(8,128)(2,1)}, bf16[512,256]{1,0:T(8,128)(2,1)}) custom-call(bf16[512,512]{1,0:T(8,128)(2,1)} %q_ref.1, bf16[512,512]{1,0:T(8,128)(2,1)} %k_ref.2, bf16[512,512]{1,0:T(8,128)(2,1)} %v_ref.2), custom_call_target="tpu_custom_call" | custom-call | bytes 4194304 | tf_op jit(solution)/shard_map/pack/pallas_call | solution.py:56
  4.0 5.5 %all-to-all-start = ((bf16[4,512,384]{2,1,0:T(8,128)(2,1)}), bf16[4,512,384]{2,1,0:T(8,128)(2,1)S(1)}, u32[]{:S(2)}, u32[]{:S(2)}) async-start(bf16[4,512,384]{2,1,0:T(8,128)(2,1)} %get-tuple-element.38), calls=%async_computation | async-start | bytes 3145728 | tf_op jit(solution)/shard_map/all_to_all | solution.py:346
  9.5 1.4 %collective-permute-start.2 = (bf16[512,256]{1,0:T(8,128)(2,1)}, bf16[512,256]{1,0:T(8,128)(2,1)}, u32[]{:S(2)}, u32[]{:S(2)}) collective-permute-start(bf16[512,256]{1,0:T(8,128)(2,1)} %get-tuple-element.36), channel_id=1, source_target_pairs={{0,32},{16,48},{32,0},{48,16},{1,33},{17,49},{33,1},{49,17},{2,34}... | collective-permute-start | bytes 786440 | tf_op jit(solution)/shard_map/ppermute | solution.py:344
  10.9 1.3 %collective-permute-start = (bf16[512,256]{1,0:T(8,128)(2,1)}, bf16[512,256]{1,0:T(8,128)(2,1)S(1)}, u32[]{:S(2)}, u32[]{:S(2)}) collective-permute-start(bf16[512,256]{1,0:T(8,128)(2,1)} %get-tuple-element.34), channel_id=1, source_target_pairs={{0,64},{16,80},{32,96},{48,112},{1,65},{17,81},{33,97},{49,113},{2... | collective-permute-start | bytes 786440 | tf_op jit(solution)/shard_map/ppermute | solution.py:345
  12.1 1.3 %collective-permute-start.1 = (bf16[512,256]{1,0:T(8,128)(2,1)}, bf16[512,256]{1,0:T(8,128)(2,1)S(1)}, u32[]{:S(2)}, u32[]{:S(2)}) collective-permute-start(bf16[512,256]{1,0:T(8,128)(2,1)} %get-tuple-element.35), channel_id=1, source_target_pairs={{0,80},{16,96},{32,112},{48,64},{1,81},{17,97},{33,113},{49,65},{2... | collective-permute-start | bytes 786440 | tf_op jit(solution)/shard_map/ppermute | solution.py:345
  13.5 1.3 %collective-permute-start.4 = (bf16[512,256]{1,0:T(8,128)(2,1)S(1)}, bf16[512,256]{1,0:T(8,128)(2,1)S(1)}, u32[]{:S(2)}, u32[]{:S(2)}) collective-permute-start(bf16[512,256]{1,0:T(8,128)(2,1)S(1)} %copy-done.7), channel_id=1, source_target_pairs={{0,112},{16,64},{32,80},{48,96},{1,113},{17,65},{33,81},{49,97},{2... | collective-permute-start | bytes 786440 | tf_op jit(solution)/shard_map/ppermute | solution.py:345
  15.0 1.3 %collective-permute-start.3 = (bf16[512,256]{1,0:T(8,128)(2,1)}, bf16[512,256]{1,0:T(8,128)(2,1)S(1)}, u32[]{:S(2)}, u32[]{:S(2)}) collective-permute-start(bf16[512,256]{1,0:T(8,128)(2,1)} %collective-permute-done.2), channel_id=1, source_target_pairs={{0,64},{16,80},{32,96},{48,112},{1,65},{17,81},{33,97},{49,113},{2... | collective-permute-start | bytes 786440 | tf_op jit(solution)/shard_map/ppermute | solution.py:347
  16.3 3.9 %collective-permute-start.6 = (bf16[128,512]{1,0:T(8,128)(2,1)S(1)}, bf16[128,512]{1,0:T(8,128)(2,1)S(1)}, u32[]{:S(2)}, u32[]{:S(2)}) collective-permute-start(bf16[128,512]{1,0:T(8,128)(2,1)S(1)} %multiply_convert_fusion), channel_id=1, source_target_pairs={{0,16},{16,32},{32,48},{48,64},{64,80},{80,96},{96,112},{1,17},{17... | collective-permute-start | bytes 393224 | tf_op jit(solution)/shard_map/ppermute | solution.py:352
  20.3 16.9 %all-to-all-done.qkv_ref = bf16[4,512,384]{2,1,0:T(8,128)(2,1)S(1)} async-done(((bf16[4,512,384]{2,1,0:T(8,128)(2,1)}), bf16[4,512,384]{2,1,0:T(8,128)(2,1)S(1)}, u32[]{:S(2)}, u32[]{:S(2)}) %all-to-all-start) | async-done | bytes 1572896 | tf_op jit(solution)/shard_map/all_to_all | solution.py:346
  37.2 5.0 %attend_own.1 = (bf16[3,512,128]{2,1,0:T(8,128)(2,1)S(1)}, f32[3,128,512]{2,1,0:T(8,128)S(1)}, f32[3,16,512]{2,1,0:T(8,128)S(1)}, bf16[1,512,128]{2,1,0:T(8,128)...) custom-call(s32[5]{0:T(128)S(1)} %stack.23.place, s32[8,512]{1,0:T(8,128)S(1)} %reshape.10.ids_ref, ...), custom_call_target="tpu_custom_call" | custom-call | flops 4000000000 | bytes 4194304 | tf_op jit(solution)/shard_map/attend_own/pallas_call | solution.py:129
  42.2 2.2 %collective-permute-done.3.rest_2_ = bf16[512,256]{1,0:T(8,128)(2,1)S(1)} collective-permute-done((bf16[512,256]{1,0:T(8,128)(2,1)}, bf16[512,256]{1,0:T(8,128)(2,1)S(1)}, u32[]{:S(2)}, u32[]{:S(2)}) %collective-permute-start.3) | collective-permute-done | bytes 262176 | tf_op jit(solution)/shard_map/ppermute | solution.py:347
  44.4 1.5 %attend_earlier.3 = (bf16[512,128]{1,0:T(8,128)(2,1)S(1)}, bf16[512,128]{1,0:T(8,128)(2,1)S(1)}, bf16[512,128]{1,0:T(8,128)(2,1)S(1)}) custom-call(s32[5]{0:T(128)S(1)} %stack.23.place, s32[8,512]{1,0:T(8,128)S(1)} %reshape.10.ids_ref, bf16[512,256]{1,0:T(8,128)(2,1)S(1)} %collective-permute-done.rest_0_, ...), custom_call_target="tpu_custom_call" | custom-call | flops 3000000 | bytes 4096 | tf_op jit(solution)/shard_map/attend_earlier/pallas_call | solution.py:174
  45.9 3.5 %collective-permute-start.7 = (bf16[512,128]{1,0:T(8,128)(2,1)S(1)}, bf16[512,128]{1,0:T(8,128)(2,1)S(1)}, u32[]{:S(2)}, u32[]{:S(2)}) collective-permute-start(bf16[512,128]{1,0:T(8,128)(2,1)S(1)} %get-tuple-element.48), channel_id=1, source_target_pairs={{0,16},{16,32},{32,48},{48,0},{64,80},{80,96},{96,112},{112,64},{1... | collective-permute-start | bytes 393224 | tf_op jit(solution)/shard_map/ppermute | solution.py:355
  49.4 3.4 %collective-permute-start.8 = (bf16[512,128]{1,0:T(8,128)(2,1)S(1)}, bf16[512,128]{1,0:T(8,128)(2,1)S(1)}, u32[]{:S(2)}, u32[]{:S(2)}) collective-permute-start(bf16[512,128]{1,0:T(8,128)(2,1)S(1)} %get-tuple-element.49), channel_id=1, source_target_pairs={{0,32},{16,48},{32,0},{48,16},{64,96},{80,112},{96,64},{112,80},{1... | collective-permute-start | bytes 393224 | tf_op jit(solution)/shard_map/ppermute | solution.py:355
  52.8 3.8 %attend_earlier.2 = bf16[512,128]{1,0:T(8,128)(2,1)S(1)} custom-call(s32[5]{0:T(128)S(1)} %stack.23.place, s32[8,512]{1,0:T(8,128)S(1)} %reshape.10.ids_ref, bf16[512,256]{1,0:T(8,128)(2,1)S(1)} %collective-permute-done.rest_0_, bf16[512,256]{1,0:T(8,128)(2,1)S(1)} %collective-permute-done.1.rest_1_, bf16[512,256]{1,0:T(8,128)(2,1)S(1)} %collective-permute-done.3.rest_2_, ...), custom_call_target="tpu_custom_call" | custom-call | flops 1000000 | bytes 4096 | tf_op jit(solution)/shard_map/attend_earlier/pallas_call | solution.py:174
  57.1 0.6 collective-permute-done.9
  58.1 1.9 %collective-permute-done.10.sib_ref = bf16[2048,128]{1,0:T(8,128)(2,1)S(1)} collective-permute-done((bf16[2048,128]{1,0:T(8,128)(2,1)S(1)}, bf16[2048,128]{1,0:T(8,128)(2,1)S(1)}, u32[]{:S(2)}, u32[]{:S(2)}) %collective-permute-start.10) | collective-permute-done | bytes 524320 | tf_op jit(solution)/shard_map/ppermute | solution.py:359
  60.0 8.7 %project.1 = (bf16[2,272,512]{2,1,0:T(8,128)(2,1)S(1)}, bf16[2,272,512]{2,1,0:T(8,128)(2,1)}, bf16[2,272,512]{2,1,0:T(8,128)(2,1)}, bf16[2,272,512]{2,1,0:T(8,12...) custom-call(s32[5]{0:T(128)S(1)} %stack.23.place, ...), custom_call_target="tpu_custom_call" | custom-call | flops 4294967296 | bytes 14680064 | tf_op jit(solution)/shard_map/project/pallas_call | solution.py:238
  68.7 2.2 %collective-permute-start.11 = (bf16[4,240,512]{2,1,0:T(8,128)(2,1)}, bf16[4,240,512]{2,1,0:T(8,128)(2,1)S(1)}, u32[]{:S(2)}, u32[]{:S(2)}) collective-permute-start(bf16[4,240,512]{2,1,0:T(8,128)(2,1)} %get-tuple-element.54), channel_id=1, source_target_pairs={{0,2},{1,3},{2,0},{3,1},{4,6},{5,7},{6,4},{7,5},{8,10},{9,11},{10,... | collective-permute-start | bytes 2949128 | tf_op jit(solution)/shard_map/ppermute | solution.py:363
  70.9 3.2 %collective-permute-start.12 = (bf16[2,272,512]{2,1,0:T(8,128)(2,1)}, bf16[2,272,512]{2,1,0:T(8,128)(2,1)S(1)}, u32[]{:S(2)}, u32[]{:S(2)}) collective-permute-start(bf16[2,272,512]{2,1,0:T(8,128)(2,1)} %get-tuple-element.57), channel_id=1, source_target_pairs={{0,8},{1,9},{2,10},{3,11},{4,12},{5,13},{6,14},{7,15},{8,0},{9,1},... | collective-permute-start | bytes 1671176 | tf_op jit(solution)/shard_map/ppermute | solution.py:364
  74.1 0.7 collective-permute-start.13
  74.8 2.6 %collective-permute-start.14 = (bf16[2,272,512]{2,1,0:T(8,128)(2,1)}, bf16[2,272,512]{2,1,0:T(8,128)(2,1)S(1)}, u32[]{:S(2)}, u32[]{:S(2)}) collective-permute-start(bf16[2,272,512]{2,1,0:T(8,128)(2,1)} %get-tuple-element.59), channel_id=1, source_target_pairs={{0,12},{1,13},{2,14},{3,15},{4,0},{5,1},{6,2},{7,3},{8,4},{9,5},{1... | collective-permute-start | bytes 1671176 | tf_op jit(solution)/shard_map/ppermute | solution.py:364
  77.3 11.5 %hyena.1 = bf16[512,512]{1,0:T(8,128)(2,1)} custom-call(bf16[512,512]{1,0:T(8,128)(2,1)S(1)} %copy-done.2, bf16[512,512]{1,0:T(8,128)(2,1)S(1)} %copy-done, bf16[512,512]{1,0:T(8,128)(2,1)S(1)} %copy-done.1, bf16[128,512]{1,0:T(8,128)(2,1)S(1)} %collective-permute-done.6.rim_ref, bf16[128,512]{1,0:T(8,128)(2,1)S(1)} %copy-done.3), custom_call_target="tpu_custom_call" | custom-call | flops 10000000 | bytes 3072 | tf_op jit(solution)/shard_map/hyena/pallas_call | solution.py:289
  88.9 4.3 %collective-permute-done.11 = bf16[4,240,512]{2,1,0:T(8,128)(2,1)S(1)} collective-permute-done((bf16[4,240,512]{2,1,0:T(8,128)(2,1)}, bf16[4,240,512]{2,1,0:T(8,128)(2,1)S(1)}, u32[]{:S(2)}, u32[]{:S(2)}) %collective-permute-start.11) | collective-permute-done | bytes 983072 | tf_op jit(solution)/shard_map/ppermute | solution.py:363
  93.6 1.6 %collective-permute-start.16 = (bf16[240,512]{1,0:T(8,128)(2,1)S(1)}, bf16[240,512]{1,0:T(8,128)(2,1)S(1)}, u32[]{:S(2)}, u32[]{:S(2)}) collective-permute-start(bf16[240,512]{1,0:T(8,128)(2,1)S(1)} %get-tuple-element.68), channel_id=1, source_target_pairs={{0,4},{1,5},{2,6},{3,7},{4,8},{5,9},{6,10},{7,11},{8,12},{9,13},{1... | collective-permute-start | bytes 737288 | tf_op jit(solution)/shard_map/ppermute | solution.py:372
  95.3 1.7 %collective-permute-start.18 = (bf16[240,512]{1,0:T(8,128)(2,1)S(1)}, bf16[240,512]{1,0:T(8,128)(2,1)S(1)}, u32[]{:S(2)}, u32[]{:S(2)}) collective-permute-start(bf16[240,512]{1,0:T(8,128)(2,1)S(1)} %get-tuple-element.69), channel_id=1, source_target_pairs={{0,12},{1,13},{2,14},{3,15},{4,0},{5,1},{6,2},{7,3},{8,4},{9,5},{1... | collective-permute-start | bytes 737288 | tf_op jit(solution)/shard_map/ppermute | solution.py:372
  96.9 2.0 %collective-permute-start.17 = (bf16[240,512]{1,0:T(8,128)(2,1)S(1)}, bf16[240,512]{1,0:T(8,128)(2,1)S(1)}, u32[]{:S(2)}, u32[]{:S(2)}) collective-permute-start(bf16[240,512]{1,0:T(8,128)(2,1)S(1)} %get-tuple-element.70), channel_id=1, source_target_pairs={{0,8},{1,9},{2,10},{3,11},{4,12},{5,13},{6,14},{7,15},{8,0},{9,1},... | collective-permute-start | bytes 737288 | tf_op jit(solution)/shard_map/ppermute | solution.py:372
  99.4 1.1 collective-permute-done.14.three_ref
  101.0 3.9 %collective-permute-done.16 = bf16[240,512]{1,0:T(8,128)(2,1)S(1)} collective-permute-done((bf16[240,512]{1,0:T(8,128)(2,1)S(1)}, bf16[240,512]{1,0:T(8,128)(2,1)S(1)}, u32[]{:S(2)}, u32[]{:S(2)}) %collective-permute-start.16) | collective-permute-done | bytes 245792 | tf_op jit(solution)/shard_map/ppermute | solution.py:372
  104.9 0.8 collective-permute-done.18
  105.7 3.8 %collective-permute-done.17 = bf16[240,512]{1,0:T(8,128)(2,1)S(1)} collective-permute-done((bf16[240,512]{1,0:T(8,128)(2,1)S(1)}, bf16[240,512]{1,0:T(8,128)(2,1)S(1)}, u32[]{:S(2)}, u32[]{:S(2)}) %collective-permute-start.17) | collective-permute-done | bytes 245792 | tf_op jit(solution)/shard_map/ppermute | solution.py:372
  109.8 0.8 pad_maximum_fusion
  (47 shorter events, 2.8 us)
Async XLA Ops:
  0.6 15.6 %collective-permute-start.5 = (bf16[512,8192]{1,0:T(8,128)(2,1)}, bf16[512,8192]{1,0:T(8,128)(2,1)}, u32[]{:S(2)}, u32[]{:S(2)}) collective-permute-start(bf16[512,8192]{1,0:T(8,128)(2,1)} %w_own.1), channel_id=1, source_target_pairs={{0,1},{1,0},{2,3},{3,2},{4,5},{5,4},{6,7},{7,6},{8,9},{9,8},{10,11... | collective-permute-start | bytes 25165832 | tf_op jit(solution)/shard_map/ppermute | solution.py:342
  4.0 9.4 %copy-start.7 = (bf16[512,256]{1,0:T(8,128)(2,1)S(1)}, bf16[512,256]{1,0:T(8,128)(2,1)}, u32[]{:S(2)}) copy-start(bf16[512,256]{1,0:T(8,128)(2,1)} %get-tuple-element.37) | copy-start | bytes 786436
  4.0 10.8 %copy-start.6 = (s32[4096]{0:T(1024)S(1)}, s32[4096]{0:T(1024)}, u32[]{:S(2)}) copy-start(s32[4096]{0:T(1024)} %param.16) | copy-start | bytes 49156
  4.0 12.2 %slice-start = ((bf16[512,512]{1,0:T(8,128)(2,1)}), bf16[128,512]{1,0:T(8,128)(2,1)S(1)}, s32[]{:S(2)}) async-start(bf16[512,512]{1,0:T(8,128)(2,1)} %k_ref.3), calls=%async_computation.1 | async-start | bytes 262144 | tf_op jit(solution)/shard_map/slice | solution.py:350
  4.0 12.2 %slice-start.1 = ((bf16[512,512]{1,0:T(8,128)(2,1)}), bf16[128,512]{1,0:T(8,128)(2,1)S(1)}, s32[]{:S(2)}) async-start(bf16[512,512]{1,0:T(8,128)(2,1)} %v_ref.3), calls=%async_computation.2 | async-start | bytes 262144 | tf_op jit(solution)/shard_map/slice | solution.py:350
  4.0 33.2 %all-to-all-start = ((bf16[4,512,384]{2,1,0:T(8,128)(2,1)}), bf16[4,512,384]{2,1,0:T(8,128)(2,1)S(1)}, u32[]{:S(2)}, u32[]{:S(2)}) async-start(bf16[4,512,384]{2,1,0:T(8,128)(2,1)} %get-tuple-element.38), calls=%async_computation | async-start | bytes 3145728 | tf_op jit(solution)/shard_map/all_to_all | solution.py:346
  9.5 5.5 %collective-permute-start.2 = (bf16[512,256]{1,0:T(8,128)(2,1)}, bf16[512,256]{1,0:T(8,128)(2,1)}, u32[]{:S(2)}, u32[]{:S(2)}) collective-permute-start(bf16[512,256]{1,0:T(8,128)(2,1)} %get-tuple-element.36), channel_id=1, source_target_pairs={{0,32},{16,48},{32,0},{48,16},{1,33},{17,49},{33,1},{49,17},{2,34}... | collective-permute-start | bytes 786440 | tf_op jit(solution)/shard_map/ppermute | solution.py:344
  10.9 31.3 %collective-permute-start = (bf16[512,256]{1,0:T(8,128)(2,1)}, bf16[512,256]{1,0:T(8,128)(2,1)S(1)}, u32[]{:S(2)}, u32[]{:S(2)}) collective-permute-start(bf16[512,256]{1,0:T(8,128)(2,1)} %get-tuple-element.34), channel_id=1, source_target_pairs={{0,64},{16,80},{32,96},{48,112},{1,65},{17,81},{33,97},{49,113},{2... | collective-permute-start | bytes 786440 | tf_op jit(solution)/shard_map/ppermute | solution.py:345
  12.1 30.1 %collective-permute-start.1 = (bf16[512,256]{1,0:T(8,128)(2,1)}, bf16[512,256]{1,0:T(8,128)(2,1)S(1)}, u32[]{:S(2)}, u32[]{:S(2)}) collective-permute-start(bf16[512,256]{1,0:T(8,128)(2,1)} %get-tuple-element.35), channel_id=1, source_target_pairs={{0,80},{16,96},{32,112},{48,64},{1,81},{17,97},{33,113},{49,65},{2... | collective-permute-start | bytes 786440 | tf_op jit(solution)/shard_map/ppermute | solution.py:345
  13.5 28.8 %collective-permute-start.4 = (bf16[512,256]{1,0:T(8,128)(2,1)S(1)}, bf16[512,256]{1,0:T(8,128)(2,1)S(1)}, u32[]{:S(2)}, u32[]{:S(2)}) collective-permute-start(bf16[512,256]{1,0:T(8,128)(2,1)S(1)} %copy-done.7), channel_id=1, source_target_pairs={{0,112},{16,64},{32,80},{48,96},{1,113},{17,65},{33,81},{49,97},{2... | collective-permute-start | bytes 786440 | tf_op jit(solution)/shard_map/ppermute | solution.py:345
  15.0 29.5 %collective-permute-start.3 = (bf16[512,256]{1,0:T(8,128)(2,1)}, bf16[512,256]{1,0:T(8,128)(2,1)S(1)}, u32[]{:S(2)}, u32[]{:S(2)}) collective-permute-start(bf16[512,256]{1,0:T(8,128)(2,1)} %collective-permute-done.2), channel_id=1, source_target_pairs={{0,64},{16,80},{32,96},{48,112},{1,65},{17,81},{33,97},{49,113},{2... | collective-permute-start | bytes 786440 | tf_op jit(solution)/shard_map/ppermute | solution.py:347
  16.3 40.3 %collective-permute-start.6 = (bf16[128,512]{1,0:T(8,128)(2,1)S(1)}, bf16[128,512]{1,0:T(8,128)(2,1)S(1)}, u32[]{:S(2)}, u32[]{:S(2)}) collective-permute-start(bf16[128,512]{1,0:T(8,128)(2,1)S(1)} %multiply_convert_fusion), channel_id=1, source_target_pairs={{0,16},{16,32},{32,48},{48,64},{64,80},{80,96},{96,112},{1,17},{17... | collective-permute-start | bytes 393224 | tf_op jit(solution)/shard_map/ppermute | solution.py:352
  45.9 10.7 %collective-permute-start.7 = (bf16[512,128]{1,0:T(8,128)(2,1)S(1)}, bf16[512,128]{1,0:T(8,128)(2,1)S(1)}, u32[]{:S(2)}, u32[]{:S(2)}) collective-permute-start(bf16[512,128]{1,0:T(8,128)(2,1)S(1)} %get-tuple-element.48), channel_id=1, source_target_pairs={{0,16},{16,32},{32,48},{48,0},{64,80},{80,96},{96,112},{112,64},{1... | collective-permute-start | bytes 393224 | tf_op jit(solution)/shard_map/ppermute | solution.py:355
  49.4 7.7 %collective-permute-start.8 = (bf16[512,128]{1,0:T(8,128)(2,1)S(1)}, bf16[512,128]{1,0:T(8,128)(2,1)S(1)}, u32[]{:S(2)}, u32[]{:S(2)}) collective-permute-start(bf16[512,128]{1,0:T(8,128)(2,1)S(1)} %get-tuple-element.49), channel_id=1, source_target_pairs={{0,32},{16,48},{32,0},{48,16},{64,96},{80,112},{96,64},{112,80},{1... | collective-permute-start | bytes 393224 | tf_op jit(solution)/shard_map/ppermute | solution.py:355
  52.8 5.0 %collective-permute-start.9 = (bf16[512,128]{1,0:T(8,128)(2,1)S(1)}, bf16[512,128]{1,0:T(8,128)(2,1)S(1)}, u32[]{:S(2)}, u32[]{:S(2)}) collective-permute-start(bf16[512,128]{1,0:T(8,128)(2,1)S(1)} %get-tuple-element.50), channel_id=1, source_target_pairs={{0,48},{16,0},{32,16},{48,32},{64,112},{80,64},{96,80},{112,96},{1... | collective-permute-start | bytes 393224 | tf_op jit(solution)/shard_map/ppermute | solution.py:355
  57.7 19.6 %copy-start = (bf16[512,512]{1,0:T(8,128)(2,1)S(1)}, bf16[512,512]{1,0:T(8,128)(2,1)}, u32[]{:S(2)}) copy-start(bf16[512,512]{1,0:T(8,128)(2,1)} %k_ref.3) | copy-start | bytes 1572868
  57.8 19.6 %copy-start.1 = (bf16[512,512]{1,0:T(8,128)(2,1)S(1)}, bf16[512,512]{1,0:T(8,128)(2,1)}, u32[]{:S(2)}) copy-start(bf16[512,512]{1,0:T(8,128)(2,1)} %v_ref.3) | copy-start | bytes 1572868
  57.8 19.6 %copy-start.2 = (bf16[512,512]{1,0:T(8,128)(2,1)S(1)}, bf16[512,512]{1,0:T(8,128)(2,1)}, u32[]{:S(2)}) copy-start(bf16[512,512]{1,0:T(8,128)(2,1)} %q_ref.2) | copy-start | bytes 1572868
  57.8 19.6 %copy-start.3 = (bf16[128,512]{1,0:T(8,128)(2,1)S(1)}, bf16[128,512]{1,0:T(8,128)(2,1)}, u32[]{:S(2)}) copy-start(bf16[128,512]{1,0:T(8,128)(2,1)} %f_ref.1) | copy-start | bytes 393220
  57.8 2.2 %collective-permute-start.10 = (bf16[2048,128]{1,0:T(8,128)(2,1)S(1)}, bf16[2048,128]{1,0:T(8,128)(2,1)S(1)}, u32[]{:S(2)}, u32[]{:S(2)}) collective-permute-start(bf16[2048,128]{1,0:T(8,128)(2,1)S(1)} %constant_dynamic-update-slice_fusion.own_ref), channel_id=1, source_target_pairs={{0,1},{1,0},{2,3},{3,2},{4,5},{5,4},{6,7},{7,6},{8,9},{9,8},{10,11... | collective-permute-start | bytes 1572872 | tf_op jit(solution)/shard_map/ppermute | solution.py:359
  68.7 24.5 %copy-start.5 = (bf16[4,240,512]{2,1,0:T(8,128)(2,1)S(1)}, bf16[4,240,512]{2,1,0:T(8,128)(2,1)}, u32[]{:S(2)}) copy-start(bf16[4,240,512]{2,1,0:T(8,128)(2,1)} %get-tuple-element.51) | copy-start | bytes 2949124
  68.7 24.4 %collective-permute-start.11 = (bf16[4,240,512]{2,1,0:T(8,128)(2,1)}, bf16[4,240,512]{2,1,0:T(8,128)(2,1)S(1)}, u32[]{:S(2)}, u32[]{:S(2)}) collective-permute-start(bf16[4,240,512]{2,1,0:T(8,128)(2,1)} %get-tuple-element.54), channel_id=1, source_target_pairs={{0,2},{1,3},{2,0},{3,1},{4,6},{5,7},{6,4},{7,5},{8,10},{9,11},{10,... | collective-permute-start | bytes 2949128 | tf_op jit(solution)/shard_map/ppermute | solution.py:363
  70.9 26.0 %collective-permute-start.12 = (bf16[2,272,512]{2,1,0:T(8,128)(2,1)}, bf16[2,272,512]{2,1,0:T(8,128)(2,1)S(1)}, u32[]{:S(2)}, u32[]{:S(2)}) collective-permute-start(bf16[2,272,512]{2,1,0:T(8,128)(2,1)} %get-tuple-element.57), channel_id=1, source_target_pairs={{0,8},{1,9},{2,10},{3,11},{4,12},{5,13},{6,14},{7,15},{8,0},{9,1},... | collective-permute-start | bytes 1671176 | tf_op jit(solution)/shard_map/ppermute | solution.py:364
  74.1 25.3 %collective-permute-start.13 = (bf16[2,272,512]{2,1,0:T(8,128)(2,1)}, bf16[2,272,512]{2,1,0:T(8,128)(2,1)S(1)}, u32[]{:S(2)}, u32[]{:S(2)}) collective-permute-start(bf16[2,272,512]{2,1,0:T(8,128)(2,1)} %get-tuple-element.58), channel_id=1, source_target_pairs={{0,4},{1,5},{2,6},{3,7},{4,8},{5,9},{6,10},{7,11},{8,12},{9,13},{1... | collective-permute-start | bytes 1671176 | tf_op jit(solution)/shard_map/ppermute | solution.py:364
  74.8 25.7 %collective-permute-start.14 = (bf16[2,272,512]{2,1,0:T(8,128)(2,1)}, bf16[2,272,512]{2,1,0:T(8,128)(2,1)S(1)}, u32[]{:S(2)}, u32[]{:S(2)}) collective-permute-start(bf16[2,272,512]{2,1,0:T(8,128)(2,1)} %get-tuple-element.59), channel_id=1, source_target_pairs={{0,12},{1,13},{2,14},{3,15},{4,0},{5,1},{6,2},{7,3},{8,4},{9,5},{1... | collective-permute-start | bytes 1671176 | tf_op jit(solution)/shard_map/ppermute | solution.py:364
  93.6 11.3 %collective-permute-start.16 = (bf16[240,512]{1,0:T(8,128)(2,1)S(1)}, bf16[240,512]{1,0:T(8,128)(2,1)S(1)}, u32[]{:S(2)}, u32[]{:S(2)}) collective-permute-start(bf16[240,512]{1,0:T(8,128)(2,1)S(1)} %get-tuple-element.68), channel_id=1, source_target_pairs={{0,4},{1,5},{2,6},{3,7},{4,8},{5,9},{6,10},{7,11},{8,12},{9,13},{1... | collective-permute-start | bytes 737288 | tf_op jit(solution)/shard_map/ppermute | solution.py:372
  95.3 10.5 %collective-permute-start.18 = (bf16[240,512]{1,0:T(8,128)(2,1)S(1)}, bf16[240,512]{1,0:T(8,128)(2,1)S(1)}, u32[]{:S(2)}, u32[]{:S(2)}) collective-permute-start(bf16[240,512]{1,0:T(8,128)(2,1)S(1)} %get-tuple-element.69), channel_id=1, source_target_pairs={{0,12},{1,13},{2,14},{3,15},{4,0},{5,1},{6,2},{7,3},{8,4},{9,5},{1... | collective-permute-start | bytes 737288 | tf_op jit(solution)/shard_map/ppermute | solution.py:372
  96.9 12.6 %collective-permute-start.17 = (bf16[240,512]{1,0:T(8,128)(2,1)S(1)}, bf16[240,512]{1,0:T(8,128)(2,1)S(1)}, u32[]{:S(2)}, u32[]{:S(2)}) collective-permute-start(bf16[240,512]{1,0:T(8,128)(2,1)S(1)} %get-tuple-element.70), channel_id=1, source_target_pairs={{0,8},{1,9},{2,10},{3,11},{4,12},{5,13},{6,14},{7,15},{8,0},{9,1},... | collective-permute-start | bytes 737288 | tf_op jit(solution)/shard_map/ppermute | solution.py:372
  100.4 9.0 %copy-start.4 = (bf16[512,512]{1,0:T(8,128)(2,1)S(1)}, bf16[512,512]{1,0:T(8,128)(2,1)}, u32[]{:S(2)}) copy-start(bf16[512,512]{1,0:T(8,128)(2,1)} %hyena.1) | copy-start | bytes 1572868
  100.7 9.0 %collective-permute-start.15 = (bf16[272,512]{1,0:T(8,128)(2,1)S(1)}, bf16[272,512]{1,0:T(8,128)(2,1)S(1)}, u32[]{:S(2)}, u32[]{:S(2)}) collective-permute-start(bf16[272,512]{1,0:T(8,128)(2,1)S(1)} %get-tuple-element.65), channel_id=1, source_target_pairs={{0,2},{1,3},{2,0},{3,1},{4,6},{5,7},{6,4},{7,5},{8,10},{9,11},{10,... | collective-permute-start | bytes 835592 | tf_op jit(solution)/shard_map/ppermute | solution.py:375

commit v5 on v4

--- a/solution.py
+++ b/solution.py
@@ -374,11 +374,11 @@
     a_part, a_mine = add_terms(a_keep, a_got)
     a_term = lax.ppermute(a_part, "head", flip_pairs(2))
     a_final = a_mine + a_term.astype(F32)
-    b_final = b_sum[0]
+    b_final = lax.optimization_barrier(hyena_out[A_ROWS:].astype(F32) + b_sum[0])
     for term in b_terms:
         b_final = b_final + term.astype(F32)
     stream_a = (hyena_out[:A_ROWS].astype(F32) + a_final).astype(BF16)
-    stream_b = (hyena_out[A_ROWS:].astype(F32) + b_final).astype(BF16)
+    stream_b = b_final.astype(BF16)
     stream = jnp.concatenate([stream_a, stream_b], axis=0)
     return (hyena_out, stream)
 

time: 111 us -> 112 us (level)
  Pallas kernels: 34.1 us -> 36.2 us
  starting transfers between devices: 37.3 us -> 35.9 us
    ppermute x3, waiting for transfers between devices: 1.03 us -> 2.47 us  [on_device(): lax.ppermute(part, 'ctx', z_pairs(by))]
    pallas_call x2, Pallas kernels: 5.3 us -> 6.71 us  [attend_earlier(): pl.pallas_call(functools.partial(attend_earlier_kernel, order), grid_spec...]
    ppermute x3, starting transfers between devices: 6.86 us -> 5.46 us  [on_device(): lax.ppermute(part, 'ctx', z_pairs(by))]
  transfers between devices with their start and end apart: 20 -> 20, of which waited for: 11 -> 11; matrix products, arithmetic and copies ran while one was open for 1% -> 1% of each run, Pallas kernels for 23% -> 25%
where the time goes in v5:
time: 112 us
  waiting for transfers between devices  36.6 us (33%)
  Pallas kernels  36.2 us (32%)
  starting transfers between devices  35.9 us (32%)
  other arithmetic  1.59 us (1%)
    all_to_all x1, waiting for transfers between devices, on_device(): lax.all_to_all(packed, 'ctx', 0, 0, axis_index_groups=[[0, 1, 2, 3], [4,...  16.9 us
    pallas_call x1, Pallas kernels, hyena(): pl.pallas_call(hyena_kernel, in_specs=vmem_specs(5), out_specs=pl.BlockSp...  11.5 us
    pallas_call x1, Pallas kernels, project(): pl.pallas_call(project_kernel, grid_spec=pltpu.PrefetchScalarGridSpec(num...  8.72 us
    ppermute x3, waiting for transfers between devices, on_device(): b_terms = [lax.ppermute(b_parts[d], 'head', y_pairs(d)) for d in (1, 2, 3)]  7.96 us
    pallas_call x2, Pallas kernels, attend_earlier(): pl.pallas_call(functools.partial(attend_earlier_kernel, order), grid_spec...  6.71 us
    ppermute x3, starting transfers between devices, on_device(): a_got = [lax.ppermute(a_terms[d], 'head', y_pairs(d)) for d in (2, 1, 3)]  6.42 us
    pallas_call x1, Pallas kernels, attend_own(): pl.pallas_call(attend_own_kernel, grid_spec=pltpu.PrefetchScalarGridSpec(...  5.69 us
    ppermute x3, starting transfers between devices, on_device(): lax.ppermute(part, 'ctx', z_pairs(by))  5.46 us
  transfers between devices with their start and end apart: 20, of which 11 were waited for; matrix products, arithmetic and copies ran while one was open for 1% of the time, Pallas kernels for 25%

profile of v5, /device:TPU:4, one launch (start us, length us, event | category | flops | bytes accessed | tf_op | source)
XLA Modules:
  0.0 112.1 jit_solution(7489380852208577701)
XLA Ops:
  0.7 3.3 %pack.1 = (bf16[4,512,384]{2,1,0:T(8,128)(2,1)}, bf16[512,256]{1,0:T(8,128)(2,1)}, bf16[512,256]{1,0:T(8,128)(2,1)}, bf16[512,256]{1,0:T(8,128)(2,1)}, bf16[512,256]{1,0:T(8,128)(2,1)}) custom-call(bf16[512,512]{1,0:T(8,128)(2,1)} %q_ref.1, bf16[512,512]{1,0:T(8,128)(2,1)} %k_ref.2, bf16[512,512]{1,0:T(8,128)(2,1)} %v_ref.2), custom_call_target="tpu_custom_call" | custom-call | bytes 4194304 | tf_op jit(solution)/shard_map/pack/pallas_call | solution.py:56
  4.0 5.5 %all-to-all-start = ((bf16[4,512,384]{2,1,0:T(8,128)(2,1)}), bf16[4,512,384]{2,1,0:T(8,128)(2,1)S(1)}, u32[]{:S(2)}, u32[]{:S(2)}) async-start(bf16[4,512,384]{2,1,0:T(8,128)(2,1)} %get-tuple-element.38), calls=%async_computation | async-start | bytes 3145728 | tf_op jit(solution)/shard_map/all_to_all | solution.py:346
  9.5 1.4 %collective-permute-start.2 = (bf16[512,256]{1,0:T(8,128)(2,1)}, bf16[512,256]{1,0:T(8,128)(2,1)}, u32[]{:S(2)}, u32[]{:S(2)}) collective-permute-start(bf16[512,256]{1,0:T(8,128)(2,1)} %get-tuple-element.36), channel_id=1, source_target_pairs={{0,32},{16,48},{32,0},{48,16},{1,33},{17,49},{33,1},{49,17},{2,34}... | collective-permute-start | bytes 786440 | tf_op jit(solution)/shard_map/ppermute | solution.py:344
  10.9 1.3 %collective-permute-start = (bf16[512,256]{1,0:T(8,128)(2,1)}, bf16[512,256]{1,0:T(8,128)(2,1)S(1)}, u32[]{:S(2)}, u32[]{:S(2)}) collective-permute-start(bf16[512,256]{1,0:T(8,128)(2,1)} %get-tuple-element.34), channel_id=1, source_target_pairs={{0,64},{16,80},{32,96},{48,112},{1,65},{17,81},{33,97},{49,113},{2... | collective-permute-start | bytes 786440 | tf_op jit(solution)/shard_map/ppermute | solution.py:345
  12.1 1.3 %collective-permute-start.1 = (bf16[512,256]{1,0:T(8,128)(2,1)}, bf16[512,256]{1,0:T(8,128)(2,1)S(1)}, u32[]{:S(2)}, u32[]{:S(2)}) collective-permute-start(bf16[512,256]{1,0:T(8,128)(2,1)} %get-tuple-element.35), channel_id=1, source_target_pairs={{0,80},{16,96},{32,112},{48,64},{1,81},{17,97},{33,113},{49,65},{2... | collective-permute-start | bytes 786440 | tf_op jit(solution)/shard_map/ppermute | solution.py:345
  13.5 1.3 %collective-permute-start.4 = (bf16[512,256]{1,0:T(8,128)(2,1)S(1)}, bf16[512,256]{1,0:T(8,128)(2,1)S(1)}, u32[]{:S(2)}, u32[]{:S(2)}) collective-permute-start(bf16[512,256]{1,0:T(8,128)(2,1)S(1)} %copy-done.7), channel_id=1, source_target_pairs={{0,112},{16,64},{32,80},{48,96},{1,113},{17,65},{33,81},{49,97},{2... | collective-permute-start | bytes 786440 | tf_op jit(solution)/shard_map/ppermute | solution.py:345
  15.0 1.3 %collective-permute-start.3 = (bf16[512,256]{1,0:T(8,128)(2,1)}, bf16[512,256]{1,0:T(8,128)(2,1)S(1)}, u32[]{:S(2)}, u32[]{:S(2)}) collective-permute-start(bf16[512,256]{1,0:T(8,128)(2,1)} %collective-permute-done.2), channel_id=1, source_target_pairs={{0,64},{16,80},{32,96},{48,112},{1,65},{17,81},{33,97},{49,113},{2... | collective-permute-start | bytes 786440 | tf_op jit(solution)/shard_map/ppermute | solution.py:347
  16.3 3.9 %collective-permute-start.6 = (bf16[128,512]{1,0:T(8,128)(2,1)S(1)}, bf16[128,512]{1,0:T(8,128)(2,1)S(1)}, u32[]{:S(2)}, u32[]{:S(2)}) collective-permute-start(bf16[128,512]{1,0:T(8,128)(2,1)S(1)} %multiply_convert_fusion), channel_id=1, source_target_pairs={{0,16},{16,32},{32,48},{48,64},{64,80},{80,96},{96,112},{1,17},{17... | collective-permute-start | bytes 393224 | tf_op jit(solution)/shard_map/ppermute | solution.py:352
  20.3 16.9 %all-to-all-done.qkv_ref = bf16[4,512,384]{2,1,0:T(8,128)(2,1)S(1)} async-done(((bf16[4,512,384]{2,1,0:T(8,128)(2,1)}), bf16[4,512,384]{2,1,0:T(8,128)(2,1)S(1)}, u32[]{:S(2)}, u32[]{:S(2)}) %all-to-all-start) | async-done | bytes 1572896 | tf_op jit(solution)/shard_map/all_to_all | solution.py:346
  37.2 5.7 %attend_own.1 = (bf16[3,512,128]{2,1,0:T(8,128)(2,1)S(1)}, f32[3,128,512]{2,1,0:T(8,128)S(1)}, f32[3,16,512]{2,1,0:T(8,128)S(1)}, bf16[1,512,128]{2,1,0:T(8,128)...) custom-call(s32[5]{0:T(128)S(1)} %stack.23.place, s32[8,512]{1,0:T(8,128)S(1)} %reshape.10.ids_ref, ...), custom_call_target="tpu_custom_call" | custom-call | flops 4000000000 | bytes 4194304 | tf_op jit(solution)/shard_map/attend_own/pallas_call | solution.py:129
  42.9 1.5 %collective-permute-done.3.rest_2_ = bf16[512,256]{1,0:T(8,128)(2,1)S(1)} collective-permute-done((bf16[512,256]{1,0:T(8,128)(2,1)}, bf16[512,256]{1,0:T(8,128)(2,1)S(1)}, u32[]{:S(2)}, u32[]{:S(2)}) %collective-permute-start.3) | collective-permute-done | bytes 262176 | tf_op jit(solution)/shard_map/ppermute | solution.py:347
  44.4 4.3 %attend_earlier.3 = (bf16[512,128]{1,0:T(8,128)(2,1)S(1)}, bf16[512,128]{1,0:T(8,128)(2,1)S(1)}, bf16[512,128]{1,0:T(8,128)(2,1)S(1)}) custom-call(s32[5]{0:T(128)S(1)} %stack.23.place, s32[8,512]{1,0:T(8,128)S(1)} %reshape.10.ids_ref, bf16[512,256]{1,0:T(8,128)(2,1)S(1)} %collective-permute-done.rest_0_, ...), custom_call_target="tpu_custom_call" | custom-call | flops 3000000 | bytes 4096 | tf_op jit(solution)/shard_map/attend_earlier/pallas_call | solution.py:174
  48.7 0.6 collective-permute-start.7
  49.4 4.8 %collective-permute-start.8 = (bf16[512,128]{1,0:T(8,128)(2,1)S(1)}, bf16[512,128]{1,0:T(8,128)(2,1)S(1)}, u32[]{:S(2)}, u32[]{:S(2)}) collective-permute-start(bf16[512,128]{1,0:T(8,128)(2,1)S(1)} %get-tuple-element.49), channel_id=1, source_target_pairs={{0,32},{16,48},{32,0},{48,16},{64,96},{80,112},{96,64},{112,80},{1... | collective-permute-start | bytes 393224 | tf_op jit(solution)/shard_map/ppermute | solution.py:355
  54.2 2.4 %attend_earlier.2 = bf16[512,128]{1,0:T(8,128)(2,1)S(1)} custom-call(s32[5]{0:T(128)S(1)} %stack.23.place, s32[8,512]{1,0:T(8,128)S(1)} %reshape.10.ids_ref, bf16[512,256]{1,0:T(8,128)(2,1)S(1)} %collective-permute-done.rest_0_, bf16[512,256]{1,0:T(8,128)(2,1)S(1)} %collective-permute-done.1.rest_1_, bf16[512,256]{1,0:T(8,128)(2,1)S(1)} %collective-permute-done.3.rest_2_, ...), custom_call_target="tpu_custom_call" | custom-call | flops 1000000 | bytes 4096 | tf_op jit(solution)/shard_map/attend_earlier/pallas_call | solution.py:174
  56.7 1.9 %collective-permute-done.8 = bf16[512,128]{1,0:T(8,128)(2,1)S(1)} collective-permute-done((bf16[512,128]{1,0:T(8,128)(2,1)S(1)}, bf16[512,128]{1,0:T(8,128)(2,1)S(1)}, u32[]{:S(2)}, u32[]{:S(2)}) %collective-permute-start.8) | collective-permute-done | bytes 131104 | tf_op jit(solution)/shard_map/ppermute | solution.py:355
  59.5 1.9 %collective-permute-done.10.sib_ref = bf16[2048,128]{1,0:T(8,128)(2,1)S(1)} collective-permute-done((bf16[2048,128]{1,0:T(8,128)(2,1)S(1)}, bf16[2048,128]{1,0:T(8,128)(2,1)S(1)}, u32[]{:S(2)}, u32[]{:S(2)}) %collective-permute-start.10) | collective-permute-done | bytes 524320 | tf_op jit(solution)/shard_map/ppermute | solution.py:359
  61.4 8.7 %project.1 = (bf16[2,272,512]{2,1,0:T(8,128)(2,1)S(1)}, bf16[2,272,512]{2,1,0:T(8,128)(2,1)}, bf16[2,272,512]{2,1,0:T(8,128)(2,1)}, bf16[2,272,512]{2,1,0:T(8,12...) custom-call(s32[5]{0:T(128)S(1)} %stack.23.place, ...), custom_call_target="tpu_custom_call" | custom-call | flops 4294967296 | bytes 14680064 | tf_op jit(solution)/shard_map/project/pallas_call | solution.py:238
  70.1 2.2 %collective-permute-start.11 = (bf16[4,240,512]{2,1,0:T(8,128)(2,1)}, bf16[4,240,512]{2,1,0:T(8,128)(2,1)S(1)}, u32[]{:S(2)}, u32[]{:S(2)}) collective-permute-start(bf16[4,240,512]{2,1,0:T(8,128)(2,1)} %get-tuple-element.54), channel_id=1, source_target_pairs={{0,2},{1,3},{2,0},{3,1},{4,6},{5,7},{6,4},{7,5},{8,10},{9,11},{10,... | collective-permute-start | bytes 2949128 | tf_op jit(solution)/shard_map/ppermute | solution.py:363
  72.3 3.2 %collective-permute-start.12 = (bf16[2,272,512]{2,1,0:T(8,128)(2,1)}, bf16[2,272,512]{2,1,0:T(8,128)(2,1)S(1)}, u32[]{:S(2)}, u32[]{:S(2)}) collective-permute-start(bf16[2,272,512]{2,1,0:T(8,128)(2,1)} %get-tuple-element.57), channel_id=1, source_target_pairs={{0,8},{1,9},{2,10},{3,11},{4,12},{5,13},{6,14},{7,15},{8,0},{9,1},... | collective-permute-start | bytes 1671176 | tf_op jit(solution)/shard_map/ppermute | solution.py:364
  75.5 0.7 collective-permute-start.13
  76.2 2.6 %collective-permute-start.14 = (bf16[2,272,512]{2,1,0:T(8,128)(2,1)}, bf16[2,272,512]{2,1,0:T(8,128)(2,1)S(1)}, u32[]{:S(2)}, u32[]{:S(2)}) collective-permute-start(bf16[2,272,512]{2,1,0:T(8,128)(2,1)} %get-tuple-element.59), channel_id=1, source_target_pairs={{0,12},{1,13},{2,14},{3,15},{4,0},{5,1},{6,2},{7,3},{8,4},{9,5},{1... | collective-permute-start | bytes 1671176 | tf_op jit(solution)/shard_map/ppermute | solution.py:364
  78.8 11.5 %hyena.1 = bf16[512,512]{1,0:T(8,128)(2,1)} custom-call(bf16[512,512]{1,0:T(8,128)(2,1)S(1)} %copy-done.2, bf16[512,512]{1,0:T(8,128)(2,1)S(1)} %copy-done, bf16[512,512]{1,0:T(8,128)(2,1)S(1)} %copy-done.1, bf16[128,512]{1,0:T(8,128)(2,1)S(1)} %collective-permute-done.6.rim_ref, bf16[128,512]{1,0:T(8,128)(2,1)S(1)} %copy-done.3), custom_call_target="tpu_custom_call" | custom-call | flops 10000000 | bytes 3072 | tf_op jit(solution)/shard_map/hyena/pallas_call | solution.py:289
  90.3 4.3 %collective-permute-done.11 = bf16[4,240,512]{2,1,0:T(8,128)(2,1)S(1)} collective-permute-done((bf16[4,240,512]{2,1,0:T(8,128)(2,1)}, bf16[4,240,512]{2,1,0:T(8,128)(2,1)S(1)}, u32[]{:S(2)}, u32[]{:S(2)}) %collective-permute-start.11) | collective-permute-done | bytes 983072 | tf_op jit(solution)/shard_map/ppermute | solution.py:363
  95.1 1.6 %collective-permute-start.16 = (bf16[240,512]{1,0:T(8,128)(2,1)S(1)}, bf16[240,512]{1,0:T(8,128)(2,1)S(1)}, u32[]{:S(2)}, u32[]{:S(2)}) collective-permute-start(bf16[240,512]{1,0:T(8,128)(2,1)S(1)} %get-tuple-element.68), channel_id=1, source_target_pairs={{0,4},{1,5},{2,6},{3,7},{4,8},{5,9},{6,10},{7,11},{8,12},{9,13},{1... | collective-permute-start | bytes 737288 | tf_op jit(solution)/shard_map/ppermute | solution.py:372
  96.7 1.7 %collective-permute-start.18 = (bf16[240,512]{1,0:T(8,128)(2,1)S(1)}, bf16[240,512]{1,0:T(8,128)(2,1)S(1)}, u32[]{:S(2)}, u32[]{:S(2)}) collective-permute-start(bf16[240,512]{1,0:T(8,128)(2,1)S(1)} %get-tuple-element.69), channel_id=1, source_target_pairs={{0,12},{1,13},{2,14},{3,15},{4,0},{5,1},{6,2},{7,3},{8,4},{9,5},{1... | collective-permute-start | bytes 737288 | tf_op jit(solution)/shard_map/ppermute | solution.py:372
  98.4 2.0 %collective-permute-start.17 = (bf16[240,512]{1,0:T(8,128)(2,1)S(1)}, bf16[240,512]{1,0:T(8,128)(2,1)S(1)}, u32[]{:S(2)}, u32[]{:S(2)}) collective-permute-start(bf16[240,512]{1,0:T(8,128)(2,1)S(1)} %get-tuple-element.70), channel_id=1, source_target_pairs={{0,8},{1,9},{2,10},{3,11},{4,12},{5,13},{6,14},{7,15},{8,0},{9,1},... | collective-permute-start | bytes 737288 | tf_op jit(solution)/shard_map/ppermute | solution.py:372
  100.8 1.1 collective-permute-done.14.three_ref
  103.0 3.4 %collective-permute-done.16 = bf16[240,512]{1,0:T(8,128)(2,1)S(1)} collective-permute-done((bf16[240,512]{1,0:T(8,128)(2,1)S(1)}, bf16[240,512]{1,0:T(8,128)(2,1)S(1)}, u32[]{:S(2)}, u32[]{:S(2)}) %collective-permute-start.16) | collective-permute-done | bytes 245792 | tf_op jit(solution)/shard_map/ppermute | solution.py:372
  106.3 0.8 collective-permute-done.18
  107.1 3.8 %collective-permute-done.17 = bf16[240,512]{1,0:T(8,128)(2,1)S(1)} collective-permute-done((bf16[240,512]{1,0:T(8,128)(2,1)S(1)}, bf16[240,512]{1,0:T(8,128)(2,1)S(1)}, u32[]{:S(2)}, u32[]{:S(2)}) %collective-permute-start.17) | collective-permute-done | bytes 245792 | tf_op jit(solution)/shard_map/ppermute | solution.py:372
  111.2 0.8 pad_maximum_fusion
  (48 shorter events, 3.5 us)
Async XLA Ops:
  0.6 15.6 %collective-permute-start.5 = (bf16[512,8192]{1,0:T(8,128)(2,1)}, bf16[512,8192]{1,0:T(8,128)(2,1)}, u32[]{:S(2)}, u32[]{:S(2)}) collective-permute-start(bf16[512,8192]{1,0:T(8,128)(2,1)} %w_own.1), channel_id=1, source_target_pairs={{0,1},{1,0},{2,3},{3,2},{4,5},{5,4},{6,7},{7,6},{8,9},{9,8},{10,11... | collective-permute-start | bytes 25165832 | tf_op jit(solution)/shard_map/ppermute | solution.py:342
  4.0 9.4 %copy-start.7 = (bf16[512,256]{1,0:T(8,128)(2,1)S(1)}, bf16[512,256]{1,0:T(8,128)(2,1)}, u32[]{:S(2)}) copy-start(bf16[512,256]{1,0:T(8,128)(2,1)} %get-tuple-element.37) | copy-start | bytes 786436
  4.0 10.8 %copy-start.6 = (s32[4096]{0:T(1024)S(1)}, s32[4096]{0:T(1024)}, u32[]{:S(2)}) copy-start(s32[4096]{0:T(1024)} %param.16) | copy-start | bytes 49156
  4.0 12.2 %slice-start = ((bf16[512,512]{1,0:T(8,128)(2,1)}), bf16[128,512]{1,0:T(8,128)(2,1)S(1)}, s32[]{:S(2)}) async-start(bf16[512,512]{1,0:T(8,128)(2,1)} %k_ref.3), calls=%async_computation.1 | async-start | bytes 262144 | tf_op jit(solution)/shard_map/slice | solution.py:350
  4.0 12.2 %slice-start.1 = ((bf16[512,512]{1,0:T(8,128)(2,1)}), bf16[128,512]{1,0:T(8,128)(2,1)S(1)}, s32[]{:S(2)}) async-start(bf16[512,512]{1,0:T(8,128)(2,1)} %v_ref.3), calls=%async_computation.2 | async-start | bytes 262144 | tf_op jit(solution)/shard_map/slice | solution.py:350
  4.0 33.2 %all-to-all-start = ((bf16[4,512,384]{2,1,0:T(8,128)(2,1)}), bf16[4,512,384]{2,1,0:T(8,128)(2,1)S(1)}, u32[]{:S(2)}, u32[]{:S(2)}) async-start(bf16[4,512,384]{2,1,0:T(8,128)(2,1)} %get-tuple-element.38), calls=%async_computation | async-start | bytes 3145728 | tf_op jit(solution)/shard_map/all_to_all | solution.py:346
  9.5 5.5 %collective-permute-start.2 = (bf16[512,256]{1,0:T(8,128)(2,1)}, bf16[512,256]{1,0:T(8,128)(2,1)}, u32[]{:S(2)}, u32[]{:S(2)}) collective-permute-start(bf16[512,256]{1,0:T(8,128)(2,1)} %get-tuple-element.36), channel_id=1, source_target_pairs={{0,32},{16,48},{32,0},{48,16},{1,33},{17,49},{33,1},{49,17},{2,34}... | collective-permute-start | bytes 786440 | tf_op jit(solution)/shard_map/ppermute | solution.py:344
  10.9 32.0 %collective-permute-start = (bf16[512,256]{1,0:T(8,128)(2,1)}, bf16[512,256]{1,0:T(8,128)(2,1)S(1)}, u32[]{:S(2)}, u32[]{:S(2)}) collective-permute-start(bf16[512,256]{1,0:T(8,128)(2,1)} %get-tuple-element.34), channel_id=1, source_target_pairs={{0,64},{16,80},{32,96},{48,112},{1,65},{17,81},{33,97},{49,113},{2... | collective-permute-start | bytes 786440 | tf_op jit(solution)/shard_map/ppermute | solution.py:345
  12.1 30.8 %collective-permute-start.1 = (bf16[512,256]{1,0:T(8,128)(2,1)}, bf16[512,256]{1,0:T(8,128)(2,1)S(1)}, u32[]{:S(2)}, u32[]{:S(2)}) collective-permute-start(bf16[512,256]{1,0:T(8,128)(2,1)} %get-tuple-element.35), channel_id=1, source_target_pairs={{0,80},{16,96},{32,112},{48,64},{1,81},{17,97},{33,113},{49,65},{2... | collective-permute-start | bytes 786440 | tf_op jit(solution)/shard_map/ppermute | solution.py:345
  13.5 29.5 %collective-permute-start.4 = (bf16[512,256]{1,0:T(8,128)(2,1)S(1)}, bf16[512,256]{1,0:T(8,128)(2,1)S(1)}, u32[]{:S(2)}, u32[]{:S(2)}) collective-permute-start(bf16[512,256]{1,0:T(8,128)(2,1)S(1)} %copy-done.7), channel_id=1, source_target_pairs={{0,112},{16,64},{32,80},{48,96},{1,113},{17,65},{33,81},{49,97},{2... | collective-permute-start | bytes 786440 | tf_op jit(solution)/shard_map/ppermute | solution.py:345
  15.0 29.5 %collective-permute-start.3 = (bf16[512,256]{1,0:T(8,128)(2,1)}, bf16[512,256]{1,0:T(8,128)(2,1)S(1)}, u32[]{:S(2)}, u32[]{:S(2)}) collective-permute-start(bf16[512,256]{1,0:T(8,128)(2,1)} %collective-permute-done.2), channel_id=1, source_target_pairs={{0,64},{16,80},{32,96},{48,112},{1,65},{17,81},{33,97},{49,113},{2... | collective-permute-start | bytes 786440 | tf_op jit(solution)/shard_map/ppermute | solution.py:347
  16.3 40.3 %collective-permute-start.6 = (bf16[128,512]{1,0:T(8,128)(2,1)S(1)}, bf16[128,512]{1,0:T(8,128)(2,1)S(1)}, u32[]{:S(2)}, u32[]{:S(2)}) collective-permute-start(bf16[128,512]{1,0:T(8,128)(2,1)S(1)} %multiply_convert_fusion), channel_id=1, source_target_pairs={{0,16},{16,32},{32,48},{48,64},{64,80},{80,96},{96,112},{1,17},{17... | collective-permute-start | bytes 393224 | tf_op jit(solution)/shard_map/ppermute | solution.py:352
  48.7 7.9 %collective-permute-start.7 = (bf16[512,128]{1,0:T(8,128)(2,1)S(1)}, bf16[512,128]{1,0:T(8,128)(2,1)S(1)}, u32[]{:S(2)}, u32[]{:S(2)}) collective-permute-start(bf16[512,128]{1,0:T(8,128)(2,1)S(1)} %get-tuple-element.48), channel_id=1, source_target_pairs={{0,16},{16,32},{32,48},{48,0},{64,80},{80,96},{96,112},{112,64},{1... | collective-permute-start | bytes 393224 | tf_op jit(solution)/shard_map/ppermute | solution.py:355
  49.4 9.2 %collective-permute-start.8 = (bf16[512,128]{1,0:T(8,128)(2,1)S(1)}, bf16[512,128]{1,0:T(8,128)(2,1)S(1)}, u32[]{:S(2)}, u32[]{:S(2)}) collective-permute-start(bf16[512,128]{1,0:T(8,128)(2,1)S(1)} %get-tuple-element.49), channel_id=1, source_target_pairs={{0,32},{16,48},{32,0},{48,16},{64,96},{80,112},{96,64},{112,80},{1... | collective-permute-start | bytes 393224 | tf_op jit(solution)/shard_map/ppermute | solution.py:355
  54.2 5.0 %collective-permute-start.9 = (bf16[512,128]{1,0:T(8,128)(2,1)S(1)}, bf16[512,128]{1,0:T(8,128)(2,1)S(1)}, u32[]{:S(2)}, u32[]{:S(2)}) collective-permute-start(bf16[512,128]{1,0:T(8,128)(2,1)S(1)} %get-tuple-element.50), channel_id=1, source_target_pairs={{0,48},{16,0},{32,16},{48,32},{64,112},{80,64},{96,80},{112,96},{1... | collective-permute-start | bytes 393224 | tf_op jit(solution)/shard_map/ppermute | solution.py:355
  59.2 19.6 %copy-start = (bf16[512,512]{1,0:T(8,128)(2,1)S(1)}, bf16[512,512]{1,0:T(8,128)(2,1)}, u32[]{:S(2)}) copy-start(bf16[512,512]{1,0:T(8,128)(2,1)} %k_ref.3) | copy-start | bytes 1572868
  59.2 19.5 %copy-start.1 = (bf16[512,512]{1,0:T(8,128)(2,1)S(1)}, bf16[512,512]{1,0:T(8,128)(2,1)}, u32[]{:S(2)}) copy-start(bf16[512,512]{1,0:T(8,128)(2,1)} %v_ref.3) | copy-start | bytes 1572868
  59.2 19.5 %copy-start.2 = (bf16[512,512]{1,0:T(8,128)(2,1)S(1)}, bf16[512,512]{1,0:T(8,128)(2,1)}, u32[]{:S(2)}) copy-start(bf16[512,512]{1,0:T(8,128)(2,1)} %q_ref.2) | copy-start | bytes 1572868
  59.2 19.5 %copy-start.3 = (bf16[128,512]{1,0:T(8,128)(2,1)S(1)}, bf16[128,512]{1,0:T(8,128)(2,1)}, u32[]{:S(2)}) copy-start(bf16[128,512]{1,0:T(8,128)(2,1)} %f_ref.1) | copy-start | bytes 393220
  59.2 2.2 %collective-permute-start.10 = (bf16[2048,128]{1,0:T(8,128)(2,1)S(1)}, bf16[2048,128]{1,0:T(8,128)(2,1)S(1)}, u32[]{:S(2)}, u32[]{:S(2)}) collective-permute-start(bf16[2048,128]{1,0:T(8,128)(2,1)S(1)} %constant_dynamic-update-slice_fusion.own_ref), channel_id=1, source_target_pairs={{0,1},{1,0},{2,3},{3,2},{4,5},{5,4},{6,7},{7,6},{8,9},{9,8},{10,11... | collective-permute-start | bytes 1572872 | tf_op jit(solution)/shard_map/ppermute | solution.py:359
  70.1 24.5 %copy-start.5 = (bf16[4,240,512]{2,1,0:T(8,128)(2,1)S(1)}, bf16[4,240,512]{2,1,0:T(8,128)(2,1)}, u32[]{:S(2)}) copy-start(bf16[4,240,512]{2,1,0:T(8,128)(2,1)} %get-tuple-element.51) | copy-start | bytes 2949124
  70.1 24.4 %collective-permute-start.11 = (bf16[4,240,512]{2,1,0:T(8,128)(2,1)}, bf16[4,240,512]{2,1,0:T(8,128)(2,1)S(1)}, u32[]{:S(2)}, u32[]{:S(2)}) collective-permute-start(bf16[4,240,512]{2,1,0:T(8,128)(2,1)} %get-tuple-element.54), channel_id=1, source_target_pairs={{0,2},{1,3},{2,0},{3,1},{4,6},{5,7},{6,4},{7,5},{8,10},{9,11},{10,... | collective-permute-start | bytes 2949128 | tf_op jit(solution)/shard_map/ppermute | solution.py:363
  72.3 26.0 %collective-permute-start.12 = (bf16[2,272,512]{2,1,0:T(8,128)(2,1)}, bf16[2,272,512]{2,1,0:T(8,128)(2,1)S(1)}, u32[]{:S(2)}, u32[]{:S(2)}) collective-permute-start(bf16[2,272,512]{2,1,0:T(8,128)(2,1)} %get-tuple-element.57), channel_id=1, source_target_pairs={{0,8},{1,9},{2,10},{3,11},{4,12},{5,13},{6,14},{7,15},{8,0},{9,1},... | collective-permute-start | bytes 1671176 | tf_op jit(solution)/shard_map/ppermute | solution.py:364
  75.5 25.3 %collective-permute-start.13 = (bf16[2,272,512]{2,1,0:T(8,128)(2,1)}, bf16[2,272,512]{2,1,0:T(8,128)(2,1)S(1)}, u32[]{:S(2)}, u32[]{:S(2)}) collective-permute-start(bf16[2,272,512]{2,1,0:T(8,128)(2,1)} %get-tuple-element.58), channel_id=1, source_target_pairs={{0,4},{1,5},{2,6},{3,7},{4,8},{5,9},{6,10},{7,11},{8,12},{9,13},{1... | collective-permute-start | bytes 1671176 | tf_op jit(solution)/shard_map/ppermute | solution.py:364
  76.2 25.7 %collective-permute-start.14 = (bf16[2,272,512]{2,1,0:T(8,128)(2,1)}, bf16[2,272,512]{2,1,0:T(8,128)(2,1)S(1)}, u32[]{:S(2)}, u32[]{:S(2)}) collective-permute-start(bf16[2,272,512]{2,1,0:T(8,128)(2,1)} %get-tuple-element.59), channel_id=1, source_target_pairs={{0,12},{1,13},{2,14},{3,15},{4,0},{5,1},{6,2},{7,3},{8,4},{9,5},{1... | collective-permute-start | bytes 1671176 | tf_op jit(solution)/shard_map/ppermute | solution.py:364
  95.1 11.3 %collective-permute-start.16 = (bf16[240,512]{1,0:T(8,128)(2,1)S(1)}, bf16[240,512]{1,0:T(8,128)(2,1)S(1)}, u32[]{:S(2)}, u32[]{:S(2)}) collective-permute-start(bf16[240,512]{1,0:T(8,128)(2,1)S(1)} %get-tuple-element.68), channel_id=1, source_target_pairs={{0,4},{1,5},{2,6},{3,7},{4,8},{5,9},{6,10},{7,11},{8,12},{9,13},{1... | collective-permute-start | bytes 737288 | tf_op jit(solution)/shard_map/ppermute | solution.py:372
  96.7 10.4 %collective-permute-start.18 = (bf16[240,512]{1,0:T(8,128)(2,1)S(1)}, bf16[240,512]{1,0:T(8,128)(2,1)S(1)}, u32[]{:S(2)}, u32[]{:S(2)}) collective-permute-start(bf16[240,512]{1,0:T(8,128)(2,1)S(1)} %get-tuple-element.69), channel_id=1, source_target_pairs={{0,12},{1,13},{2,14},{3,15},{4,0},{5,1},{6,2},{7,3},{8,4},{9,5},{1... | collective-permute-start | bytes 737288 | tf_op jit(solution)/shard_map/ppermute | solution.py:372
  98.4 12.6 %collective-permute-start.17 = (bf16[240,512]{1,0:T(8,128)(2,1)S(1)}, bf16[240,512]{1,0:T(8,128)(2,1)S(1)}, u32[]{:S(2)}, u32[]{:S(2)}) collective-permute-start(bf16[240,512]{1,0:T(8,128)(2,1)S(1)} %get-tuple-element.70), channel_id=1, source_target_pairs={{0,8},{1,9},{2,10},{3,11},{4,12},{5,13},{6,14},{7,15},{8,0},{9,1},... | collective-permute-start | bytes 737288 | tf_op jit(solution)/shard_map/ppermute | solution.py:372
  101.9 1.0 copy-start.4
  102.1 9.0 %collective-permute-start.15 = (bf16[272,512]{1,0:T(8,128)(2,1)S(1)}, bf16[272,512]{1,0:T(8,128)(2,1)S(1)}, u32[]{:S(2)}, u32[]{:S(2)}) collective-permute-start(bf16[272,512]{1,0:T(8,128)(2,1)S(1)} %get-tuple-element.65), channel_id=1, source_target_pairs={{0,2},{1,3},{2,0},{3,1},{4,6},{5,7},{6,4},{7,5},{8,10},{9,11},{10,... | collective-permute-start | bytes 835592 | tf_op jit(solution)/shard_map/ppermute | solution.py:375
